TPU v7x, 32 devices: a whole 2x2x4 slice. The times are simulated.
32 devices in a mesh: groups: 2 (over x), patch: 16 (over z, y, core).
Axes of the slice: x: 2, y: 2, z: 4, core: 2. Of those that a mesh axis runs over, the one named last changes fastest.
Arguments:
- nodes: bfloat16 [10240, 512], P(('groups', 'patch')), parts along dimension 0, may hold values from -6 to 6
- edges: bfloat16 [49152, 512], P(('groups', 'patch')), parts along dimension 0, may hold values from -6 to 6
- node_cot: bfloat16 [10240, 512], P(('groups', 'patch')), parts along dimension 0, may hold values from -6 to 6
- edge_cot: bfloat16 [49152, 512], P(('groups', 'patch')), parts along dimension 0, may hold values from -6 to 6
- w_edge: bfloat16 [512, 512], replicated, may hold values from -0.15625 to 0.15625
- w_send: bfloat16 [512, 512], replicated, may hold values from -0.15625 to 0.15625
- w_recv: bfloat16 [512, 512], replicated, may hold values from -0.15625 to 0.15625
- edge_bias: float32 [512], replicated, may hold values from -3 to 3
- w_edge_out: bfloat16 [512, 512], replicated, may hold values from -0.25 to 0.25
- edge_out_bias: float32 [512], replicated, may hold values from -3 to 3
- edge_gain: float32 [512], replicated, may hold values from 0.25 to 1.75
- w_node: bfloat16 [512, 512], replicated, may hold values from -0.1875 to 0.1875
- w_agg: bfloat16 [512, 512], replicated, may hold values from -0.1875 to 0.1875
- node_bias: float32 [512], replicated, may hold values from -3 to 3
- w_node_out: bfloat16 [512, 512], replicated, may hold values from -0.25 to 0.25
- node_out_bias: float32 [512], replicated, may hold values from -3 to 3
- node_gain: float32 [512], replicated, may hold values from 0.25 to 1.75
- send_slots: int32 [24576], P('patch'), may hold values from 0 to 607, as said below
- recv_slots: int32 [24576], P('patch'), may hold values from 0 to 319
- neighbour_send_lists: int32 [64, 64], P('patch'), may hold values from 0 to 319
- coarse_rows: int32 [128], P('patch'), may hold values from 0 to 319, as said below
- far_lists: int32 [16, 16, 2], P('patch'), may hold values from 0 to 7
- block_count: int32 [16], P('patch'), may hold values from 6 to 12, as said below
Outputs:
- new_nodes: bfloat16 [10240, 512], P(('groups', 'patch')), parts along dimension 0
- new_edges: bfloat16 [49152, 512], P(('groups', 'patch')), parts along dimension 0
- node_grad: bfloat16 [10240, 512], P(('groups', 'patch')), parts along dimension 0
- edge_grad: bfloat16 [49152, 512], P(('groups', 'patch')), parts along dimension 0
There are 2 independent parts, one for each index of `groups`. A program takes and returns all parts, laid end to end along the dimension named above; an argument that names none is the same for every part. Nothing has to cross between parts.
Inputs may be any that keep to these rules, and one draw needn't show every extreme that they name: `send_slots`: addresses below 320 are rows of the edge's own patch, the next 256 are neighbour slots, the last 16 * 2 are distant slots. `coarse_rows`: the 8 rows of one patch are distinct. `block_count`: some patches have all 12 blocks live in every draw.
All inputs are finite; a program needn't handle non-finite values.
Results may differ from a plain program's by a relative error of at most 0.013.
Values may be sent and summed in bfloat16 or wider, within the bound.
No kernel may reach another device: no remote copies, remote signals or barrier semaphores. Data moves between devices by JAX's collectives and lax.ppermute only.
A program may use at most 128 MiB of HBM per device.

v0:
```python
import jax
import jax.numpy as jnp
from jax import lax
from jax.sharding import PartitionSpec as P

BLOCK = 128


def passed_along(value, axis, steps):
    count = lax.axis_size(axis)
    pairs = [(source, (source + steps) % count) for source in range(count)]
    return lax.ppermute(value, axis, pairs)


def normalize(values):
    center = values - jnp.mean(values, axis=-1, keepdims=True)
    spread = jnp.mean(center * center, axis=-1, keepdims=True)
    return center * lax.rsqrt(spread + 1e-05)


def layer(node_rows, edge_rows, table, sending_patch, receiver, live, params):
    (
        w_edge,
        w_send,
        w_recv,
        edge_bias,
        w_edge_out,
        edge_out_bias,
        edge_gain,
        w_node,
        w_agg,
        node_bias,
        w_node_out,
        node_out_bias,
        node_gain,
    ) = params
    send_rows = jnp.take(table, sending_patch, axis=0).astype(jnp.bfloat16)
    recv_rows = jnp.take(node_rows, receiver, axis=0).astype(jnp.bfloat16)
    pre_edge = jnp.dot(edge_rows.astype(jnp.bfloat16), w_edge, preferred_element_type=jnp.float32)
    pre_edge = pre_edge + jnp.dot(send_rows, w_send, preferred_element_type=jnp.float32)
    pre_edge = pre_edge + jnp.dot(recv_rows, w_recv, preferred_element_type=jnp.float32) + edge_bias
    edge_hidden = jax.nn.silu(pre_edge).astype(jnp.bfloat16)
    edge_out = jnp.dot(edge_hidden, w_edge_out, preferred_element_type=jnp.float32) + edge_out_bias
    message = live[:, None] * edge_gain * normalize(edge_out)
    new_edges = edge_rows + message
    sent_message = message.astype(jnp.bfloat16)
    aggregate = jax.ops.segment_sum(
        sent_message.astype(jnp.float32), receiver, num_segments=node_rows.shape[0]
    )
    aggregate = aggregate.astype(jnp.bfloat16)
    pre_node = jnp.dot(node_rows.astype(jnp.bfloat16), w_node, preferred_element_type=jnp.float32)
    pre_node = pre_node + jnp.dot(aggregate, w_agg, preferred_element_type=jnp.float32) + node_bias
    node_hidden = jax.nn.silu(pre_node).astype(jnp.bfloat16)
    node_out = jnp.dot(node_hidden, w_node_out, preferred_element_type=jnp.float32) + node_out_bias
    new_nodes = node_rows + node_gain * normalize(node_out)
    return (new_nodes, new_edges)


def local(
    nodes,
    edges,
    node_cot,
    edge_cot,
    w_edge,
    w_send,
    w_recv,
    edge_bias,
    w_edge_out,
    edge_out_bias,
    edge_gain,
    w_node,
    w_agg,
    node_bias,
    w_node_out,
    node_out_bias,
    node_gain,
    send_slots,
    recv_slots,
    neighbour_send_lists,
    coarse_rows,
    far_lists,
    block_count,
):
    params = (
        w_edge,
        w_send,
        w_recv,
        edge_bias,
        w_edge_out,
        edge_out_bias,
        edge_gain,
        w_node,
        w_agg,
        node_bias,
        w_node_out,
        node_out_bias,
        node_gain,
    )
    own_rows = nodes.shape[0]
    width = nodes.shape[1]
    peers = lax.axis_size("patch")
    near_steps = neighbour_send_lists.shape[0]
    near_width = neighbour_send_lists.shape[1]
    offsets = [(index // 2 + 1) * (1 - 2 * (index % 2)) for index in range(near_steps)]
    near_parts = []
    for index in range(near_steps):
        listed = jnp.take(nodes, neighbour_send_lists[index], axis=0)
        near_parts.append(passed_along(listed, "patch", offsets[index]))
    near_block = jnp.concatenate(near_parts, axis=0)
    wanted = far_lists[0]
    asked = lax.all_to_all(wanted, "patch", split_axis=0, concat_axis=0, tiled=True)
    answer_rows = jnp.take(coarse_rows, asked.reshape(-1), axis=0)
    outgoing = jnp.take(nodes, answer_rows, axis=0).reshape(peers, -1, width)
    far_block = lax.all_to_all(outgoing, "patch", split_axis=0, concat_axis=0, tiled=True).reshape(
        -1, width
    )
    table = jnp.concatenate([nodes, near_block, far_block], axis=0).astype(jnp.float32)
    live = (jnp.arange(edges.shape[0], dtype=jnp.int32) // BLOCK < block_count[0]).astype(
        jnp.float32
    )

    def forward(node_rows, edge_rows, table_rows):
        return layer(node_rows, edge_rows, table_rows, send_slots, recv_slots, live, params)

    (new_nodes, new_edges), pull = jax.vjp(
        forward, nodes.astype(jnp.float32), edges.astype(jnp.float32), table
    )
    node_grad, edge_grad, table_grad = pull(
        (node_cot.astype(jnp.float32), edge_cot.astype(jnp.float32))
    )
    node_grad = node_grad + table_grad[:own_rows]
    near_grad = table_grad[own_rows : own_rows + near_steps * near_width].reshape(
        near_steps, near_width, width
    )
    for index in range(near_steps):
        returned = passed_along(
            near_grad[index].astype(jnp.bfloat16), "patch", -offsets[index]
        ).astype(jnp.float32)
        node_grad = node_grad.at[neighbour_send_lists[index]].add(returned)
    far_grad = table_grad[own_rows + near_steps * near_width :].reshape(peers, -1, width)
    came_back = (
        lax.all_to_all(
            far_grad.astype(jnp.bfloat16), "patch", split_axis=0, concat_axis=0, tiled=True
        )
        .astype(far_grad.dtype)
        .reshape(-1, width)
    )
    node_grad = node_grad.at[answer_rows].add(came_back)
    return (
        new_nodes.astype(jnp.bfloat16),
        new_edges.astype(jnp.bfloat16),
        node_grad.astype(jnp.bfloat16),
        edge_grad.astype(jnp.bfloat16),
    )


def solution(mesh):
    placed = (
        P(("groups", "patch"), None),
        P(("groups", "patch"), None),
        P(("groups", "patch"), None),
        P(("groups", "patch"), None),
        P(),
        P(),
        P(),
        P(),
        P(),
        P(),
        P(),
        P(),
        P(),
        P(),
        P(),
        P(),
        P(),
        P("patch"),
        P("patch"),
        P("patch", None),
        P("patch"),
        P("patch", None, None),
        P("patch"),
    )
    return jax.shard_map(
        local,
        mesh=mesh,
        in_specs=placed,
        out_specs=(
            P(("groups", "patch"), None),
            P(("groups", "patch"), None),
            P(("groups", "patch"), None),
            P(("groups", "patch"), None),
        ),
        check_vma=False,
    )
```

profile of v0, /device:TPU:0, one launch (start us, length us, event | category | flops | bytes accessed | tf_op | source)
XLA Modules:
  0.0 170.7 jit_solution(1157636006075244540)
XLA Ops:
  0.7 0.9 compare_and_fusion.3
  1.6 1.7 %gather_fusion.5 = bf16[64,512]{1,0:T(8,128)(2,1)S(1)} fusion(bf16[320,512]{1,0:T(8,128)(2,1)} %param.25, s32[1024]{0:T(1024)S(1)} %pad_clamp_fusion.8), kind=kCustom, calls=%fused_computation.clone | custom fusion | bytes 131328 | tf_op jit(solution)/shard_map/jit(_take)/gather | solution.py:107
  3.4 0.5 collective-permute-start
  4.0 1.7 %gather_fusion.6 = bf16[64,512]{1,0:T(8,128)(2,1)S(1)} fusion(bf16[320,512]{1,0:T(8,128)(2,1)} %param.25, s32[1024]{0:T(1024)S(1)} %pad_clamp_fusion.7), kind=kCustom, calls=%fused_computation.1.clone | custom fusion | bytes 131328 | tf_op jit(solution)/shard_map/jit(_take)/gather | solution.py:107
  5.8 5.1 %collective-permute-start.1 = (bf16[64,512]{1,0:T(8,128)(2,1)S(1)}, bf16[64,512]{1,0:T(8,128)(2,1)S(1)}, u32[]{:S(2)}, u32[]{:S(2)}) collective-permute-start(bf16[64,512]{1,0:T(8,128)(2,1)S(1)} %broadcast_select_fusion.2), channel_id=1, source_target_pairs={{0,15},{1,0},{2,1},{3,2},{4,3},{5,4},{6,5},{7,6},{8,7},{9,8},{10,9... | collective-permute-start | bytes 196616 | tf_op jit(solution)/shard_map/ppermute | solution.py:12
  10.8 1.7 %gather_fusion.7 = bf16[64,512]{1,0:T(8,128)(2,1)S(1)} fusion(bf16[320,512]{1,0:T(8,128)(2,1)} %param.25, s32[1024]{0:T(1024)S(1)} %pad_clamp_fusion.6), kind=kCustom, calls=%fused_computation.2.clone | custom fusion | bytes 131328 | tf_op jit(solution)/shard_map/jit(_take)/gather | solution.py:107
  12.7 1.7 %gather_fusion.8 = bf16[64,512]{1,0:T(8,128)(2,1)S(1)} fusion(bf16[320,512]{1,0:T(8,128)(2,1)} %param.25, s32[1024]{0:T(1024)S(1)} %pad_clamp_fusion.5), kind=kCustom, calls=%fused_computation.3.clone | custom fusion | bytes 131328 | tf_op jit(solution)/shard_map/jit(_take)/gather | solution.py:107
  14.5 0.7 broadcast_select_fusion
  15.2 4.7 %collective-permute-start.3 = (bf16[64,512]{1,0:T(8,128)(2,1)}, bf16[64,512]{1,0:T(8,128)(2,1)}, u32[]{:S(2)}, u32[]{:S(2)}) collective-permute-start(bf16[64,512]{1,0:T(8,128)(2,1)} %broadcast_select_fusion), channel_id=1, source_target_pairs={{0,14},{1,15},{2,0},{3,1},{4,2},{5,3},{6,4},{7,5},{8,6},{9,7},{10,... | collective-permute-start | bytes 196616 | tf_op jit(solution)/shard_map/ppermute | solution.py:12
  19.9 1.4 copy.46
  21.2 3.5 %all-to-all-start = ((s32[16,1,2]{2,1,0:T(1,128)}), s32[16,1,2]{2,1,0:T(1,128)S(1)}, u32[]{:S(2)}, u32[]{:S(2)}) async-start(s32[16,1,2]{2,1,0:T(1,128)} %copy.46), calls=%async_computation | async-start | bytes 16384 | tf_op jit(solution)/shard_map/all_to_all | solution.py:111
  24.8 0.6 compare_and_fusion.2
  25.4 0.6 fusion.60
  26.0 2.2 %fusion.71 = f32[320,512]{1,0:T(8,128)} fusion(bf16[320,512]{1,0:T(8,128)(2,1)S(1)} %copy-done.1, bf16[512,512]{1,0:T(8,128)(2,1)} %param.36), kind=kOutput, calls=%fused_computation.174 | convolution fusion | flops 167772160 | bytes 1507328 | tf_op jit(solution)/shard_map/jvp()/dot_general | solution.py:51
  28.2 1.6 copy.51
  29.8 3.7 %fusion.72 = f32[1536,512]{1,0:T(8,128)} fusion(bf16[1536,512]{1,0:T(8,128)(2,1)S(1)} %copy-done.6, bf16[512,512]{1,0:T(8,128)(2,1)} %param.29), kind=kOutput, calls=%fused_computation.175 | convolution fusion | flops 805306368 | bytes 5242880 | tf_op jit(solution)/shard_map/jvp()/dot_general | solution.py:39
  33.5 0.6 pad_clamp_fusion
  34.7 0.6 compare_and_fusion
  35.3 5.4 %gather_fusion.3 = bf16[1536,512]{1,0:T(8,128)(2,1)} fusion(bf16[320,512]{1,0:T(8,128)(2,1)S(1)} %copy-done.1, s32[2048]{0:T(1024)S(1)} %get-tuple-element.55), kind=kCustom, calls=%fused_computation.7 | custom fusion | bytes 3151872 | tf_op jit(solution)/shard_map/jvp(jit(_take))/gather | solution.py:38
  40.7 1.7 %copy.53 = bf16[1536,512]{0,1:T(8,128)(2,1)S(1)} copy(bf16[1536,512]{1,0:T(8,128)(2,1)} %param.28) | data formatting | bytes 3145728 | tf_op args[3]
  43.0 0.7 reduce.3
  43.8 0.7 gather_fusion
  44.6 0.6 gather_fusion.1
  45.5 0.7 broadcast_select_fusion.4
  46.3 6.0 %all-to-all-start.1 = ((bf16[16,2,512]{2,1,0:T(2,128)(2,1)}), bf16[16,2,512]{2,1,0:T(2,128)(2,1)S(1)}, u32[]{:S(2)}, u32[]{:S(2)}) async-start(bf16[16,2,512]{2,1,0:T(2,128)(2,1)} %broadcast_select_fusion.4), calls=%async_computation.1 | async-start | bytes 65536 | tf_op jit(solution)/shard_map/all_to_all | solution.py:114
  52.3 6.6 %all-to-all-done.1 = bf16[16,2,512]{2,1,0:T(2,128)(2,1)S(1)} async-done(((bf16[16,2,512]{2,1,0:T(2,128)(2,1)}), bf16[16,2,512]{2,1,0:T(2,128)(2,1)S(1)}, u32[]{:S(2)}, u32[]{:S(2)}) %all-to-all-start.1) | async-done | bytes 32800 | tf_op jit(solution)/shard_map/all_to_all | solution.py:114
  59.0 0.8 constant_dynamic-update-slice_fusion.1
  59.8 5.4 %gather_fusion.2 = bf16[1536,512]{1,0:T(8,128)(2,1)} fusion(bf16[608,512]{1,0:T(8,128)(2,1)S(1)} %constant_dynamic-update-slice_fusion, s32[2048]{0:T(1024)S(1)} %pad_clamp_fusion.2), kind=kCustom, calls=%fused_computation.6 | custom fusion | bytes 3151872 | tf_op jit(solution)/shard_map/jvp(jit(_take))/gather | solution.py:37
  65.3 3.8 %convolution_add_fusion.2 = f32[1536,512]{1,0:T(8,128)S(1)} fusion(f32[1536,512]{1,0:T(8,128)} %fusion.72, bf16[512,512]{1,0:T(8,128)(2,1)} %param.30, bf16[1536,512]{1,0:T(8,128)(2,1)} %gather_fusion.2, pred[1536]{0:T(1024)(128)(4,1)S(1)} %copy-done.29), kind=kOutput, calls=%fused_computation.28 | convolution fusion | flops 806879232 | bytes 8390144 | tf_op jit(solution)/shard_map/jvp()/dot_general | solution.py:40
  69.1 1.1 fusion
  70.2 1.2 fusion.69
  72.3 1.2 copy-done.3
  73.5 2.2 %fusion.16 = f32[1536,512]{0,1:T(8,128)} fusion(f32[1536,512]{0,1:T(8,128)S(1)} %get-tuple-element.51, f32[1536]{0:T(1024)S(1)} %fusion.54, f32[1536]{0:T(1024)S(1)} %broadcast_multiply_fusion, f32[512]{0:T(512)S(1)} %copy-done.26, f32[1536]{0:T(1024)S(1)} %get-tuple-element.56), kind=kLoop, calls=%fused_computation.51 | loop fusion | flops 4718592 | bytes 6311936 | tf_op jit(solution)/shard_map/jvp()/convert_element_type | solution.py:48
  75.7 3.6 %copy.50 = f32[1536,512]{1,0:T(8,128)} copy(f32[1536,512]{0,1:T(8,128)} %fusion.16) | data formatting | bytes 6291456 | tf_op jit(solution)/shard_map/jvp()/convert_element_type | solution.py:48
  79.3 11.1 %scatter_custom_fusion = f32[320,512]{1,0:T(8,128)} fusion(s32[1536]{0:T(1024)S(1)} %copy-done.21, f32[1536,512]{1,0:T(8,128)} %copy.50, f32[]{:T(128)} %constant.83.clone.1), kind=kCustom, calls=%fused_computation.86 | custom fusion | flops 786432 | bytes 655872 | tf_op jit(solution)/shard_map/jvp()/scatter-add | solution.py:47
  90.4 1.6 fusion.23
  92.1 1.6 fusion.70
  94.0 1.1 fusion.66
  95.1 0.6 fusion.33
  96.8 5.4 %gather_fusion.4 = bf16[1536,512]{1,0:T(8,128)(2,1)} fusion(bf16[320,512]{1,0:T(8,128)(2,1)S(1)} %fusion.75, s32[2048]{0:T(1024)S(1)} %copy-done.22), kind=kCustom, calls=%fused_computation.8 | custom fusion | bytes 3151872 | tf_op jit(solution)/shard_map/transpose(jvp())/gather | solution.py:47
  102.2 2.6 %copy.52 = bf16[1536,512]{0,1:T(8,128)(2,1)} copy(bf16[1536,512]{1,0:T(8,128)(2,1)} %gather_fusion.4) | data formatting | bytes 3145728 | tf_op jit(solution)/shard_map/transpose(jvp())/gather | solution.py:47
  104.8 3.5 %multiply_reduce_fusion = f32[1536]{0:T(1024)S(1)} fusion(bf16[1536,512]{0,1:T(8,128)(2,1)S(1)} %copy.53, f32[1536,512]{0,1:T(8,128)} %copy-done.3, f32[1536]{0:T(1024)S(1)} %broadcast_multiply_fusion, f32[512]{0:T(512)S(1)} %copy-done.26, f32[1536]{0:T(1024)S(1)} %get-tuple-element.56, bf16[1536,512]{0,1:T(8,128)(2,1)} %copy.52, ...), kind=kLoop, calls=%fused_computation.38 | loop fusion | flops 7076352 | bytes 6313472 | tf_op jit(solution)/shard_map/transpose(jvp())/reduce_sum | solution.py:18
  109.1 3.0 %fusion.67 = (f32[1536]{0:T(1024)S(1)}, f32[1536,512]{0,1:T(8,128)S(1)}, bf16[1536,512]{0,1:T(8,128)(2,1)}) fusion(f32[1536]{0:T(1024)S(1)} %multiply_multiply_fusion.2, f32[1536,512]{0,1:T(8,128)S(1)} %copy-done.4, f32[1536]{0:T(1024)S(1)} %broadcast_multiply_fusion, f32[1536]{0:T(1024)S(1)} %fusion.54, bf16[1536,512]{0,1:T(8,128)(2,1)S(1)} %copy.53, ...), kind=kLoop, calls=%fused_computation.170 | loop fusion | flops 13367808 | bytes 12617216 | tf_op jit(solution)/shard_map/transpose(jvp())/reduce_sum | solution.py:16
  112.1 2.0 %fusion.2 = bf16[1536,512]{1,0:T(8,128)(2,1)S(1)} fusion(f32[1536,512]{1,0:T(8,128)S(1)} %copy-done.11, bf16[512,512]{1,0:T(8,128)(2,1)S(1)} %copy-done, f32[1536,512]{0,1:T(8,128)S(1)} %get-tuple-element.20, f32[1536]{0:T(1024)S(1)} %negate_multiply_fusion), kind=kOutput, calls=%fused_computation.30 | convolution fusion | flops 815529984 | bytes 8394752 | tf_op jit(solution)/shard_map/transpose(jvp())/dot_general | solution.py:43
  114.1 2.2 %fusion.74 = bf16[1536,512]{1,0:T(8,128)(2,1)} fusion(bf16[1536,512]{1,0:T(8,128)(2,1)S(1)} %fusion.2, bf16[512,512]{1,0:T(8,128)(2,1)S(1)} %copy-done.18), kind=kOutput, calls=%fused_computation.177 | convolution fusion | flops 805306368 | bytes 3670016 | tf_op jit(solution)/shard_map/transpose(jvp())/dot_general | solution.py:40
  116.3 2.2 %fusion.73 = bf16[1536,512]{1,0:T(8,128)(2,1)} fusion(bf16[1536,512]{1,0:T(8,128)(2,1)S(1)} %fusion.2, bf16[512,512]{1,0:T(8,128)(2,1)S(1)} %copy-done.20), kind=kOutput, calls=%fused_computation.176 | convolution fusion | flops 805306368 | bytes 3670016 | tf_op jit(solution)/shard_map/transpose(jvp())/dot_general | solution.py:41
  118.5 11.4 %scatter_custom_fusion.1 = f32[608,512]{1,0:T(8,128)} fusion(s32[1536]{0:T(1024)} %copy-done.24, bf16[1536,512]{1,0:T(8,128)(2,1)} %fusion.74, f32[]{:T(128)} %constant.83.clone.1), kind=kCustom, calls=%fused_computation.34 | custom fusion | flops 1572864 | bytes 2818560 | tf_op jit(solution)/shard_map/transpose(jvp(jit(_take)))/scatter-add | solution.py:37
  129.9 1.4 convert.8
  131.2 0.7 fusion.68
  131.9 3.7 %fusion.1 = bf16[1536,512]{0,1:T(8,128)(2,1)} fusion(bf16[1536,512]{0,1:T(8,128)(2,1)S(1)} %copy.53, bf16[1536,512]{1,0:T(8,128)(2,1)} %copy-done.39, bf16[512,512]{1,0:T(8,128)(2,1)} %param.29), kind=kOutput, calls=%fused_computation.29 | convolution fusion | flops 808452096 | bytes 5242880 | tf_op jit(solution)/shard_map/transpose(jvp())/dot_general | solution.py:39
  136.2 1.1 collective-permute-start.6
  137.3 0.9 collective-permute-start.7
  138.2 0.6 convert_element_type.159
  138.8 7.6 %all-to-all-start.2 = ((bf16[16,2,512]{2,1,0:T(2,128)(2,1)}), bf16[16,2,512]{2,1,0:T(2,128)(2,1)S(1)}, u32[]{:S(2)}, u32[]{:S(2)}) async-start(bf16[16,2,512]{2,1,0:T(2,128)(2,1)} %convert_element_type.159), calls=%async_computation.2 | async-start | bytes 65536 | tf_op jit(solution)/shard_map/all_to_all | solution.py:142
  146.4 1.6 fusion.27
  148.1 1.6 copy.55
  149.7 2.7 %copy.56 = bf16[1536,512]{1,0:T(8,128)(2,1)} copy(bf16[1536,512]{0,1:T(8,128)(2,1)} %fusion.1) | data formatting | bytes 3145728
  152.4 10.2 %scatter_custom_fusion.2 = f32[320,512]{1,0:T(8,128)S(1)} fusion(f32[320,512]{1,0:T(8,128)S(1)} %fusion.27, s32[1536]{0:T(1024)} %copy-done.25, bf16[1536,512]{1,0:T(8,128)(2,1)S(1)} %copy-done.15), kind=kCustom, calls=%fused_computation.32 | custom fusion | flops 1572864 | bytes 2228224 | tf_op jit(solution)/shard_map/transpose(jvp(jit(_take)))/scatter-add | solution.py:38
  162.6 1.6 scatter_custom_fusion.3
  164.2 1.6 scatter_custom_fusion.4
  165.7 1.6 scatter_custom_fusion.5
  167.3 1.6 scatter_custom_fusion.6
  168.9 1.1 scatter_fusion
  169.9 0.8 convert_element_type.160
  (132 shorter events, 5.1 us)
Async XLA Ops:
  0.6 69.6 %copy-start = (bf16[512,512]{1,0:T(8,128)(2,1)S(1)}, bf16[512,512]{1,0:T(8,128)(2,1)}, u32[]{:S(2)}) copy-start(bf16[512,512]{1,0:T(8,128)(2,1)} %param.33) | copy-start | bytes 1572868
  0.6 24.7 %copy-start.30 = (s32[4,64]{1,0:T(4,128)S(1)}, s32[4,64]{1,0:T(4,128)}, u32[]{:S(2)}) copy-start(s32[4,64]{1,0:T(4,128)} %param.44) | copy-start | bytes 3076
  0.7 24.1 %copy-start.1 = (bf16[320,512]{1,0:T(8,128)(2,1)S(1)}, bf16[320,512]{1,0:T(8,128)(2,1)}, u32[]{:S(2)}) copy-start(bf16[320,512]{1,0:T(8,128)(2,1)} %param.25) | copy-start | bytes 983044
  0.7 24.1 %copy-start.23 = (s32[1536]{0:T(1024)S(1)}, s32[1536]{0:T(1024)}, u32[]{:S(2)}) copy-start(s32[1536]{0:T(1024)} %param.42) | copy-start | bytes 18436
  0.7 27.5 %copy-start.6 = (bf16[1536,512]{1,0:T(8,128)(2,1)S(1)}, bf16[1536,512]{1,0:T(8,128)(2,1)}, u32[]{:S(2)}) copy-start(bf16[1536,512]{1,0:T(8,128)(2,1)} %param.26) | copy-start | bytes 4718596
  3.4 55.5 %collective-permute-start = (bf16[64,512]{1,0:T(8,128)(2,1)S(1)}, bf16[64,512]{1,0:T(8,128)(2,1)S(1)}, u32[]{:S(2)}, u32[]{:S(2)}) collective-permute-start(bf16[64,512]{1,0:T(8,128)(2,1)S(1)} %broadcast_select_fusion.3), channel_id=1, source_target_pairs={{0,1},{1,2},{2,3},{3,4},{4,5},{5,6},{6,7},{7,8},{8,9},{9,10},{10,1... | collective-permute-start | bytes 196616 | tf_op jit(solution)/shard_map/ppermute | solution.py:12
  5.8 53.1 %collective-permute-start.1 = (bf16[64,512]{1,0:T(8,128)(2,1)S(1)}, bf16[64,512]{1,0:T(8,128)(2,1)S(1)}, u32[]{:S(2)}, u32[]{:S(2)}) collective-permute-start(bf16[64,512]{1,0:T(8,128)(2,1)S(1)} %broadcast_select_fusion.2), channel_id=1, source_target_pairs={{0,15},{1,0},{2,1},{3,2},{4,3},{5,4},{6,5},{7,6},{8,7},{9,8},{10,9... | collective-permute-start | bytes 196616 | tf_op jit(solution)/shard_map/ppermute | solution.py:12
  12.7 46.3 %collective-permute-start.2 = (bf16[64,512]{1,0:T(8,128)(2,1)S(1)}, bf16[64,512]{1,0:T(8,128)(2,1)S(1)}, u32[]{:S(2)}, u32[]{:S(2)}) collective-permute-start(bf16[64,512]{1,0:T(8,128)(2,1)S(1)} %broadcast_select_fusion.1), channel_id=1, source_target_pairs={{0,2},{1,3},{2,4},{3,5},{4,6},{5,7},{6,8},{7,9},{8,10},{9,11},{10,... | collective-permute-start | bytes 196616 | tf_op jit(solution)/shard_map/ppermute | solution.py:12
  15.2 43.8 %collective-permute-start.3 = (bf16[64,512]{1,0:T(8,128)(2,1)}, bf16[64,512]{1,0:T(8,128)(2,1)}, u32[]{:S(2)}, u32[]{:S(2)}) collective-permute-start(bf16[64,512]{1,0:T(8,128)(2,1)} %broadcast_select_fusion), channel_id=1, source_target_pairs={{0,14},{1,15},{2,0},{3,1},{4,2},{5,3},{6,4},{7,5},{8,6},{9,7},{10,... | collective-permute-start | bytes 196616 | tf_op jit(solution)/shard_map/ppermute | solution.py:12
  21.2 21.2 %all-to-all-start = ((s32[16,1,2]{2,1,0:T(1,128)}), s32[16,1,2]{2,1,0:T(1,128)S(1)}, u32[]{:S(2)}, u32[]{:S(2)}) async-start(s32[16,1,2]{2,1,0:T(1,128)} %copy.46), calls=%async_computation | async-start | bytes 16384 | tf_op jit(solution)/shard_map/all_to_all | solution.py:111
  24.8 27.5 %copy-start.24 = (s32[1536]{0:T(1024)}, s32[1536]{0:T(1024)S(1)}, u32[]{:S(2)}) copy-start(s32[1536]{0:T(1024)S(1)} %compare_select_fusion.1) | copy-start | bytes 18436
  29.8 3.7 %copy-start.21 = (s32[1536]{0:T(1024)S(1)}, s32[1536]{0:T(1024)}, u32[]{:S(2)}) copy-start(s32[1536]{0:T(1024)} %param.43) | copy-start | bytes 18436
  33.5 7.3 %copy-start.25 = (s32[1536]{0:T(1024)}, s32[1536]{0:T(1024)S(1)}, u32[]{:S(2)}) copy-start(s32[1536]{0:T(1024)S(1)} %compare_select_fusion) | copy-start | bytes 18436
  40.7 3.0 %copy-start.2 = (s32[8]{0:T(128)S(1)}, s32[8]{0:T(128)}, u32[]{:S(2)}) copy-start(s32[8]{0:T(128)} %param.45) | copy-start | bytes 100
  44.5 0.8 copy-start.32
  46.3 12.6 %all-to-all-start.1 = ((bf16[16,2,512]{2,1,0:T(2,128)(2,1)}), bf16[16,2,512]{2,1,0:T(2,128)(2,1)S(1)}, u32[]{:S(2)}, u32[]{:S(2)}) async-start(bf16[16,2,512]{2,1,0:T(2,128)(2,1)} %broadcast_select_fusion.4), calls=%async_computation.1 | async-start | bytes 65536 | tf_op jit(solution)/shard_map/all_to_all | solution.py:114
  59.8 5.4 %copy-start.29 = (pred[1536]{0:T(1024)(128)(4,1)S(1)}, pred[1536]{0:T(1024)(128)(4,1)}, u32[]{:S(2)}) copy-start(pred[1536]{0:T(1024)(128)(4,1)} %compare_and_fusion.2) | copy-start | bytes 4612
  65.2 3.8 %copy-start.9 = (bf16[1536,512]{1,0:T(8,128)(2,1)S(1)}, bf16[1536,512]{1,0:T(8,128)(2,1)}, u32[]{:S(2)}) copy-start(bf16[1536,512]{1,0:T(8,128)(2,1)} %gather_fusion.3) | copy-start | bytes 4718596
  65.2 3.8 %copy-start.19 = (bf16[512,512]{1,0:T(8,128)(2,1)S(1)}, bf16[512,512]{1,0:T(8,128)(2,1)}, u32[]{:S(2)}) copy-start(bf16[512,512]{1,0:T(8,128)(2,1)} %param.31) | copy-start | bytes 1572868
  65.3 3.8 %copy-start.31 = (pred[1536]{0:T(1024)(128)(4,1)S(1)}, pred[1536]{0:T(1024)(128)(4,1)}, u32[]{:S(2)}) copy-start(pred[1536]{0:T(1024)(128)(4,1)} %get-tuple-element.37) | copy-start | bytes 4612
  65.3 3.8 %copy-start.35 = (f32[512]{0:T(512)S(1)}, f32[512]{0:T(512)}, u32[]{:S(2)}) copy-start(f32[512]{0:T(512)} %param.32) | copy-start | bytes 6148
  69.1 1.1 copy-start.37
  70.2 1.6 copy-start.10
  71.8 1.7 copy-start.3
  71.8 1.7 copy-start.26
  75.7 14.7 %copy-start.13 = (f32[320,512]{1,0:T(8,128)S(1)}, f32[320,512]{1,0:T(8,128)}, u32[]{:S(2)}) copy-start(f32[320,512]{1,0:T(8,128)} %fusion.71) | copy-start | bytes 1966084
  75.7 14.7 %copy-start.34 = (f32[512]{0:T(512)S(1)}, f32[512]{0:T(512)}, u32[]{:S(2)}) copy-start(f32[512]{0:T(512)} %param.38) | copy-start | bytes 6148
  79.3 12.7 %copy-start.38 = (f32[512]{0:T(512)S(1)}, f32[512]{0:T(512)}, u32[]{:S(2)}) copy-start(f32[512]{0:T(512)} %param.40) | copy-start | bytes 6148
  90.4 3.2 %copy-start.12 = (bf16[320,512]{1,0:T(8,128)(2,1)S(1)}, bf16[320,512]{1,0:T(8,128)(2,1)}, u32[]{:S(2)}) copy-start(bf16[320,512]{1,0:T(8,128)(2,1)} %param.27) | copy-start | bytes 983044
  90.4 3.2 %copy-start.28 = (f32[512]{0:T(512)S(1)}, f32[512]{0:T(512)}, u32[]{:S(2)}) copy-start(f32[512]{0:T(512)} %param.41) | copy-start | bytes 6148
  92.0 3.0 %copy-start.36 = (bf16[512,512]{1,0:T(8,128)(2,1)S(1)}, bf16[512,512]{1,0:T(8,128)(2,1)}, u32[]{:S(2)}) copy-start(bf16[512,512]{1,0:T(8,128)(2,1)} %param.39) | copy-start | bytes 1572868
  95.0 1.0 copy-start.14
  95.1 1.8 %copy-start.22 = (s32[2048]{0:T(1024)S(1)}, s32[2048]{0:T(1024)}, u32[]{:S(2)}) copy-start(s32[2048]{0:T(1024)} %get-tuple-element.54) | copy-start | bytes 24580
  96.1 0.7 copy-start.16
  102.2 2.6 %copy-start.27 = (pred[1536]{0:T(1024)(128)(4,1)S(1)}, pred[1536]{0:T(1024)(128)(4,1)}, u32[]{:S(2)}) copy-start(pred[1536]{0:T(1024)(128)(4,1)} %get-tuple-element.36) | copy-start | bytes 4612
  104.8 3.5 %copy-start.4 = (f32[1536,512]{0,1:T(8,128)S(1)}, f32[1536,512]{0,1:T(8,128)}, u32[]{:S(2)}) copy-start(f32[1536,512]{0,1:T(8,128)} %copy-done.3) | copy-start | bytes 9437188
  104.8 3.8 %copy-start.5 = (bf16[1536,512]{0,1:T(8,128)(2,1)S(1)}, bf16[1536,512]{0,1:T(8,128)(2,1)}, u32[]{:S(2)}) copy-start(bf16[1536,512]{0,1:T(8,128)(2,1)} %copy.52) | copy-start | bytes 4718596
  104.8 4.2 %copy-start.7 = (bf16[1536,512]{0,1:T(8,128)(2,1)S(1)}, bf16[1536,512]{0,1:T(8,128)(2,1)}, u32[]{:S(2)}) copy-start(bf16[1536,512]{0,1:T(8,128)(2,1)} %copy.51) | copy-start | bytes 4718596
  109.1 3.0 %copy-start.11 = (f32[1536,512]{1,0:T(8,128)S(1)}, f32[1536,512]{1,0:T(8,128)}, u32[]{:S(2)}) copy-start(f32[1536,512]{1,0:T(8,128)} %copy-done.10) | copy-start | bytes 9437188
  112.1 2.0 %copy-start.18 = (bf16[512,512]{1,0:T(8,128)(2,1)S(1)}, bf16[512,512]{1,0:T(8,128)(2,1)}, u32[]{:S(2)}) copy-start(bf16[512,512]{1,0:T(8,128)(2,1)} %param.30) | copy-start | bytes 1572868
  114.1 2.2 %copy-start.39 = (bf16[1536,512]{1,0:T(8,128)(2,1)}, bf16[1536,512]{1,0:T(8,128)(2,1)S(1)}, u32[]{:S(2)}) copy-start(bf16[1536,512]{1,0:T(8,128)(2,1)S(1)} %fusion.2) | copy-start | bytes 4718596
  114.1 2.2 %copy-start.20 = (bf16[512,512]{1,0:T(8,128)(2,1)S(1)}, bf16[512,512]{1,0:T(8,128)(2,1)}, u32[]{:S(2)}) copy-start(bf16[512,512]{1,0:T(8,128)(2,1)} %param.31) | copy-start | bytes 1572868
  131.9 14.5 %copy-start.17 = (bf16[320,512]{1,0:T(8,128)(2,1)S(1)}, bf16[320,512]{1,0:T(8,128)(2,1)}, u32[]{:S(2)}) copy-start(bf16[320,512]{1,0:T(8,128)(2,1)} %copy-done.16) | copy-start | bytes 983044
  135.6 12.4 %copy-start.8 = (bf16[1536,512]{0,1:T(8,128)(2,1)S(1)}, bf16[1536,512]{0,1:T(8,128)(2,1)}, u32[]{:S(2)}) copy-start(bf16[1536,512]{0,1:T(8,128)(2,1)} %get-tuple-element.29) | copy-start | bytes 4718596
  135.7 26.9 %collective-permute-start.4 = (bf16[64,512]{1,0:T(8,128)(2,1)}, bf16[64,512]{1,0:T(8,128)(2,1)}, u32[]{:S(2)}, u32[]{:S(2)}) collective-permute-start(bf16[64,512]{1,0:T(8,128)(2,1)} %get-tuple-element.35), channel_id=1, source_target_pairs={{0,15},{1,0},{2,1},{3,2},{4,3},{5,4},{6,5},{7,6},{8,7},{9,8},{10,9... | collective-permute-start | bytes 196616 | tf_op jit(solution)/shard_map/ppermute | solution.py:12
  135.8 28.3 %collective-permute-start.5 = (bf16[64,512]{1,0:T(8,128)(2,1)}, bf16[64,512]{1,0:T(8,128)(2,1)}, u32[]{:S(2)}, u32[]{:S(2)}) collective-permute-start(bf16[64,512]{1,0:T(8,128)(2,1)} %get-tuple-element.34), channel_id=1, source_target_pairs={{0,1},{1,2},{2,3},{3,4},{4,5},{5,6},{6,7},{7,8},{8,9},{9,10},{10,1... | collective-permute-start | bytes 196616 | tf_op jit(solution)/shard_map/ppermute | solution.py:12
  136.2 29.6 %collective-permute-start.6 = (bf16[64,512]{1,0:T(8,128)(2,1)}, bf16[64,512]{1,0:T(8,128)(2,1)}, u32[]{:S(2)}, u32[]{:S(2)}) collective-permute-start(bf16[64,512]{1,0:T(8,128)(2,1)} %get-tuple-element.33), channel_id=1, source_target_pairs={{0,14},{1,15},{2,0},{3,1},{4,2},{5,3},{6,4},{7,5},{8,6},{9,7},{10,... | collective-permute-start | bytes 196616 | tf_op jit(solution)/shard_map/ppermute | solution.py:12
  137.3 30.0 %collective-permute-start.7 = (bf16[64,512]{1,0:T(8,128)(2,1)S(1)}, bf16[64,512]{1,0:T(8,128)(2,1)}, u32[]{:S(2)}, u32[]{:S(2)}) collective-permute-start(bf16[64,512]{1,0:T(8,128)(2,1)S(1)} %get-tuple-element.32), channel_id=1, source_target_pairs={{0,2},{1,3},{2,4},{3,5},{4,6},{5,7},{6,8},{7,9},{8,10},{9,11},{10,... | collective-permute-start | bytes 196616 | tf_op jit(solution)/shard_map/ppermute | solution.py:12
  138.8 23.7 %all-to-all-start.2 = ((bf16[16,2,512]{2,1,0:T(2,128)(2,1)}), bf16[16,2,512]{2,1,0:T(2,128)(2,1)S(1)}, u32[]{:S(2)}, u32[]{:S(2)}) async-start(bf16[16,2,512]{2,1,0:T(2,128)(2,1)} %convert_element_type.159), calls=%async_computation.2 | async-start | bytes 65536 | tf_op jit(solution)/shard_map/all_to_all | solution.py:142
  149.7 2.7 %copy-start.15 = (bf16[1536,512]{1,0:T(8,128)(2,1)S(1)}, bf16[1536,512]{1,0:T(8,128)(2,1)}, u32[]{:S(2)}) copy-start(bf16[1536,512]{1,0:T(8,128)(2,1)} %fusion.73) | copy-start | bytes 4718596
  152.4 16.5 %copy-start.33 = (s32[32]{0:T(128)S(1)}, s32[32]{0:T(128)}, u32[]{:S(2)}) copy-start(s32[32]{0:T(128)} %copy-done.32) | copy-start | bytes 388
where the time goes:
time: 172 us; the launch traced here: 171 us
  other arithmetic  58.3 us (34%)
  local copies, waits for them, and re-layouts  46 us (27%)
  starting transfers between devices  30 us (17%)
  matrix products  27.8 us (16%)
  waiting for transfers between devices  6.63 us (4%)
  between operations  2.02 us (1%)
    ppermute x8, starting transfers between devices, passed_along(): return lax.ppermute(value, axis, pairs)  12.9 us
    unnamed x89, local copies, waits for them, and re-layouts  11.7 us
    scatter-add x1, other arithmetic, layer(): send_rows = jnp.take(table, sending_patch, axis=0).astype(jnp.bfloat16)  11.4 us
    scatter-add x1, other arithmetic, layer(): jax.ops.segment_sum(sent_message.astype(jnp.float32), receiver, num_segme...  11.1 us
    scatter-add x1, other arithmetic, layer(): recv_rows = jnp.take(node_rows, receiver, axis=0).astype(jnp.bfloat16)  10.2 us
    gather x2, local copies, waits for them, and re-layouts, layer(): jax.ops.segment_sum(sent_message.astype(jnp.float32), receiver, num_segme...  7.98 us
    all_to_all x1, starting transfers between devices, local(): lax.all_to_all(far_grad.astype(jnp.bfloat16), 'patch', split_axis=0, conc...  7.62 us
    dot_general x2, matrix products, layer(): jnp.dot(edge_rows.astype(jnp.bfloat16), w_edge, preferred_element_type=jn...  7.39 us
  transfers between devices with their start and end apart: 11, of which 1 were waited for; matrix products, arithmetic and copies ran while one was open for 29% of the time, Pallas kernels for 0%

commit v1 on v0

v1 whole, which is shorter than its diff:
```python
import jax
import jax.numpy as jnp
from jax import lax
from jax.experimental import pallas as pl
from jax.experimental.pallas import tpu as pltpu
from jax.sharding import PartitionSpec as P

BLOCK = 128
LANES = 128
ROWS = 256
CHUNK = 32
EPS = 1e-05
BF = jnp.bfloat16
F32 = jnp.float32


def passed_along(value, axis, steps):
    count = lax.axis_size(axis)
    pairs = [(source, (source + steps) % count) for source in range(count)]
    return lax.ppermute(value, axis, pairs)


def mm(a, b):
    return lax.dot_general(a, b, (((1,), (0,)), ((), ())), preferred_element_type=F32)


def mm_t(a, b):
    return lax.dot_general(a, b, (((1,), (1,)), ((), ())), preferred_element_type=F32)


def mm_l(a, b):
    return lax.dot_general(a, b, (((0,), (0,)), ((), ())), preferred_element_type=F32)


def ones_where(mask):
    return jnp.where(mask, 1.0, 0.0).astype(BF)


def as_columns(row):
    return jnp.broadcast_to(row.astype(F32), (LANES, LANES)).T.astype(jnp.int32)


def lane_ids(tile):
    return lax.broadcasted_iota(jnp.int32, (LANES, LANES), 1) + tile * LANES


def own_pick(send, recv, own):
    sender = as_columns(jnp.where(send < own, send, -1))
    receiver = as_columns(recv + own)
    tiles = []
    for tile in range(2 * own // LANES):
        ids = lane_ids(tile)
        if (tile + 1) * LANES <= own:
            hit = sender == ids
        elif tile * LANES >= own:
            hit = receiver == ids
        else:
            hit = (sender == ids) | (receiver == ids)
        tiles.append(ones_where(hit))
    return jnp.concatenate(tiles, axis=1)


def own_pick_t(send, recv, own):
    sender = jnp.where(send < own, send, -1)
    ids = lax.broadcasted_iota(jnp.int32, (own, LANES), 0)
    return jnp.concatenate([ones_where(ids == sender), ones_where(ids == recv)], axis=0)


def remote_index(send, own, near, peers, shift):
    far = send - (own + near)
    far_index = near + (far & ((1 << shift) - 1)) * peers + (far >> shift)
    return jnp.where(send < own + near, send - own, far_index)


def pick(row, width):
    column = as_columns(row)
    return jnp.concatenate(
        [ones_where(column == lane_ids(tile)) for tile in range(width // LANES)], axis=1
    )


def pick_t(row, height):
    return ones_where(lax.broadcasted_iota(jnp.int32, (height, LANES), 0) == row)


def silu_parts(value):
    gate = 0.5 * jnp.tanh(0.5 * value) + 0.5
    hidden = value * gate
    slope = gate * (1.0 + value - hidden)
    return hidden, slope


def norm_parts(value):
    center = value - jnp.mean(value, axis=-1, keepdims=True)
    inverse = lax.rsqrt(jnp.mean(center * center, axis=-1, keepdims=True) + EPS)
    return center * inverse, inverse


def norm_back(grad, unit, inverse):
    first = jnp.mean(grad, axis=-1, keepdims=True)
    second = jnp.mean(grad * unit, axis=-1, keepdims=True)
    return inverse * (grad - first - unit * second)


def pack_kernel(nodes, lists, coarse, *outs):
    rows = nodes[...]
    own = rows.shape[0]
    steps, width = lists.shape
    ids = lax.broadcasted_iota(jnp.int32, (own, width), 0)
    for index in range(steps):
        hit = ones_where(ids == lists[index : index + 1, :])
        outs[index][...] = mm_l(hit, rows).astype(BF)
    count = coarse.shape[1]
    hit = ones_where(lax.broadcasted_iota(jnp.int32, (own, count), 0) == coarse[...])
    picked = mm_l(hit, rows).astype(BF)
    out = outs[steps]

    def put(index, carry):
        out[index] = picked
        return carry

    lax.fori_loop(0, out.shape[0], put, 0)


def local_kernel(nodes, edges, w_edge, w_send, w_recv, bias, send, recv, out, table):
    own = nodes.shape[0]
    rows = nodes[...]
    table[:own] = mm(rows, w_send[...]).astype(BF)
    table[own:] = mm(rows, w_recv[...]).astype(BF)
    parts = ROWS // LANES

    def step(index, carry):
        start = pl.multiple_of(index * ROWS, ROWS)
        hit = jnp.concatenate(
            [
                own_pick(
                    send[pl.ds(index * parts + part, 1), :],
                    recv[pl.ds(index * parts + part, 1), :],
                    own,
                )
                for part in range(parts)
            ],
            axis=0,
        )
        value = mm(edges[pl.ds(start, ROWS), :], w_edge[...]) + mm(hit, table[...]) + bias[...]
        out[pl.ds(start, ROWS), :] = value
        return carry

    lax.fori_loop(0, edges.shape[0] // ROWS, step, 0)


def main_kernel(
    shift,
    steps,
    count,
    *refs,
):
    (pre_in, edges, edge_cot, nodes, node_cot, send, recv, far_lists, coarse) = refs[:9]
    near = refs[9 : 9 + steps]
    (
        w_send,
        w_edge_out,
        edge_out_bias,
        edge_gain,
        w_node,
        w_agg,
        node_bias,
        w_node_out,
        node_out_bias,
        node_gain,
    ) = refs[9 + steps : 19 + steps]
    (new_nodes, new_edges, d_pre, d_node) = refs[19 + steps : 23 + steps]
    near_out = refs[23 + steps : 23 + 2 * steps]
    far_out = refs[23 + 2 * steps]
    (rows2, table2, slope, unit, inverse, agg, d_agg, sums2) = refs[24 + 2 * steps :]
    own = nodes.shape[0]
    width = nodes.shape[1]
    peers, far_width = far_lists.shape
    near_width = near[0].shape[0]
    near_rows = steps * near_width
    height = table2.shape[0]
    coarse_rows = coarse.shape[0] // peers
    parts = ROWS // LANES
    blocks = edges.shape[0] // ROWS
    live_count = count[0]

    far_ids = lax.broadcasted_iota(jnp.int32, (peers, coarse.shape[0]), 1)
    far_base = lax.broadcasted_iota(jnp.int32, (peers, coarse.shape[0]), 0) * coarse_rows
    far_hits = [
        ones_where(far_ids == far_base + far_lists[:, slot : slot + 1])
        for slot in range(far_width)
    ]
    rows2[...] = jnp.zeros(rows2.shape, BF)
    for index in range(steps):
        rows2[index * near_width : (index + 1) * near_width] = near[index][...]
    for slot in range(far_width):
        start = near_rows + slot * peers
        rows2[start : start + peers] = mm(far_hits[slot], coarse[...]).astype(BF)
    table2[...] = mm(rows2[...], w_send[...]).astype(BF)
    agg[...] = jnp.zeros(agg.shape, F32)

    def block_rows(ref, index, part):
        return ref[pl.ds(index * parts + part, 1), :]

    def ahead(index, carry):
        start = pl.multiple_of(index * ROWS, ROWS)
        hit = jnp.concatenate(
            [
                pick(remote_index(block_rows(send, index, part), own, near_rows, peers, shift), height)
                for part in range(parts)
            ],
            axis=0,
        )
        remote = mm(hit, table2[...])
        hidden = []
        for low in range(0, ROWS, CHUNK):
            here = pl.ds(start + low, CHUNK)
            value = pre_in[here, :] + remote[low : low + CHUNK]
            part_hidden, part_slope = silu_parts(value)
            slope[here, :] = part_slope
            hidden.append(part_hidden.astype(BF))
        out = mm(jnp.concatenate(hidden, axis=0), w_edge_out[...])
        sent = []
        for low in range(0, ROWS, CHUNK):
            here = pl.ds(start + low, CHUNK)
            live = jnp.where(index * parts + low // BLOCK < live_count, 1.0, 0.0).astype(F32)
            part_unit, part_inverse = norm_parts(out[low : low + CHUNK] + edge_out_bias[...])
            unit[here, :] = part_unit
            inverse[here, :] = part_inverse
            message = part_unit * (edge_gain[...] * live)
            new_edges[here, :] = (edges[here, :].astype(F32) + message).astype(BF)
            sent.append(message.astype(BF))
        hit_t = jnp.concatenate(
            [pick_t(block_rows(recv, index, part), own) for part in range(parts)], axis=1
        )
        agg[...] += mm(hit_t, jnp.concatenate(sent, axis=0))
        return carry

    lax.fori_loop(0, blocks, ahead, 0)

    rows = nodes[...]
    pre_node = mm(rows, w_node[...]) + mm(agg[...].astype(BF), w_agg[...]) + node_bias[...]
    node_hidden, node_slope = silu_parts(pre_node)
    node_out = mm(node_hidden.astype(BF), w_node_out[...]) + node_out_bias[...]
    node_unit, node_inverse = norm_parts(node_out)
    new_nodes[...] = (rows.astype(F32) + node_gain[...] * node_unit).astype(BF)
    cot = node_cot[...].astype(F32)
    d_out = norm_back(cot * node_gain[...], node_unit, node_inverse).astype(BF)
    d_hidden = mm_t(d_out, w_node_out[...]).astype(BF).astype(F32)
    d_pre_node = (d_hidden * node_slope).astype(BF)
    d_agg[...] = jnp.zeros(d_agg.shape, BF)
    d_agg[:own] = mm_t(d_pre_node, w_agg[...]).astype(BF)
    d_node[...] = cot + mm_t(d_pre_node, w_node[...])
    sums2[...] = jnp.zeros(sums2.shape, F32)

    def back(index, carry):
        start = pl.multiple_of(index * ROWS, ROWS)
        hit = jnp.concatenate(
            [pick(block_rows(recv, index, part), d_agg.shape[0]) for part in range(parts)], axis=0
        )
        d_sent = mm(hit, d_agg[...])
        outs = []
        for low in range(0, ROWS, CHUNK):
            here = pl.ds(start + low, CHUNK)
            live = jnp.where(index * parts + low // BLOCK < live_count, 1.0, 0.0).astype(F32)
            d_message = edge_cot[here, :].astype(F32) + d_sent[low : low + CHUNK]
            d_unit = d_message * (edge_gain[...] * live)
            outs.append(norm_back(d_unit, unit[here, :], inverse[here, :]).astype(BF))
        d_hid = mm_t(jnp.concatenate(outs, axis=0), w_edge_out[...])
        pres = []
        for low in range(0, ROWS, CHUNK):
            here = pl.ds(start + low, CHUNK)
            part = (d_hid[low : low + CHUNK] * slope[here, :]).astype(BF)
            d_pre[here, :] = part
            pres.append(part)
        hit_t = jnp.concatenate(
            [
                pick_t(
                    remote_index(block_rows(send, index, part), own, near_rows, peers, shift),
                    height,
                )
                for part in range(parts)
            ],
            axis=1,
        )
        sums2[...] += mm(hit_t, jnp.concatenate(pres, axis=0))
        return carry

    lax.fori_loop(0, blocks, back, 0)

    d_rows2 = mm_t(sums2[...].astype(BF), w_send[...])
    for index in range(steps):
        near_out[index][...] = d_rows2[index * near_width : (index + 1) * near_width].astype(BF)
    d_coarse = None
    for slot in range(far_width):
        start = near_rows + slot * peers
        term = mm_l(far_hits[slot], d_rows2[start : start + peers].astype(BF))
        d_coarse = term if d_coarse is None else d_coarse + term
    far_out[...] = d_coarse.astype(BF)


def local_back_kernel(d_pre, edge_cot, d_node, w_edge, w_send, w_recv, send, recv, edge_grad, node_sum, sums):
    own = d_node.shape[0]
    parts = ROWS // LANES
    sums[...] = jnp.zeros(sums.shape, F32)

    def step(index, carry):
        start = pl.multiple_of(index * ROWS, ROWS)
        here = pl.ds(start, ROWS)
        grads = d_pre[here, :]
        value = edge_cot[here, :].astype(F32) + mm_t(grads, w_edge[...])
        edge_grad[here, :] = value.astype(BF)
        hit = jnp.concatenate(
            [
                own_pick_t(
                    send[pl.ds(index * parts + part, 1), :],
                    recv[pl.ds(index * parts + part, 1), :],
                    own,
                )
                for part in range(parts)
            ],
            axis=1,
        )
        sums[...] += mm(hit, grads)
        return carry

    lax.fori_loop(0, d_pre.shape[0] // ROWS, step, 0)
    total = sums[...].astype(BF)
    node_sum[...] = d_node[...] + mm_t(total[:own], w_send[...]) + mm_t(total[own:], w_recv[...])


def combine_kernel(coarse, node_sum, lists, far, *refs):
    steps, width = lists.shape
    near = refs[:steps]
    out, total = refs[steps], refs[steps + 1]
    own = node_sum.shape[0]
    ids = lax.broadcasted_iota(jnp.int32, (own, width), 0)
    value = node_sum[...]
    for index in range(steps):
        value = value + mm(ones_where(ids == lists[index : index + 1, :]), near[index][...])
    total[...] = value
    peers, count, _ = far.shape

    def add(index, carry):
        return carry + far[index].astype(F32)

    grads = lax.fori_loop(0, peers, add, jnp.zeros(far.shape[1:], F32))
    for index in range(count):
        here = pl.ds(coarse[index], 1)
        total[here, :] = total[here, :] + grads[index : index + 1]
    out[...] = total[...].astype(BF)


def vmem(count):
    return [pl.BlockSpec(memory_space=pltpu.VMEM) for _ in range(count)]


def smem():
    return pl.BlockSpec(memory_space=pltpu.SMEM)


def local(
    nodes,
    edges,
    node_cot,
    edge_cot,
    w_edge,
    w_send,
    w_recv,
    edge_bias,
    w_edge_out,
    edge_out_bias,
    edge_gain,
    w_node,
    w_agg,
    node_bias,
    w_node_out,
    node_out_bias,
    node_gain,
    send_slots,
    recv_slots,
    neighbour_send_lists,
    coarse_rows,
    far_lists,
    block_count,
):
    own, width = nodes.shape
    hidden = w_edge.shape[1]
    edge_rows = edges.shape[0]
    peers = lax.axis_size("patch")
    steps, near_width = neighbour_send_lists.shape
    offsets = [(index // 2 + 1) * (1 - 2 * (index % 2)) for index in range(steps)]
    coarse_count = coarse_rows.shape[0]
    far_width = far_lists.shape[2]
    shift = far_width.bit_length() - 1
    if far_width != 1 << shift or own % 64 or edge_rows % ROWS or hidden != width:
        raise ValueError("unsupported sizes")
    slots = steps * near_width + peers * far_width
    height = -(-slots // LANES) * LANES
    own_pad = -(-own // LANES) * LANES
    send = send_slots.reshape(-1, LANES)
    recv = recv_slots.reshape(-1, LANES)
    row = lambda value: value.reshape(1, -1)
    shape = jax.ShapeDtypeStruct

    packed = pl.pallas_call(
        pack_kernel,
        out_shape=[shape((near_width, width), BF)] * steps
        + [shape((peers, coarse_count, width), BF)],
        in_specs=vmem(3),
        out_specs=vmem(steps + 1),
        name="pack",
    )(nodes, neighbour_send_lists, row(coarse_rows))
    near = [passed_along(packed[index], "patch", offsets[index]) for index in range(steps)]
    coarse = lax.all_to_all(
        packed[steps], "patch", split_axis=0, concat_axis=0, tiled=True
    ).reshape(-1, width)

    pre_local = pl.pallas_call(
        local_kernel,
        out_shape=shape((edge_rows, hidden), F32),
        in_specs=vmem(8),
        out_specs=vmem(1)[0],
        scratch_shapes=[pltpu.VMEM((2 * own, hidden), BF)],
        cost_estimate=pl.CostEstimate(
            flops=2 * edge_rows * width * hidden * 3, transcendentals=0, bytes_accessed=6 << 20
        ),
        name="local_ahead",
    )(nodes, edges, w_edge, w_send, w_recv, row(edge_bias), send, recv)

    outs = pl.pallas_call(
        lambda *refs: main_kernel(shift, steps, *refs),
        out_shape=[
            shape((own, width), BF),
            shape((edge_rows, width), BF),
            shape((edge_rows, hidden), BF),
            shape((own, width), F32),
        ]
        + [shape((near_width, width), BF)] * steps
        + [shape((peers * coarse_count, width), BF)],
        in_specs=[smem()] + vmem(19 + steps),
        out_specs=vmem(5 + steps),
        scratch_shapes=[
            pltpu.VMEM((height, width), BF),
            pltpu.VMEM((height, hidden), BF),
            pltpu.VMEM((edge_rows, hidden), F32),
            pltpu.VMEM((edge_rows, width), F32),
            pltpu.VMEM((edge_rows, 1), F32),
            pltpu.VMEM((own, width), F32),
            pltpu.VMEM((own_pad, width), BF),
            pltpu.VMEM((height, hidden), F32),
        ],
        cost_estimate=pl.CostEstimate(
            flops=2 * edge_rows * width * hidden * 8, transcendentals=0, bytes_accessed=16 << 20
        ),
        name="main",
    )(
        block_count,
        pre_local,
        edges,
        edge_cot,
        nodes,
        node_cot,
        send,
        recv,
        far_lists[0],
        coarse,
        *near,
        w_send,
        w_edge_out,
        row(edge_out_bias),
        row(edge_gain),
        w_node,
        w_agg,
        row(node_bias),
        w_node_out,
        row(node_out_bias),
        row(node_gain),
    )
    new_nodes, new_edges, d_pre, d_node = outs[:4]
    returned = [
        passed_along(outs[4 + index], "patch", -offsets[index]) for index in range(steps)
    ]
    far_back = lax.all_to_all(
        outs[4 + steps].reshape(peers, coarse_count, width),
        "patch",
        split_axis=0,
        concat_axis=0,
        tiled=True,
    )

    edge_grad, node_sum = pl.pallas_call(
        local_back_kernel,
        out_shape=[shape((edge_rows, width), BF), shape((own, width), F32)],
        in_specs=vmem(8),
        out_specs=vmem(2),
        scratch_shapes=[pltpu.VMEM((2 * own, hidden), F32)],
        cost_estimate=pl.CostEstimate(
            flops=2 * edge_rows * width * hidden * 3, transcendentals=0, bytes_accessed=6 << 20
        ),
        name="local_back",
    )(d_pre, edge_cot, d_node, w_edge, w_send, w_recv, send, recv)

    node_grad = pl.pallas_call(
        combine_kernel,
        out_shape=shape((own, width), BF),
        in_specs=[smem()] + vmem(3 + steps),
        out_specs=vmem(1)[0],
        scratch_shapes=[pltpu.VMEM((own, width), F32)],
        name="combine",
    )(coarse_rows, node_sum, neighbour_send_lists, far_back, *returned)
    return new_nodes, new_edges, node_grad, edge_grad


def solution(mesh):
    rows = P(("groups", "patch"), None)
    placed = (
        (rows,) * 4
        + (P(),) * 13
        + (
            P("patch"),
            P("patch"),
            P("patch", None),
            P("patch"),
            P("patch", None, None),
            P("patch"),
        )
    )
    return jax.shard_map(
        local,
        mesh=mesh,
        in_specs=placed,
        out_specs=(rows,) * 4,
        check_vma=False,
    )
```

time: 172 us -> 71.8 us (0.42)
  the two profiles are of different devices: /device:TPU:0 before, /device:TPU:1 now
where the time goes in v1:
time: 71.8 us; the launch traced here: 71.5 us
  Pallas kernels  39.4 us (55%)
  starting transfers between devices  28.6 us (40%)
  local copies, waits for them, and re-layouts  2.04 us (3%)
  between operations  1.43 us (2%)
    pallas_call x1, Pallas kernels, local(): pl.pallas_call(lambda *refs: main_kernel(shift, steps, *refs), out_shape=...  20.1 us
    ppermute x8, starting transfers between devices, passed_along(): return lax.ppermute(value, axis, pairs)  14.4 us
    pallas_call x1, Pallas kernels, local(): pl.pallas_call(local_kernel, out_shape=shape((edge_rows, hidden), F32), i...  7.49 us
    all_to_all x1, starting transfers between devices, local(): lax.all_to_all(packed[steps], 'patch', split_axis=0, concat_axis=0, tiled...  7.34 us
    pallas_call x1, Pallas kernels, local(): pl.pallas_call(local_back_kernel, out_shape=[shape((edge_rows, width), BF...  7.01 us
    all_to_all x1, starting transfers between devices, local(): lax.all_to_all(outs[4 + steps].reshape(peers, coarse_count, width), 'patc...  6.83 us
    pallas_call x1, Pallas kernels, local(): pl.pallas_call(combine_kernel, out_shape=shape((own, width), BF), in_spec...  2.55 us
    pallas_call x1, Pallas kernels, local(): pl.pallas_call(pack_kernel, out_shape=[shape((near_width, width), BF)] *...  2.25 us
  transfers between devices with their start and end apart: 10, of which 0 were waited for; matrix products, arithmetic and copies ran while one was open for 1% of the time, Pallas kernels for 20%

profile of v1, /device:TPU:1, one launch (start us, length us, event | category | flops | bytes accessed | tf_op | source)
XLA Modules:
  0.0 71.5 jit_solution(16997075181957770949)
XLA Ops:
  0.6 2.2 %pack.1 = (bf16[64,512]{1,0:T(8,128)(2,1)}, bf16[64,512]{1,0:T(8,128)(2,1)}, bf16[64,512]{1,0:T(8,128)(2,1)}, bf16[64,512]{1,0:T(8,128)(2,1)}, bf16[16,8,512]{2,1,0:T(8,128)(2,1)}) custom-call(bf16[320,512]{1,0:T(8,128)(2,1)} %refs_4_.1, s32[4,64]{1,0:T(4,128)} %lists.3, s32[1,8]{1,0:T(1,128)} %bitcast.14), custom_call_target="tpu_custom_call" | custom-call | tf_op jit(solution)/shard_map/pack/pallas_call | solution.py:406
  2.9 7.3 %all-to-all-start = ((bf16[16,8,512]{2,1,0:T(8,128)(2,1)}), bf16[16,8,512]{2,1,0:T(8,128)(2,1)S(1)}, u32[]{:S(2)}, u32[]{:S(2)}) async-start(bf16[16,8,512]{2,1,0:T(8,128)(2,1)} %get-tuple-element.20), calls=%async_computation | async-start | bytes 262144 | tf_op jit(solution)/shard_map/all_to_all | solution.py:415
  10.2 1.6 %collective-permute-start = (bf16[64,512]{1,0:T(8,128)(2,1)}, bf16[64,512]{1,0:T(8,128)(2,1)S(1)}, u32[]{:S(2)}, u32[]{:S(2)}) collective-permute-start(bf16[64,512]{1,0:T(8,128)(2,1)} %get-tuple-element.21), channel_id=1, source_target_pairs={{0,1},{1,2},{2,3},{3,4},{4,5},{5,6},{6,7},{7,8},{8,9},{9,10},{10,1... | collective-permute-start | bytes 196616 | tf_op jit(solution)/shard_map/ppermute | solution.py:20
  11.8 0.0 collective-permute-start.1
  11.8 1.2 %collective-permute-start.2 = (bf16[64,512]{1,0:T(8,128)(2,1)}, bf16[64,512]{1,0:T(8,128)(2,1)S(1)}, u32[]{:S(2)}, u32[]{:S(2)}) collective-permute-start(bf16[64,512]{1,0:T(8,128)(2,1)} %get-tuple-element.23), channel_id=1, source_target_pairs={{0,2},{1,3},{2,4},{3,5},{4,6},{5,7},{6,8},{7,9},{8,10},{9,11},{10,... | collective-permute-start | bytes 196616 | tf_op jit(solution)/shard_map/ppermute | solution.py:20
  13.0 3.0 %collective-permute-start.3 = (bf16[64,512]{1,0:T(8,128)(2,1)}, bf16[64,512]{1,0:T(8,128)(2,1)S(1)}, u32[]{:S(2)}, u32[]{:S(2)}) collective-permute-start(bf16[64,512]{1,0:T(8,128)(2,1)} %get-tuple-element.24), channel_id=1, source_target_pairs={{0,14},{1,15},{2,0},{3,1},{4,2},{5,3},{6,4},{7,5},{8,6},{9,7},{10,... | collective-permute-start | bytes 196616 | tf_op jit(solution)/shard_map/ppermute | solution.py:20
  16.0 0.0 copy-start.6
  16.0 7.5 %local_ahead.1.refs_1_ = f32[1536,512]{1,0:T(8,128)} custom-call(bf16[320,512]{1,0:T(8,128)(2,1)} %refs_4_.1, bf16[1536,512]{1,0:T(8,128)(2,1)} %refs_2_.1, bf16[512,512]{1,0:T(8,128)(2,1)} %w_edge.3, bf16[512,512]{1,0:T(8,128)(2,1)} %w_send.3, bf16[512,512]{1,0:T(8,128)(2,1)} %w_recv.3, f32[1,512]{1,0:T(1,128)} %bitcast.22, s32[12,128]{1,0:T(8,128)} %bitcast.16, ...), custom_call_target="tpu_custom_call" | custom-call | flops 2415919104 | bytes 6291456 | tf_op jit(solution)/shard_map/local_ahead/pallas_call | solution.py:419
  24.2 0.0 copy-done.6
  24.2 0.7 copy.27.refs_8_
  24.9 0.0 collective-permute-done.refs_10_
  24.9 0.0 copy-start.7
  24.9 0.0 collective-permute-done.1.refs_11_
  24.9 0.0 copy-start.8
  24.9 0.0 collective-permute-done.2.refs_12_
  24.9 0.0 copy-start.9
  24.9 0.0 collective-permute-done.3.refs_13_
  24.9 0.0 copy-start.10
  24.9 0.0 all-to-all-done
  24.9 0.0 copy-start.1
  24.9 0.5 copy-done.7
  25.5 0.0 copy-done.8
  25.5 0.0 copy-done.9
  25.5 0.0 copy-done.10
  25.5 0.1 copy-done.1
  25.6 20.1 %main.1 = (bf16[320,512]{1,0:T(8,128)(2,1)}, bf16[1536,512]{1,0:T(8,128)(2,1)}, bf16[1536,512]{1,0:T(8,128)(2,1)}, f32[320,512]{1,0:T(8,128)}, bf16[64,512]{1,0:...) custom-call(s32[1]{0:T(128)S(6)} %copy.28.refs_0_, ...), custom_call_target="tpu_custom_call" | custom-call | flops 6442450944 | bytes 16777216 | tf_op jit(solution)/shard_map/main/pallas_call | solution.py:431
  45.7 6.8 %all-to-all-start.1 = ((bf16[16,8,512]{2,1,0:T(8,128)(2,1)}), bf16[16,8,512]{2,1,0:T(8,128)(2,1)S(1)}, u32[]{:S(2)}, u32[]{:S(2)}) async-start(bf16[16,8,512]{2,1,0:T(8,128)(2,1)} %bitcast.13), calls=%async_computation.1 | async-start | bytes 262144 | tf_op jit(solution)/shard_map/all_to_all | solution.py:484
  52.6 0.3 collective-permute-start.4
  52.8 1.5 %collective-permute-start.5 = (bf16[64,512]{1,0:T(8,128)(2,1)}, bf16[64,512]{1,0:T(8,128)(2,1)S(1)}, u32[]{:S(2)}, u32[]{:S(2)}) collective-permute-start(bf16[64,512]{1,0:T(8,128)(2,1)} %get-tuple-element.32), channel_id=1, source_target_pairs={{0,1},{1,2},{2,3},{3,4},{4,5},{5,6},{6,7},{7,8},{8,9},{9,10},{10,1... | collective-permute-start | bytes 196616 | tf_op jit(solution)/shard_map/ppermute | solution.py:20
  54.3 6.8 %collective-permute-start.6 = (bf16[64,512]{1,0:T(8,128)(2,1)}, bf16[64,512]{1,0:T(8,128)(2,1)S(1)}, u32[]{:S(2)}, u32[]{:S(2)}) collective-permute-start(bf16[64,512]{1,0:T(8,128)(2,1)} %get-tuple-element.33), channel_id=1, source_target_pairs={{0,14},{1,15},{2,0},{3,1},{4,2},{5,3},{6,4},{7,5},{8,6},{9,7},{10,... | collective-permute-start | bytes 196616 | tf_op jit(solution)/shard_map/ppermute | solution.py:20
  61.1 0.0 collective-permute-start.7
  61.1 7.0 %local_back.1 = (bf16[1536,512]{1,0:T(8,128)(2,1)}, f32[320,512]{1,0:T(8,128)}) custom-call(bf16[1536,512]{1,0:T(8,128)(2,1)} %get-tuple-element.27.d_pre, bf16[1536,512]{1,0:T(8,128)(2,1)} %edge_cot.1, f32[320,512]{1,0:T(8,128)} %get-tuple-element.28.d_node, bf16[512,512]{1,0:T(8,128)(2,1)} %w_edge.3, bf16[512,512]{1,0:T(8,128)(2,1)} %w_send.3, ...), custom_call_target="tpu_custom_call" | custom-call | flops 2415919104 | bytes 6291456 | tf_op jit(solution)/shard_map/local_back/pallas_call | solution.py:492
  68.1 0.0 collective-permute-done.4.refs_0_
  68.2 0.0 copy-start.2
  68.2 0.0 collective-permute-done.5.refs_1_
  68.2 0.0 copy-start.3
  68.2 0.0 collective-permute-done.6.refs_2_
  68.2 0.0 copy-start.4
  68.2 0.0 collective-permute-done.7.refs_3_
  68.2 0.0 copy-start.5
  68.2 0.0 all-to-all-done.1.far
  68.2 0.0 copy-start
  68.2 0.5 copy-done.2
  68.8 0.0 copy-done.3
  68.8 0.0 copy-done.4
  68.8 0.0 copy-done.5
  68.9 0.1 copy-done
  68.9 2.6 %combine.1 = bf16[320,512]{1,0:T(8,128)(2,1)} custom-call(s32[8]{0:T(128)} %coarse.1, f32[320,512]{1,0:T(8,128)} %get-tuple-element.29.node_sum, s32[4,64]{1,0:T(4,128)} %lists.3, bf16[16,8,512]{2,1,0:T(8,128)(2,1)} %copy-done, bf16[64,512]{1,0:T(8,128)(2,1)} %copy-done.2, bf16[64,512]{1,0:T(8,128)(2,1)} %copy-done.3, bf16[64,512]{1,0:T(8,128)(2,1)} %copy-done.4, ...), custom_call_target="tpu_custom_call" | custom-call | tf_op jit(solution)/shard_map/combine/pallas_call | solution.py:504
Async XLA Ops:
  2.9 22.0 %all-to-all-start = ((bf16[16,8,512]{2,1,0:T(8,128)(2,1)}), bf16[16,8,512]{2,1,0:T(8,128)(2,1)S(1)}, u32[]{:S(2)}, u32[]{:S(2)}) async-start(bf16[16,8,512]{2,1,0:T(8,128)(2,1)} %get-tuple-element.20), calls=%async_computation | async-start | bytes 262144 | tf_op jit(solution)/shard_map/all_to_all | solution.py:415
  10.2 14.6 %collective-permute-start = (bf16[64,512]{1,0:T(8,128)(2,1)}, bf16[64,512]{1,0:T(8,128)(2,1)S(1)}, u32[]{:S(2)}, u32[]{:S(2)}) collective-permute-start(bf16[64,512]{1,0:T(8,128)(2,1)} %get-tuple-element.21), channel_id=1, source_target_pairs={{0,1},{1,2},{2,3},{3,4},{4,5},{5,6},{6,7},{7,8},{8,9},{9,10},{10,1... | collective-permute-start | bytes 196616 | tf_op jit(solution)/shard_map/ppermute | solution.py:20
  11.8 13.0 %collective-permute-start.1 = (bf16[64,512]{1,0:T(8,128)(2,1)}, bf16[64,512]{1,0:T(8,128)(2,1)S(1)}, u32[]{:S(2)}, u32[]{:S(2)}) collective-permute-start(bf16[64,512]{1,0:T(8,128)(2,1)} %get-tuple-element.22), channel_id=1, source_target_pairs={{0,15},{1,0},{2,1},{3,2},{4,3},{5,4},{6,5},{7,6},{8,7},{9,8},{10,9... | collective-permute-start | bytes 196616 | tf_op jit(solution)/shard_map/ppermute | solution.py:20
  11.8 13.0 %collective-permute-start.2 = (bf16[64,512]{1,0:T(8,128)(2,1)}, bf16[64,512]{1,0:T(8,128)(2,1)S(1)}, u32[]{:S(2)}, u32[]{:S(2)}) collective-permute-start(bf16[64,512]{1,0:T(8,128)(2,1)} %get-tuple-element.23), channel_id=1, source_target_pairs={{0,2},{1,3},{2,4},{3,5},{4,6},{5,7},{6,8},{7,9},{8,10},{9,11},{10,... | collective-permute-start | bytes 196616 | tf_op jit(solution)/shard_map/ppermute | solution.py:20
  13.0 11.9 %collective-permute-start.3 = (bf16[64,512]{1,0:T(8,128)(2,1)}, bf16[64,512]{1,0:T(8,128)(2,1)S(1)}, u32[]{:S(2)}, u32[]{:S(2)}) collective-permute-start(bf16[64,512]{1,0:T(8,128)(2,1)} %get-tuple-element.24), channel_id=1, source_target_pairs={{0,14},{1,15},{2,0},{3,1},{4,2},{5,3},{6,4},{7,5},{8,6},{9,7},{10,... | collective-permute-start | bytes 196616 | tf_op jit(solution)/shard_map/ppermute | solution.py:20
  16.0 8.1 %copy-start.6 = (s32[1,16,2]{1,2,0:T(2,128)S(1)}, s32[1,16,2]{1,2,0:T(2,128)}, u32[]{:S(2)}) copy-start(s32[1,16,2]{1,2,0:T(2,128)} %param.44) | copy-start | bytes 388
  24.9 0.6 copy-start.7
  24.9 0.6 copy-start.8
  24.9 0.6 copy-start.9
  24.9 0.6 copy-start.10
  24.9 0.7 copy-start.1
  45.7 22.5 %all-to-all-start.1 = ((bf16[16,8,512]{2,1,0:T(8,128)(2,1)}), bf16[16,8,512]{2,1,0:T(8,128)(2,1)S(1)}, u32[]{:S(2)}, u32[]{:S(2)}) async-start(bf16[16,8,512]{2,1,0:T(8,128)(2,1)} %bitcast.13), calls=%async_computation.1 | async-start | bytes 262144 | tf_op jit(solution)/shard_map/all_to_all | solution.py:484
  52.6 15.6 %collective-permute-start.4 = (bf16[64,512]{1,0:T(8,128)(2,1)}, bf16[64,512]{1,0:T(8,128)(2,1)S(1)}, u32[]{:S(2)}, u32[]{:S(2)}) collective-permute-start(bf16[64,512]{1,0:T(8,128)(2,1)} %get-tuple-element.31), channel_id=1, source_target_pairs={{0,15},{1,0},{2,1},{3,2},{4,3},{5,4},{6,5},{7,6},{8,7},{9,8},{10,9... | collective-permute-start | bytes 196616 | tf_op jit(solution)/shard_map/ppermute | solution.py:20
  52.8 15.3 %collective-permute-start.5 = (bf16[64,512]{1,0:T(8,128)(2,1)}, bf16[64,512]{1,0:T(8,128)(2,1)S(1)}, u32[]{:S(2)}, u32[]{:S(2)}) collective-permute-start(bf16[64,512]{1,0:T(8,128)(2,1)} %get-tuple-element.32), channel_id=1, source_target_pairs={{0,1},{1,2},{2,3},{3,4},{4,5},{5,6},{6,7},{7,8},{8,9},{9,10},{10,1... | collective-permute-start | bytes 196616 | tf_op jit(solution)/shard_map/ppermute | solution.py:20
  54.3 13.9 %collective-permute-start.6 = (bf16[64,512]{1,0:T(8,128)(2,1)}, bf16[64,512]{1,0:T(8,128)(2,1)S(1)}, u32[]{:S(2)}, u32[]{:S(2)}) collective-permute-start(bf16[64,512]{1,0:T(8,128)(2,1)} %get-tuple-element.33), channel_id=1, source_target_pairs={{0,14},{1,15},{2,0},{3,1},{4,2},{5,3},{6,4},{7,5},{8,6},{9,7},{10,... | collective-permute-start | bytes 196616 | tf_op jit(solution)/shard_map/ppermute | solution.py:20
  61.1 7.1 %collective-permute-start.7 = (bf16[64,512]{1,0:T(8,128)(2,1)}, bf16[64,512]{1,0:T(8,128)(2,1)S(1)}, u32[]{:S(2)}, u32[]{:S(2)}) collective-permute-start(bf16[64,512]{1,0:T(8,128)(2,1)} %get-tuple-element.34), channel_id=1, source_target_pairs={{0,2},{1,3},{2,4},{3,5},{4,6},{5,7},{6,8},{7,9},{8,10},{9,11},{10,... | collective-permute-start | bytes 196616 | tf_op jit(solution)/shard_map/ppermute | solution.py:20
  68.2 0.6 copy-start.2
  68.2 0.6 copy-start.3
  68.2 0.6 copy-start.4
  68.2 0.7 copy-start.5
  68.2 0.7 copy-start

commit v2 on v1

--- a/solution.py
+++ b/solution.py
@@ -9,6 +9,7 @@
 LANES = 128
 ROWS = 256
 CHUNK = 32
+FIXED = 7
 EPS = 1e-05
 BF = jnp.bfloat16
 F32 = jnp.float32
@@ -122,15 +123,40 @@
     lax.fori_loop(0, out.shape[0], put, 0)
 
 
-def local_kernel(nodes, edges, w_edge, w_send, w_recv, bias, send, recv, out, table):
+def local_kernel(bias, send, recv, nodes_in, edges_in, w_send_in, w_recv_in, w_edge_in, out, *scratch):
+    nodes, edges, w_send, w_recv, w_edge, table, value, load, store = scratch
     own = nodes.shape[0]
+    parts = ROWS // LANES
+    blocks = edges.shape[0] // ROWS
+    fixed = [
+        pltpu.make_async_copy(source, target, load.at[index])
+        for index, (source, target) in enumerate(
+            [(nodes_in, nodes), (w_send_in, w_send), (w_recv_in, w_recv), (w_edge_in, w_edge)]
+        )
+    ]
+
+    def block_in(index):
+        here = pl.ds(pl.multiple_of(index * ROWS, ROWS), ROWS)
+        return pltpu.make_async_copy(edges_in.at[here, :], edges.at[here, :], load.at[4 + index])
+
+    def block_out(index):
+        here = pl.ds(pl.multiple_of(index * ROWS, ROWS), ROWS)
+        return pltpu.make_async_copy(value.at[here, :], out.at[here, :], store.at[index])
+
+    for copy in fixed:
+        copy.start()
+    for index in range(blocks):
+        block_in(index).start()
+    fixed[0].wait()
+    fixed[1].wait()
     rows = nodes[...]
     table[:own] = mm(rows, w_send[...]).astype(BF)
+    fixed[2].wait()
     table[own:] = mm(rows, w_recv[...]).astype(BF)
-    parts = ROWS // LANES
+    fixed[3].wait()
 
     def step(index, carry):
-        start = pl.multiple_of(index * ROWS, ROWS)
+        here = pl.ds(pl.multiple_of(index * ROWS, ROWS), ROWS)
         hit = jnp.concatenate(
             [
                 own_pick(
@@ -142,37 +168,33 @@
             ],
             axis=0,
         )
-        value = mm(edges[pl.ds(start, ROWS), :], w_edge[...]) + mm(hit, table[...]) + bias[...]
-        out[pl.ds(start, ROWS), :] = value
+        near = mm(hit, table[...]) + bias[...]
+        block_in(index).wait()
+        value[here, :] = near + mm(edges[here, :], w_edge[...])
+        block_out(index).start()
         return carry
 
-    lax.fori_loop(0, edges.shape[0] // ROWS, step, 0)
-
-
-def main_kernel(
-    shift,
-    steps,
-    count,
-    *refs,
-):
-    (pre_in, edges, edge_cot, nodes, node_cot, send, recv, far_lists, coarse) = refs[:9]
-    near = refs[9 : 9 + steps]
-    (
-        w_send,
-        w_edge_out,
-        edge_out_bias,
-        edge_gain,
-        w_node,
-        w_agg,
-        node_bias,
-        w_node_out,
-        node_out_bias,
-        node_gain,
-    ) = refs[9 + steps : 19 + steps]
-    (new_nodes, new_edges, d_pre, d_node) = refs[19 + steps : 23 + steps]
-    near_out = refs[23 + steps : 23 + 2 * steps]
-    far_out = refs[23 + 2 * steps]
-    (rows2, table2, slope, unit, inverse, agg, d_agg, sums2) = refs[24 + 2 * steps :]
+    lax.fori_loop(0, blocks, step, 0)
+    for index in range(blocks):
+        block_out(index).wait()
+
+
+def main_kernel(shift, steps, *refs):
+    take = iter(refs)
+    count, send, recv, far_lists = [next(take) for _ in range(4)]
+    edge_out_bias, edge_gain, node_bias, node_out_bias, node_gain = [next(take) for _ in range(5)]
+    near = [next(take) for _ in range(steps)]
+    coarse = next(take)
+    sources = [next(take) for _ in range(FIXED + 3)]
+    new_nodes, new_edges_out, d_pre_out, d_node = [next(take) for _ in range(4)]
+    near_out = [next(take) for _ in range(steps)]
+    far_out = next(take)
+    targets = [next(take) for _ in range(FIXED + 3)]
+    new_edges, d_pre = [next(take) for _ in range(2)]
+    rows2, table2, slope, unit, inverse, agg, d_agg, sums2 = [next(take) for _ in range(8)]
+    load, store = next(take), next(take)
+    w_send, w_edge_out, nodes, w_agg, w_node, w_node_out, node_cot = targets[:FIXED]
+    pre_in, edges, edge_cot = targets[FIXED:]
     own = nodes.shape[0]
     width = nodes.shape[1]
     peers, far_width = far_lists.shape
@@ -183,6 +205,37 @@
     parts = ROWS // LANES
     blocks = edges.shape[0] // ROWS
     live_count = count[0]
+    fixed = [
+        pltpu.make_async_copy(sources[index], targets[index], load.at[index])
+        for index in range(FIXED)
+    ]
+
+    def block_in(which, index):
+        here = pl.ds(pl.multiple_of(index * ROWS, ROWS), ROWS)
+        return pltpu.make_async_copy(
+            sources[FIXED + which].at[here, :],
+            targets[FIXED + which].at[here, :],
+            load.at[FIXED + which * blocks + index],
+        )
+
+    def block_out(which, index):
+        here = pl.ds(pl.multiple_of(index * ROWS, ROWS), ROWS)
+        source, target = ((new_edges, new_edges_out), (d_pre, d_pre_out))[which]
+        return pltpu.make_async_copy(
+            source.at[here, :], target.at[here, :], store.at[which * blocks + index]
+        )
+
+    fixed[0].start()
+    block_in(0, 0).start()
+    block_in(1, 0).start()
+    fixed[1].start()
+    for index in range(1, blocks):
+        block_in(0, index).start()
+        block_in(1, index).start()
+    for copy in fixed[2:]:
+        copy.start()
+    for index in range(blocks):
+        block_in(2, index).start()
 
     far_ids = lax.broadcasted_iota(jnp.int32, (peers, coarse.shape[0]), 1)
     far_base = lax.broadcasted_iota(jnp.int32, (peers, coarse.shape[0]), 0) * coarse_rows
@@ -196,7 +249,9 @@
     for slot in range(far_width):
         start = near_rows + slot * peers
         rows2[start : start + peers] = mm(far_hits[slot], coarse[...]).astype(BF)
+    fixed[0].wait()
     table2[...] = mm(rows2[...], w_send[...]).astype(BF)
+    fixed[1].wait()
     agg[...] = jnp.zeros(agg.shape, F32)
 
     def block_rows(ref, index, part):
@@ -212,6 +267,8 @@
             axis=0,
         )
         remote = mm(hit, table2[...])
+        block_in(0, index).wait()
+        block_in(1, index).wait()
         hidden = []
         for low in range(0, ROWS, CHUNK):
             here = pl.ds(start + low, CHUNK)
@@ -230,6 +287,7 @@
             message = part_unit * (edge_gain[...] * live)
             new_edges[here, :] = (edges[here, :].astype(F32) + message).astype(BF)
             sent.append(message.astype(BF))
+        block_out(0, index).start()
         hit_t = jnp.concatenate(
             [pick_t(block_rows(recv, index, part), own) for part in range(parts)], axis=1
         )
@@ -238,6 +296,8 @@
 
     lax.fori_loop(0, blocks, ahead, 0)
 
+    for copy in fixed[2:]:
+        copy.wait()
     rows = nodes[...]
     pre_node = mm(rows, w_node[...]) + mm(agg[...].astype(BF), w_agg[...]) + node_bias[...]
     node_hidden, node_slope = silu_parts(pre_node)
@@ -259,6 +319,7 @@
             [pick(block_rows(recv, index, part), d_agg.shape[0]) for part in range(parts)], axis=0
         )
         d_sent = mm(hit, d_agg[...])
+        block_in(2, index).wait()
         outs = []
         for low in range(0, ROWS, CHUNK):
             here = pl.ds(start + low, CHUNK)
@@ -273,6 +334,7 @@
             part = (d_hid[low : low + CHUNK] * slope[here, :]).astype(BF)
             d_pre[here, :] = part
             pres.append(part)
+        block_out(1, index).start()
         hit_t = jnp.concatenate(
             [
                 pick_t(
@@ -297,19 +359,46 @@
         term = mm_l(far_hits[slot], d_rows2[start : start + peers].astype(BF))
         d_coarse = term if d_coarse is None else d_coarse + term
     far_out[...] = d_coarse.astype(BF)
-
-
-def local_back_kernel(d_pre, edge_cot, d_node, w_edge, w_send, w_recv, send, recv, edge_grad, node_sum, sums):
+    for index in range(blocks):
+        block_out(0, index).wait()
+        block_out(1, index).wait()
+
+
+def local_back_kernel(send, recv, d_pre_in, cot_in, w_edge_in, w_send_in, w_recv_in, d_node_in, *refs):
+    edge_grad_out, node_sum = refs[:2]
+    d_pre, cot, w_edge, w_send, w_recv, d_node, edge_grad, sums, load, store = refs[2:]
     own = d_node.shape[0]
     parts = ROWS // LANES
+    blocks = d_pre.shape[0] // ROWS
+    fixed = [
+        pltpu.make_async_copy(source, target, load.at[index])
+        for index, (source, target) in enumerate(
+            [(w_edge_in, w_edge), (w_send_in, w_send), (w_recv_in, w_recv), (d_node_in, d_node)]
+        )
+    ]
+
+    def block_in(which, index):
+        here = pl.ds(pl.multiple_of(index * ROWS, ROWS), ROWS)
+        source, target = ((d_pre_in, d_pre), (cot_in, cot))[which]
+        return pltpu.make_async_copy(
+            source.at[here, :], target.at[here, :], load.at[4 + which * blocks + index]
+        )
+
+    def block_out(index):
+        here = pl.ds(pl.multiple_of(index * ROWS, ROWS), ROWS)
+        return pltpu.make_async_copy(edge_grad.at[here, :], edge_grad_out.at[here, :], store.at[index])
+
+    fixed[0].start()
+    for index in range(blocks):
+        block_in(0, index).start()
+        block_in(1, index).start()
+    for copy in fixed[1:]:
+        copy.start()
     sums[...] = jnp.zeros(sums.shape, F32)
+    fixed[0].wait()
 
     def step(index, carry):
-        start = pl.multiple_of(index * ROWS, ROWS)
-        here = pl.ds(start, ROWS)
-        grads = d_pre[here, :]
-        value = edge_cot[here, :].astype(F32) + mm_t(grads, w_edge[...])
-        edge_grad[here, :] = value.astype(BF)
+        here = pl.ds(pl.multiple_of(index * ROWS, ROWS), ROWS)
         hit = jnp.concatenate(
             [
                 own_pick_t(
@@ -321,12 +410,22 @@
             ],
             axis=1,
         )
+        block_in(0, index).wait()
+        block_in(1, index).wait()
+        grads = d_pre[here, :]
+        value = cot[here, :].astype(F32) + mm_t(grads, w_edge[...])
+        edge_grad[here, :] = value.astype(BF)
+        block_out(index).start()
         sums[...] += mm(hit, grads)
         return carry
 
-    lax.fori_loop(0, d_pre.shape[0] // ROWS, step, 0)
+    lax.fori_loop(0, blocks, step, 0)
+    for copy in fixed[1:]:
+        copy.wait()
     total = sums[...].astype(BF)
     node_sum[...] = d_node[...] + mm_t(total[:own], w_send[...]) + mm_t(total[own:], w_recv[...])
+    for index in range(blocks):
+        block_out(index).wait()
 
 
 def combine_kernel(coarse, node_sum, lists, far, *refs):
@@ -353,6 +452,10 @@
 
 def vmem(count):
     return [pl.BlockSpec(memory_space=pltpu.VMEM) for _ in range(count)]
+
+
+def hbm(count):
+    return [pl.BlockSpec(memory_space=pltpu.HBM) for _ in range(count)]
 
 
 def smem():
@@ -400,6 +503,7 @@
     own_pad = -(-own // LANES) * LANES
     send = send_slots.reshape(-1, LANES)
     recv = recv_slots.reshape(-1, LANES)
+    blocks = edge_rows // ROWS
     row = lambda value: value.reshape(1, -1)
     shape = jax.ShapeDtypeStruct
 
@@ -419,14 +523,24 @@
     pre_local = pl.pallas_call(
         local_kernel,
         out_shape=shape((edge_rows, hidden), F32),
-        in_specs=vmem(8),
-        out_specs=vmem(1)[0],
-        scratch_shapes=[pltpu.VMEM((2 * own, hidden), BF)],
+        in_specs=vmem(3) + hbm(5),
+        out_specs=hbm(1)[0],
+        scratch_shapes=[
+            pltpu.VMEM((own, width), BF),
+            pltpu.VMEM((edge_rows, width), BF),
+            pltpu.VMEM((width, hidden), BF),
+            pltpu.VMEM((width, hidden), BF),
+            pltpu.VMEM((width, hidden), BF),
+            pltpu.VMEM((2 * own, hidden), BF),
+            pltpu.VMEM((edge_rows, hidden), F32),
+            pltpu.SemaphoreType.DMA((4 + blocks,)),
+            pltpu.SemaphoreType.DMA((blocks,)),
+        ],
         cost_estimate=pl.CostEstimate(
             flops=2 * edge_rows * width * hidden * 3, transcendentals=0, bytes_accessed=6 << 20
         ),
         name="local_ahead",
-    )(nodes, edges, w_edge, w_send, w_recv, row(edge_bias), send, recv)
+    )(row(edge_bias), send, recv, nodes, edges, w_send, w_recv, w_edge)
 
     outs = pl.pallas_call(
         lambda *refs: main_kernel(shift, steps, *refs),
@@ -438,9 +552,21 @@
         ]
         + [shape((near_width, width), BF)] * steps
         + [shape((peers * coarse_count, width), BF)],
-        in_specs=[smem()] + vmem(19 + steps),
-        out_specs=vmem(5 + steps),
+        in_specs=[smem()] + vmem(9 + steps) + hbm(FIXED + 3),
+        out_specs=vmem(1) + hbm(2) + vmem(2 + steps),
         scratch_shapes=[
+            pltpu.VMEM((width, hidden), BF),
+            pltpu.VMEM((hidden, width), BF),
+            pltpu.VMEM((own, width), BF),
+            pltpu.VMEM((width, hidden), BF),
+            pltpu.VMEM((width, hidden), BF),
+            pltpu.VMEM((hidden, width), BF),
+            pltpu.VMEM((own, width), BF),
+            pltpu.VMEM((edge_rows, hidden), F32),
+            pltpu.VMEM((edge_rows, width), BF),
+            pltpu.VMEM((edge_rows, width), BF),
+            pltpu.VMEM((edge_rows, width), BF),
+            pltpu.VMEM((edge_rows, hidden), BF),
             pltpu.VMEM((height, width), BF),
             pltpu.VMEM((height, hidden), BF),
             pltpu.VMEM((edge_rows, hidden), F32),
@@ -449,6 +575,8 @@
             pltpu.VMEM((own, width), F32),
             pltpu.VMEM((own_pad, width), BF),
             pltpu.VMEM((height, hidden), F32),
+            pltpu.SemaphoreType.DMA((FIXED + 3 * blocks,)),
+            pltpu.SemaphoreType.DMA((2 * blocks,)),
         ],
         cost_estimate=pl.CostEstimate(
             flops=2 * edge_rows * width * hidden * 8, transcendentals=0, bytes_accessed=16 << 20
@@ -456,26 +584,26 @@
         name="main",
     )(
         block_count,
+        send,
+        recv,
+        far_lists[0],
+        row(edge_out_bias),
+        row(edge_gain),
+        row(node_bias),
+        row(node_out_bias),
+        row(node_gain),
+        *near,
+        coarse,
+        w_send,
+        w_edge_out,
+        nodes,
+        w_agg,
+        w_node,
+        w_node_out,
+        node_cot,
         pre_local,
         edges,
         edge_cot,
-        nodes,
-        node_cot,
-        send,
-        recv,
-        far_lists[0],
-        coarse,
-        *near,
-        w_send,
-        w_edge_out,
-        row(edge_out_bias),
-        row(edge_gain),
-        w_node,
-        w_agg,
-        row(node_bias),
-        w_node_out,
-        row(node_out_bias),
-        row(node_gain),
     )
     new_nodes, new_edges, d_pre, d_node = outs[:4]
     returned = [
@@ -492,14 +620,25 @@
     edge_grad, node_sum = pl.pallas_call(
         local_back_kernel,
         out_shape=[shape((edge_rows, width), BF), shape((own, width), F32)],
-        in_specs=vmem(8),
-        out_specs=vmem(2),
-        scratch_shapes=[pltpu.VMEM((2 * own, hidden), F32)],
+        in_specs=vmem(2) + hbm(6),
+        out_specs=hbm(1) + vmem(1),
+        scratch_shapes=[
+            pltpu.VMEM((edge_rows, hidden), BF),
+            pltpu.VMEM((edge_rows, width), BF),
+            pltpu.VMEM((width, hidden), BF),
+            pltpu.VMEM((width, hidden), BF),
+            pltpu.VMEM((width, hidden), BF),
+            pltpu.VMEM((own, width), F32),
+            pltpu.VMEM((edge_rows, width), BF),
+            pltpu.VMEM((2 * own, hidden), F32),
+            pltpu.SemaphoreType.DMA((4 + 2 * blocks,)),
+            pltpu.SemaphoreType.DMA((blocks,)),
+        ],
         cost_estimate=pl.CostEstimate(
             flops=2 * edge_rows * width * hidden * 3, transcendentals=0, bytes_accessed=6 << 20
         ),
         name="local_back",
-    )(d_pre, edge_cot, d_node, w_edge, w_send, w_recv, send, recv)
+    )(send, recv, d_pre, edge_cot, w_edge, w_send, w_recv, d_node)
 
     node_grad = pl.pallas_call(
         combine_kernel,

time: 71.8 us -> 71.2 us (level)
  Pallas kernels: 39.4 us -> 38.6 us
where the time goes in v2:
time: 71.2 us; the launch traced here: 70.7 us
  Pallas kernels  38.6 us (54%)
  starting transfers between devices  28.6 us (40%)
  local copies, waits for them, and re-layouts  2.03 us (3%)
  between operations  1.46 us (2%)
    pallas_call x1, Pallas kernels, local(): pl.pallas_call(lambda *refs: main_kernel(shift, steps, *refs), out_shape=...  19.7 us
    ppermute x8, starting transfers between devices, passed_along(): return lax.ppermute(value, axis, pairs)  14.4 us
    all_to_all x1, starting transfers between devices, local(): lax.all_to_all(packed[steps], 'patch', split_axis=0, concat_axis=0, tiled...  7.34 us
    pallas_call x1, Pallas kernels, local(): pl.pallas_call(local_kernel, out_shape=shape((edge_rows, hidden), F32), i...  7.21 us
    pallas_call x1, Pallas kernels, local(): pl.pallas_call(local_back_kernel, out_shape=[shape((edge_rows, width), BF...  6.96 us
    all_to_all x1, starting transfers between devices, local(): lax.all_to_all(outs[4 + steps].reshape(peers, coarse_count, width), 'patc...  6.83 us
    pallas_call x1, Pallas kernels, local(): pl.pallas_call(combine_kernel, out_shape=shape((own, width), BF), in_spec...  2.54 us
    pallas_call x1, Pallas kernels, local(): pl.pallas_call(pack_kernel, out_shape=[shape((near_width, width), BF)] *...  2.25 us
  transfers between devices with their start and end apart: 10, of which 0 were waited for; matrix products, arithmetic and copies ran while one was open for 1% of the time, Pallas kernels for 20%

profile of v2, /device:TPU:1, one launch (start us, length us, event | category | flops | bytes accessed | tf_op | source)
XLA Modules:
  0.0 70.7 jit_solution(17489426000543670351)
XLA Ops:
  0.6 2.2 %pack.1 = (bf16[64,512]{1,0:T(8,128)(2,1)}, bf16[64,512]{1,0:T(8,128)(2,1)}, bf16[64,512]{1,0:T(8,128)(2,1)}, bf16[64,512]{1,0:T(8,128)(2,1)}, bf16[16,8,512]{2,1,0:T(8,128)(2,1)}) custom-call(bf16[320,512]{1,0:T(8,128)(2,1)} %refs_16_.1, s32[4,64]{1,0:T(4,128)} %lists.3, s32[1,8]{1,0:T(1,128)} %bitcast.14), custom_call_target="tpu_custom_call" | custom-call | tf_op jit(solution)/shard_map/pack/pallas_call | solution.py:510
  2.9 7.3 %all-to-all-start = ((bf16[16,8,512]{2,1,0:T(8,128)(2,1)}), bf16[16,8,512]{2,1,0:T(8,128)(2,1)S(1)}, u32[]{:S(2)}, u32[]{:S(2)}) async-start(bf16[16,8,512]{2,1,0:T(8,128)(2,1)} %get-tuple-element.24), calls=%async_computation | async-start | bytes 262144 | tf_op jit(solution)/shard_map/all_to_all | solution.py:519
  10.2 1.6 %collective-permute-start = (bf16[64,512]{1,0:T(8,128)(2,1)}, bf16[64,512]{1,0:T(8,128)(2,1)S(1)}, u32[]{:S(2)}, u32[]{:S(2)}) collective-permute-start(bf16[64,512]{1,0:T(8,128)(2,1)} %get-tuple-element.20), channel_id=1, source_target_pairs={{0,1},{1,2},{2,3},{3,4},{4,5},{5,6},{6,7},{7,8},{8,9},{9,10},{10,1... | collective-permute-start | bytes 196616 | tf_op jit(solution)/shard_map/ppermute | solution.py:21
  11.8 0.0 collective-permute-start.1
  11.8 1.2 %collective-permute-start.2 = (bf16[64,512]{1,0:T(8,128)(2,1)}, bf16[64,512]{1,0:T(8,128)(2,1)S(1)}, u32[]{:S(2)}, u32[]{:S(2)}) collective-permute-start(bf16[64,512]{1,0:T(8,128)(2,1)} %get-tuple-element.22), channel_id=1, source_target_pairs={{0,2},{1,3},{2,4},{3,5},{4,6},{5,7},{6,8},{7,9},{8,10},{9,11},{10,... | collective-permute-start | bytes 196616 | tf_op jit(solution)/shard_map/ppermute | solution.py:21
  13.0 3.0 %collective-permute-start.3 = (bf16[64,512]{1,0:T(8,128)(2,1)}, bf16[64,512]{1,0:T(8,128)(2,1)S(1)}, u32[]{:S(2)}, u32[]{:S(2)}) collective-permute-start(bf16[64,512]{1,0:T(8,128)(2,1)} %get-tuple-element.23), channel_id=1, source_target_pairs={{0,14},{1,15},{2,0},{3,1},{4,2},{5,3},{6,4},{7,5},{8,6},{9,7},{10,... | collective-permute-start | bytes 196616 | tf_op jit(solution)/shard_map/ppermute | solution.py:21
  16.0 0.0 copy-start.6
  16.0 7.2 %local_ahead.1.refs_21_ = f32[1536,512]{1,0:T(8,128)} custom-call(f32[1,512]{1,0:T(1,128)} %bitcast.22, s32[12,128]{1,0:T(8,128)} %bitcast.16, s32[12,128]{1,0:T(8,128)} %bitcast.19, bf16[320,512]{1,0:T(8,128)(2,1)} %refs_16_.1, bf16[1536,512]{1,0:T(8,128)(2,1)} %refs_22_.1, bf16[512,512]{1,0:T(8,128)(2,1)} %w_send_in.3, bf16[512,512]{1,0:T(8,128)(2,1)} %w_recv_in.3, ...), custom_call_target="tpu_custom_call" | custom-call | flops 2415919104 | bytes 6291456 | tf_op jit(solution)/shard_map/local_ahead/pallas_call | solution.py:523
  23.9 0.0 copy-done.6
  23.9 0.7 copy.27.refs_3_
  24.6 0.0 collective-permute-done.refs_9_
  24.6 0.0 copy-start.7
  24.6 0.0 collective-permute-done.1.refs_10_
  24.6 0.0 copy-start.8
  24.6 0.0 collective-permute-done.2.refs_11_
  24.6 0.0 copy-start.9
  24.6 0.0 collective-permute-done.3.refs_12_
  24.6 0.0 copy-start.10
  24.6 0.0 all-to-all-done
  24.6 0.0 copy-start.1
  24.7 0.5 copy-done.7
  25.2 0.0 copy-done.8
  25.2 0.0 copy-done.9
  25.2 0.0 copy-done.10
  25.3 0.1 copy-done.1
  25.3 19.7 %main.1 = (bf16[320,512]{1,0:T(8,128)(2,1)}, bf16[1536,512]{1,0:T(8,128)(2,1)}, bf16[1536,512]{1,0:T(8,128)(2,1)}, f32[320,512]{1,0:T(8,128)}, bf16[64,512]{1,0:...) custom-call(s32[1]{0:T(128)S(6)} %copy.28.refs_0_, ...), custom_call_target="tpu_custom_call" | custom-call | flops 6442450944 | bytes 16777216 | tf_op jit(solution)/shard_map/main/pallas_call | solution.py:545
  45.0 6.8 %all-to-all-start.1 = ((bf16[16,8,512]{2,1,0:T(8,128)(2,1)}), bf16[16,8,512]{2,1,0:T(8,128)(2,1)S(1)}, u32[]{:S(2)}, u32[]{:S(2)}) async-start(bf16[16,8,512]{2,1,0:T(8,128)(2,1)} %bitcast.13), calls=%async_computation.1 | async-start | bytes 262144 | tf_op jit(solution)/shard_map/all_to_all | solution.py:612
  51.8 0.3 collective-permute-start.4
  52.1 1.5 %collective-permute-start.5 = (bf16[64,512]{1,0:T(8,128)(2,1)}, bf16[64,512]{1,0:T(8,128)(2,1)S(1)}, u32[]{:S(2)}, u32[]{:S(2)}) collective-permute-start(bf16[64,512]{1,0:T(8,128)(2,1)} %get-tuple-element.32), channel_id=1, source_target_pairs={{0,1},{1,2},{2,3},{3,4},{4,5},{5,6},{6,7},{7,8},{8,9},{9,10},{10,1... | collective-permute-start | bytes 196616 | tf_op jit(solution)/shard_map/ppermute | solution.py:21
  53.6 6.8 %collective-permute-start.6 = (bf16[64,512]{1,0:T(8,128)(2,1)}, bf16[64,512]{1,0:T(8,128)(2,1)S(1)}, u32[]{:S(2)}, u32[]{:S(2)}) collective-permute-start(bf16[64,512]{1,0:T(8,128)(2,1)} %get-tuple-element.33), channel_id=1, source_target_pairs={{0,14},{1,15},{2,0},{3,1},{4,2},{5,3},{6,4},{7,5},{8,6},{9,7},{10,... | collective-permute-start | bytes 196616 | tf_op jit(solution)/shard_map/ppermute | solution.py:21
  60.4 0.0 collective-permute-start.7
  60.4 7.0 %local_back.1 = (bf16[1536,512]{1,0:T(8,128)(2,1)}, f32[320,512]{1,0:T(8,128)}) custom-call(s32[12,128]{1,0:T(8,128)} %bitcast.18, s32[12,128]{1,0:T(8,128)} %bitcast.21, bf16[1536,512]{1,0:T(8,128)(2,1)} %get-tuple-element.27.d_pre_in, bf16[1536,512]{1,0:T(8,128)(2,1)} %cot_in.1, bf16[512,512]{1,0:T(8,128)(2,1)} %w_edge_in.3, bf16[512,512]{1,0:T(8,128)(2,1)} %w_send_in.3, ...), custom_call_target="tpu_custom_call" | custom-call | flops 2415919104 | bytes 6291456 | tf_op jit(solution)/shard_map/local_back/pallas_call | solution.py:620
  67.4 0.0 collective-permute-done.4.refs_0_
  67.4 0.0 copy-start.2
  67.4 0.0 collective-permute-done.5.refs_1_
  67.4 0.0 copy-start.3
  67.4 0.0 collective-permute-done.6.refs_2_
  67.4 0.0 copy-start.4
  67.4 0.0 collective-permute-done.7.refs_3_
  67.4 0.0 copy-start.5
  67.5 0.0 all-to-all-done.1.far
  67.5 0.0 copy-start
  67.5 0.5 copy-done.2
  68.0 0.0 copy-done.3
  68.0 0.0 copy-done.4
  68.1 0.0 copy-done.5
  68.1 0.1 copy-done
  68.1 2.5 %combine.1 = bf16[320,512]{1,0:T(8,128)(2,1)} custom-call(s32[8]{0:T(128)} %coarse.1, f32[320,512]{1,0:T(8,128)} %get-tuple-element.29.node_sum, s32[4,64]{1,0:T(4,128)} %lists.3, bf16[16,8,512]{2,1,0:T(8,128)(2,1)} %copy-done, bf16[64,512]{1,0:T(8,128)(2,1)} %copy-done.2, bf16[64,512]{1,0:T(8,128)(2,1)} %copy-done.3, bf16[64,512]{1,0:T(8,128)(2,1)} %copy-done.4, ...), custom_call_target="tpu_custom_call" | custom-call | tf_op jit(solution)/shard_map/combine/pallas_call | solution.py:643
Async XLA Ops:
  2.9 21.8 %all-to-all-start = ((bf16[16,8,512]{2,1,0:T(8,128)(2,1)}), bf16[16,8,512]{2,1,0:T(8,128)(2,1)S(1)}, u32[]{:S(2)}, u32[]{:S(2)}) async-start(bf16[16,8,512]{2,1,0:T(8,128)(2,1)} %get-tuple-element.24), calls=%async_computation | async-start | bytes 262144 | tf_op jit(solution)/shard_map/all_to_all | solution.py:519
  10.2 14.4 %collective-permute-start = (bf16[64,512]{1,0:T(8,128)(2,1)}, bf16[64,512]{1,0:T(8,128)(2,1)S(1)}, u32[]{:S(2)}, u32[]{:S(2)}) collective-permute-start(bf16[64,512]{1,0:T(8,128)(2,1)} %get-tuple-element.20), channel_id=1, source_target_pairs={{0,1},{1,2},{2,3},{3,4},{4,5},{5,6},{6,7},{7,8},{8,9},{9,10},{10,1... | collective-permute-start | bytes 196616 | tf_op jit(solution)/shard_map/ppermute | solution.py:21
  11.8 12.7 %collective-permute-start.1 = (bf16[64,512]{1,0:T(8,128)(2,1)}, bf16[64,512]{1,0:T(8,128)(2,1)S(1)}, u32[]{:S(2)}, u32[]{:S(2)}) collective-permute-start(bf16[64,512]{1,0:T(8,128)(2,1)} %get-tuple-element.21), channel_id=1, source_target_pairs={{0,15},{1,0},{2,1},{3,2},{4,3},{5,4},{6,5},{7,6},{8,7},{9,8},{10,9... | collective-permute-start | bytes 196616 | tf_op jit(solution)/shard_map/ppermute | solution.py:21
  11.8 12.7 %collective-permute-start.2 = (bf16[64,512]{1,0:T(8,128)(2,1)}, bf16[64,512]{1,0:T(8,128)(2,1)S(1)}, u32[]{:S(2)}, u32[]{:S(2)}) collective-permute-start(bf16[64,512]{1,0:T(8,128)(2,1)} %get-tuple-element.22), channel_id=1, source_target_pairs={{0,2},{1,3},{2,4},{3,5},{4,6},{5,7},{6,8},{7,9},{8,10},{9,11},{10,... | collective-permute-start | bytes 196616 | tf_op jit(solution)/shard_map/ppermute | solution.py:21
  13.0 11.6 %collective-permute-start.3 = (bf16[64,512]{1,0:T(8,128)(2,1)}, bf16[64,512]{1,0:T(8,128)(2,1)S(1)}, u32[]{:S(2)}, u32[]{:S(2)}) collective-permute-start(bf16[64,512]{1,0:T(8,128)(2,1)} %get-tuple-element.23), channel_id=1, source_target_pairs={{0,14},{1,15},{2,0},{3,1},{4,2},{5,3},{6,4},{7,5},{8,6},{9,7},{10,... | collective-permute-start | bytes 196616 | tf_op jit(solution)/shard_map/ppermute | solution.py:21
  16.0 7.9 %copy-start.6 = (s32[1,16,2]{1,2,0:T(2,128)S(1)}, s32[1,16,2]{1,2,0:T(2,128)}, u32[]{:S(2)}) copy-start(s32[1,16,2]{1,2,0:T(2,128)} %param.44) | copy-start | bytes 388
  24.6 0.6 copy-start.7
  24.6 0.6 copy-start.8
  24.6 0.6 copy-start.9
  24.6 0.6 copy-start.10
  24.6 0.7 copy-start.1
  45.0 22.5 %all-to-all-start.1 = ((bf16[16,8,512]{2,1,0:T(8,128)(2,1)}), bf16[16,8,512]{2,1,0:T(8,128)(2,1)S(1)}, u32[]{:S(2)}, u32[]{:S(2)}) async-start(bf16[16,8,512]{2,1,0:T(8,128)(2,1)} %bitcast.13), calls=%async_computation.1 | async-start | bytes 262144 | tf_op jit(solution)/shard_map/all_to_all | solution.py:612
  51.8 15.6 %collective-permute-start.4 = (bf16[64,512]{1,0:T(8,128)(2,1)}, bf16[64,512]{1,0:T(8,128)(2,1)S(1)}, u32[]{:S(2)}, u32[]{:S(2)}) collective-permute-start(bf16[64,512]{1,0:T(8,128)(2,1)} %get-tuple-element.31), channel_id=1, source_target_pairs={{0,15},{1,0},{2,1},{3,2},{4,3},{5,4},{6,5},{7,6},{8,7},{9,8},{10,9... | collective-permute-start | bytes 196616 | tf_op jit(solution)/shard_map/ppermute | solution.py:21
  52.1 15.3 %collective-permute-start.5 = (bf16[64,512]{1,0:T(8,128)(2,1)}, bf16[64,512]{1,0:T(8,128)(2,1)S(1)}, u32[]{:S(2)}, u32[]{:S(2)}) collective-permute-start(bf16[64,512]{1,0:T(8,128)(2,1)} %get-tuple-element.32), channel_id=1, source_target_pairs={{0,1},{1,2},{2,3},{3,4},{4,5},{5,6},{6,7},{7,8},{8,9},{9,10},{10,1... | collective-permute-start | bytes 196616 | tf_op jit(solution)/shard_map/ppermute | solution.py:21
  53.6 13.9 %collective-permute-start.6 = (bf16[64,512]{1,0:T(8,128)(2,1)}, bf16[64,512]{1,0:T(8,128)(2,1)S(1)}, u32[]{:S(2)}, u32[]{:S(2)}) collective-permute-start(bf16[64,512]{1,0:T(8,128)(2,1)} %get-tuple-element.33), channel_id=1, source_target_pairs={{0,14},{1,15},{2,0},{3,1},{4,2},{5,3},{6,4},{7,5},{8,6},{9,7},{10,... | collective-permute-start | bytes 196616 | tf_op jit(solution)/shard_map/ppermute | solution.py:21
  60.4 7.0 %collective-permute-start.7 = (bf16[64,512]{1,0:T(8,128)(2,1)}, bf16[64,512]{1,0:T(8,128)(2,1)S(1)}, u32[]{:S(2)}, u32[]{:S(2)}) collective-permute-start(bf16[64,512]{1,0:T(8,128)(2,1)} %get-tuple-element.34), channel_id=1, source_target_pairs={{0,2},{1,3},{2,4},{3,5},{4,6},{5,7},{6,8},{7,9},{8,10},{9,11},{10,... | collective-permute-start | bytes 196616 | tf_op jit(solution)/shard_map/ppermute | solution.py:21
  67.4 0.6 copy-start.2
  67.4 0.6 copy-start.3
  67.4 0.6 copy-start.4
  67.4 0.6 copy-start.5
  67.5 0.7 copy-start

commit v3 on v1

--- a/solution.py
+++ b/solution.py
@@ -7,8 +7,11 @@
 
 BLOCK = 128
 LANES = 128
-ROWS = 256
-CHUNK = 32
+ROWS = 512
+MAIN_ROWS = 1536
+COPY = 256
+CHUNK = 16
+FIXED = 15
 EPS = 1e-05
 BF = jnp.bfloat16
 F32 = jnp.float32
@@ -102,6 +105,27 @@
     return inverse * (grad - first - unit * second)
 
 
+def copies_of(sources, targets, sems):
+    return [
+        pltpu.make_async_copy(source, target, sems.at[index])
+        for index, (source, target) in enumerate(zip(sources, targets))
+    ]
+
+
+def start_all(copies):
+    for copy in copies:
+        copy.start()
+
+
+def wait_all(copies):
+    for copy in copies:
+        copy.wait()
+
+
+def rows_of(index):
+    return pl.ds(pl.multiple_of(index * COPY, COPY), COPY)
+
+
 def pack_kernel(nodes, lists, coarse, *outs):
     rows = nodes[...]
     own = rows.shape[0]
@@ -122,15 +146,36 @@
     lax.fori_loop(0, out.shape[0], put, 0)
 
 
-def local_kernel(nodes, edges, w_edge, w_send, w_recv, bias, send, recv, out, table):
+def local_kernel(*refs):
+    sources, edges_in, out = refs[:7], refs[7], refs[8]
+    targets, edges, table, value, load, store = refs[9:16], *refs[16:]
+    nodes, w_send, w_recv, send, recv, w_edge, bias = targets
     own = nodes.shape[0]
+    parts = ROWS // LANES
+    copies = edges.shape[0] // COPY
+    ratio = ROWS // COPY
+    fixed = copies_of(sources, targets, load)
+
+    def block_in(index):
+        here = rows_of(index)
+        return pltpu.make_async_copy(edges_in.at[here, :], edges.at[here, :], load.at[7 + index])
+
+    def block_out(index):
+        here = rows_of(index)
+        return pltpu.make_async_copy(value.at[here, :], out.at[here, :], store.at[index])
+
+    start_all(fixed)
+    for index in range(copies):
+        block_in(index).start()
+    wait_all(fixed[:2])
     rows = nodes[...]
     table[:own] = mm(rows, w_send[...]).astype(BF)
+    fixed[2].wait()
     table[own:] = mm(rows, w_recv[...]).astype(BF)
-    parts = ROWS // LANES
+    wait_all(fixed[3:])
 
     def step(index, carry):
-        start = pl.multiple_of(index * ROWS, ROWS)
+        here = pl.ds(pl.multiple_of(index * ROWS, ROWS), ROWS)
         hit = jnp.concatenate(
             [
                 own_pick(
@@ -142,52 +187,85 @@
             ],
             axis=0,
         )
-        value = mm(edges[pl.ds(start, ROWS), :], w_edge[...]) + mm(hit, table[...]) + bias[...]
-        out[pl.ds(start, ROWS), :] = value
+        near = mm(hit, table[...]) + bias[...]
+        for part in range(ratio):
+            block_in(index * ratio + part).wait()
+        value[here, :] = (near + mm(edges[here, :], w_edge[...])).astype(BF)
+        for part in range(ratio):
+            block_out(index * ratio + part).start()
         return carry
 
     lax.fori_loop(0, edges.shape[0] // ROWS, step, 0)
-
-
-def main_kernel(
-    shift,
-    steps,
-    count,
-    *refs,
-):
-    (pre_in, edges, edge_cot, nodes, node_cot, send, recv, far_lists, coarse) = refs[:9]
-    near = refs[9 : 9 + steps]
-    (
-        w_send,
-        w_edge_out,
-        edge_out_bias,
-        edge_gain,
-        w_node,
-        w_agg,
-        node_bias,
-        w_node_out,
-        node_out_bias,
-        node_gain,
-    ) = refs[9 + steps : 19 + steps]
-    (new_nodes, new_edges, d_pre, d_node) = refs[19 + steps : 23 + steps]
-    near_out = refs[23 + steps : 23 + 2 * steps]
-    far_out = refs[23 + 2 * steps]
-    (rows2, table2, slope, unit, inverse, agg, d_agg, sums2) = refs[24 + 2 * steps :]
+    for index in range(copies):
+        block_out(index).wait()
+
+
+def main_kernel(shift, steps, *refs):
+    take = iter(refs)
+    count = next(take)
+    near = [next(take) for _ in range(steps)]
+    coarse = next(take)
+    sources = [next(take) for _ in range(FIXED)]
+    block_sources = [next(take) for _ in range(3)]
+    near_out = [next(take) for _ in range(steps)]
+    far_out = next(take)
+    new_nodes_out, d_node_out, new_edges_out, d_pre_out = [next(take) for _ in range(4)]
+    targets = [next(take) for _ in range(FIXED)]
+    pre_in, edges, edge_cot = block_targets = [next(take) for _ in range(3)]
+    new_nodes, d_node, new_edges, d_pre = [next(take) for _ in range(4)]
+    rows2, table2, slope, unit, inverse, agg, d_agg, sums2 = [next(take) for _ in range(8)]
+    load, store = next(take), next(take)
+    far_lists, w_send, send, recv, w_edge_out, edge_out_bias, edge_gain = targets[:7]
+    nodes, w_agg, w_node, node_bias, w_node_out, node_out_bias, node_cot, node_gain = targets[7:]
     own = nodes.shape[0]
     width = nodes.shape[1]
-    peers, far_width = far_lists.shape
+    far_width, peers = far_lists.shape
     near_width = near[0].shape[0]
     near_rows = steps * near_width
     height = table2.shape[0]
     coarse_rows = coarse.shape[0] // peers
-    parts = ROWS // LANES
-    blocks = edges.shape[0] // ROWS
+    parts = MAIN_ROWS // LANES
+    blocks = edges.shape[0] // MAIN_ROWS
+    copies = edges.shape[0] // COPY
+    ratio = MAIN_ROWS // COPY
     live_count = count[0]
-
-    far_ids = lax.broadcasted_iota(jnp.int32, (peers, coarse.shape[0]), 1)
-    far_base = lax.broadcasted_iota(jnp.int32, (peers, coarse.shape[0]), 0) * coarse_rows
+    fixed = copies_of(sources, targets, load)
+
+    def block_in(which, index):
+        here = rows_of(index)
+        return pltpu.make_async_copy(
+            block_sources[which].at[here, :],
+            block_targets[which].at[here, :],
+            load.at[FIXED + which * copies + index],
+        )
+
+    def block_out(which, index):
+        here = rows_of(index)
+        source, target = ((new_edges, new_edges_out), (d_pre, d_pre_out))[which]
+        return pltpu.make_async_copy(
+            source.at[here, :], target.at[here, :], store.at[which * copies + index]
+        )
+
+    node_outs = [
+        pltpu.make_async_copy(new_nodes, new_nodes_out, store.at[2 * copies]),
+        pltpu.make_async_copy(d_node, d_node_out, store.at[2 * copies + 1]),
+    ]
+    start_all(fixed[:4])
+    block_in(0, 0).start()
+    start_all(fixed[4:7])
+    block_in(1, 0).start()
+    for index in range(1, copies):
+        block_in(0, index).start()
+        block_in(1, index).start()
+    start_all(fixed[7:])
+    for index in range(copies):
+        block_in(2, index).start()
+
+    fixed[0].wait()
+    far_ids = lax.broadcasted_iota(jnp.int32, (coarse.shape[0], peers), 0)
+    far_base = lax.broadcasted_iota(jnp.int32, (coarse.shape[0], peers), 1) * coarse_rows
     far_hits = [
-        ones_where(far_ids == far_base + far_lists[:, slot : slot + 1])
+        ones_where(far_ids == far_base + far_lists[slot : slot + 1, :])
         for slot in range(far_width)
     ]
     rows2[...] = jnp.zeros(rows2.shape, BF)
@@ -195,15 +273,18 @@
         rows2[index * near_width : (index + 1) * near_width] = near[index][...]
     for slot in range(far_width):
         start = near_rows + slot * peers
-        rows2[start : start + peers] = mm(far_hits[slot], coarse[...]).astype(BF)
+        rows2[start : start + peers] = mm_l(far_hits[slot], coarse[...]).astype(BF)
+    fixed[1].wait()
     table2[...] = mm(rows2[...], w_send[...]).astype(BF)
+    wait_all(fixed[2:4])
     agg[...] = jnp.zeros(agg.shape, F32)
+    wait_all(fixed[4:7])
 
     def block_rows(ref, index, part):
         return ref[pl.ds(index * parts + part, 1), :]
 
     def ahead(index, carry):
-        start = pl.multiple_of(index * ROWS, ROWS)
+        start = pl.multiple_of(index * MAIN_ROWS, MAIN_ROWS)
         hit = jnp.concatenate(
             [
                 pick(remote_index(block_rows(send, index, part), own, near_rows, peers, shift), height)
@@ -213,23 +294,31 @@
         )
         remote = mm(hit, table2[...])
         hidden = []
-        for low in range(0, ROWS, CHUNK):
+        for low in range(0, MAIN_ROWS, CHUNK):
+            if low % COPY == 0:
+                block_in(0, index * ratio + low // COPY).wait()
             here = pl.ds(start + low, CHUNK)
-            value = pre_in[here, :] + remote[low : low + CHUNK]
+            value = pre_in[here, :].astype(F32) + remote[low : low + CHUNK]
             part_hidden, part_slope = silu_parts(value)
             slope[here, :] = part_slope
             hidden.append(part_hidden.astype(BF))
         out = mm(jnp.concatenate(hidden, axis=0), w_edge_out[...])
         sent = []
-        for low in range(0, ROWS, CHUNK):
+        for low in range(0, MAIN_ROWS, CHUNK):
+            if low % COPY == 0:
+                block_in(1, index * ratio + low // COPY).wait()
             here = pl.ds(start + low, CHUNK)
-            live = jnp.where(index * parts + low // BLOCK < live_count, 1.0, 0.0).astype(F32)
+            if low % BLOCK == 0:
+                live = jnp.where(index * parts + low // BLOCK < live_count, 1.0, 0.0)
+                live_gain = edge_gain[...] * live.astype(F32)
             part_unit, part_inverse = norm_parts(out[low : low + CHUNK] + edge_out_bias[...])
             unit[here, :] = part_unit
             inverse[here, :] = part_inverse
-            message = part_unit * (edge_gain[...] * live)
+            message = part_unit * live_gain
             new_edges[here, :] = (edges[here, :].astype(F32) + message).astype(BF)
             sent.append(message.astype(BF))
+            if (low + CHUNK) % COPY == 0:
+                block_out(0, index * ratio + low // COPY).start()
         hit_t = jnp.concatenate(
             [pick_t(block_rows(recv, index, part), own) for part in range(parts)], axis=1
         )
@@ -238,6 +327,7 @@
 
     lax.fori_loop(0, blocks, ahead, 0)
 
+    wait_all(fixed[7:])
     rows = nodes[...]
     pre_node = mm(rows, w_node[...]) + mm(agg[...].astype(BF), w_agg[...]) + node_bias[...]
     node_hidden, node_slope = silu_parts(pre_node)
@@ -252,27 +342,34 @@
     d_agg[:own] = mm_t(d_pre_node, w_agg[...]).astype(BF)
     d_node[...] = cot + mm_t(d_pre_node, w_node[...])
     sums2[...] = jnp.zeros(sums2.shape, F32)
+    start_all(node_outs)
 
     def back(index, carry):
-        start = pl.multiple_of(index * ROWS, ROWS)
+        start = pl.multiple_of(index * MAIN_ROWS, MAIN_ROWS)
         hit = jnp.concatenate(
             [pick(block_rows(recv, index, part), d_agg.shape[0]) for part in range(parts)], axis=0
         )
         d_sent = mm(hit, d_agg[...])
         outs = []
-        for low in range(0, ROWS, CHUNK):
+        for low in range(0, MAIN_ROWS, CHUNK):
+            if low % COPY == 0:
+                block_in(2, index * ratio + low // COPY).wait()
             here = pl.ds(start + low, CHUNK)
-            live = jnp.where(index * parts + low // BLOCK < live_count, 1.0, 0.0).astype(F32)
+            if low % BLOCK == 0:
+                live = jnp.where(index * parts + low // BLOCK < live_count, 1.0, 0.0)
+                live_gain = edge_gain[...] * live.astype(F32)
             d_message = edge_cot[here, :].astype(F32) + d_sent[low : low + CHUNK]
-            d_unit = d_message * (edge_gain[...] * live)
+            d_unit = d_message * live_gain
             outs.append(norm_back(d_unit, unit[here, :], inverse[here, :]).astype(BF))
         d_hid = mm_t(jnp.concatenate(outs, axis=0), w_edge_out[...])
         pres = []
-        for low in range(0, ROWS, CHUNK):
+        for low in range(0, MAIN_ROWS, CHUNK):
             here = pl.ds(start + low, CHUNK)
             part = (d_hid[low : low + CHUNK] * slope[here, :]).astype(BF)
             d_pre[here, :] = part
             pres.append(part)
+            if (low + CHUNK) % COPY == 0:
+                block_out(1, index * ratio + low // COPY).start()
         hit_t = jnp.concatenate(
             [
                 pick_t(
@@ -294,22 +391,50 @@
     d_coarse = None
     for slot in range(far_width):
         start = near_rows + slot * peers
-        term = mm_l(far_hits[slot], d_rows2[start : start + peers].astype(BF))
+        term = mm(far_hits[slot], d_rows2[start : start + peers].astype(BF))
         d_coarse = term if d_coarse is None else d_coarse + term
     far_out[...] = d_coarse.astype(BF)
-
-
-def local_back_kernel(d_pre, edge_cot, d_node, w_edge, w_send, w_recv, send, recv, edge_grad, node_sum, sums):
+    for index in range(copies):
+        block_out(0, index).wait()
+        block_out(1, index).wait()
+    wait_all(node_outs)
+
+
+def local_back_kernel(*refs):
+    sources, block_sources = refs[:7], refs[7:9]
+    edge_grad_out, node_sum, near_hit = refs[9:12]
+    targets, block_targets = refs[12:19], refs[19:21]
+    edge_grad, sums, load, store = refs[21:]
+    send, recv, w_edge, w_send, w_recv, d_node, lists = targets
+    d_pre, cot = block_targets
     own = d_node.shape[0]
     parts = ROWS // LANES
+    copies = d_pre.shape[0] // COPY
+    ratio = ROWS // COPY
+    fixed = copies_of(sources, targets, load)
+
+    def block_in(which, index):
+        here = rows_of(index)
+        return pltpu.make_async_copy(
+            block_sources[which].at[here, :],
+            block_targets[which].at[here, :],
+            load.at[7 + which * copies + index],
+        )
+
+    def block_out(index):
+        here = rows_of(index)
+        return pltpu.make_async_copy(edge_grad.at[here, :], edge_grad_out.at[here, :], store.at[index])
+
+    start_all(fixed[:3])
+    for index in range(copies):
+        block_in(0, index).start()
+        block_in(1, index).start()
+    start_all(fixed[3:])
     sums[...] = jnp.zeros(sums.shape, F32)
+    wait_all(fixed[:3])
 
     def step(index, carry):
-        start = pl.multiple_of(index * ROWS, ROWS)
-        here = pl.ds(start, ROWS)
-        grads = d_pre[here, :]
-        value = edge_cot[here, :].astype(F32) + mm_t(grads, w_edge[...])
-        edge_grad[here, :] = value.astype(BF)
+        here = pl.ds(pl.multiple_of(index * ROWS, ROWS), ROWS)
         hit = jnp.concatenate(
             [
                 own_pick_t(
@@ -321,30 +446,39 @@
             ],
             axis=1,
         )
+        for part in range(ratio):
+            block_in(0, index * ratio + part).wait()
+            block_in(1, index * ratio + part).wait()
+        grads = d_pre[here, :]
+        value = cot[here, :].astype(F32) + mm_t(grads, w_edge[...])
+        edge_grad[here, :] = value.astype(BF)
+        for part in range(ratio):
+            block_out(index * ratio + part).start()
         sums[...] += mm(hit, grads)
         return carry
 
     lax.fori_loop(0, d_pre.shape[0] // ROWS, step, 0)
+    wait_all(fixed[3:])
     total = sums[...].astype(BF)
     node_sum[...] = d_node[...] + mm_t(total[:own], w_send[...]) + mm_t(total[own:], w_recv[...])
-
-
-def combine_kernel(coarse, node_sum, lists, far, *refs):
     steps, width = lists.shape
-    near = refs[:steps]
+    ids = lax.broadcasted_iota(jnp.int32, (own, width), 0)
+    near_hit[...] = jnp.concatenate(
+        [ones_where(ids == lists[index : index + 1, :]) for index in range(steps)], axis=1
+    )
+    for index in range(copies):
+        block_out(index).wait()
+
+
+def combine_kernel(coarse, node_sum, hit, far, *refs):
+    steps = len(refs) - 2
+    near = jnp.concatenate([ref[...] for ref in refs[:steps]], axis=0)
     out, total = refs[steps], refs[steps + 1]
-    own = node_sum.shape[0]
-    ids = lax.broadcasted_iota(jnp.int32, (own, width), 0)
-    value = node_sum[...]
-    for index in range(steps):
-        value = value + mm(ones_where(ids == lists[index : index + 1, :]), near[index][...])
-    total[...] = value
+    total[...] = node_sum[...] + mm(hit[...], near)
     peers, count, _ = far.shape
-
-    def add(index, carry):
-        return carry + far[index].astype(F32)
-
-    grads = lax.fori_loop(0, peers, add, jnp.zeros(far.shape[1:], F32))
+    grads = far[0].astype(F32)
+    for index in range(1, peers):
+        grads = grads + far[index].astype(F32)
     for index in range(count):
         here = pl.ds(coarse[index], 1)
         total[here, :] = total[here, :] + grads[index : index + 1]
@@ -353,6 +487,10 @@
 
 def vmem(count):
     return [pl.BlockSpec(memory_space=pltpu.VMEM) for _ in range(count)]
+
+
+def hbm(count):
+    return [pl.BlockSpec(memory_space=pltpu.HBM) for _ in range(count)]
 
 
 def smem():
@@ -393,54 +531,100 @@
     coarse_count = coarse_rows.shape[0]
     far_width = far_lists.shape[2]
     shift = far_width.bit_length() - 1
-    if far_width != 1 << shift or own % 64 or edge_rows % ROWS or hidden != width:
+    if far_width != 1 << shift or own % 64 or edge_rows % ROWS or edge_rows % MAIN_ROWS or hidden != width:
         raise ValueError("unsupported sizes")
     slots = steps * near_width + peers * far_width
     height = -(-slots // LANES) * LANES
     own_pad = -(-own // LANES) * LANES
     send = send_slots.reshape(-1, LANES)
     recv = recv_slots.reshape(-1, LANES)
+    blocks = edge_rows // ROWS
+    copies = edge_rows // COPY
     row = lambda value: value.reshape(1, -1)
     shape = jax.ShapeDtypeStruct
 
+    small = lambda: pltpu.VMEM((1, width), F32)
+    square = lambda: pltpu.VMEM((width, hidden), BF)
+    index_rows = lambda: pltpu.VMEM((edge_rows // LANES, LANES), jnp.int32)
+    edge_like = lambda: pltpu.VMEM((edge_rows, width), BF)
+    node_like = lambda: pltpu.VMEM((own, width), BF)
+    here = lambda value: pltpu.with_memory_space_constraint(value, pltpu.VMEM)
+
     packed = pl.pallas_call(
         pack_kernel,
-        out_shape=[shape((near_width, width), BF)] * steps
-        + [shape((peers, coarse_count, width), BF)],
+        out_shape=[pltpu.VMEM((near_width, width), BF)] * steps
+        + [pltpu.VMEM((peers, coarse_count, width), BF)],
         in_specs=vmem(3),
         out_specs=vmem(steps + 1),
         name="pack",
     )(nodes, neighbour_send_lists, row(coarse_rows))
-    near = [passed_along(packed[index], "patch", offsets[index]) for index in range(steps)]
-    coarse = lax.all_to_all(
-        packed[steps], "patch", split_axis=0, concat_axis=0, tiled=True
-    ).reshape(-1, width)
+    near = [here(passed_along(packed[index], "patch", offsets[index])) for index in range(steps)]
+    coarse = here(
+        lax.all_to_all(packed[steps], "patch", split_axis=0, concat_axis=0, tiled=True).reshape(
+            -1, width
+        )
+    )
 
     pre_local = pl.pallas_call(
         local_kernel,
-        out_shape=shape((edge_rows, hidden), F32),
-        in_specs=vmem(8),
-        out_specs=vmem(1)[0],
-        scratch_shapes=[pltpu.VMEM((2 * own, hidden), BF)],
+        out_shape=shape((edge_rows, hidden), BF),
+        in_specs=hbm(8),
+        out_specs=hbm(1)[0],
+        scratch_shapes=[
+            node_like(),
+            square(),
+            square(),
+            index_rows(),
+            index_rows(),
+            square(),
+            small(),
+            edge_like(),
+            pltpu.VMEM((2 * own, hidden), BF),
+            edge_like(),
+            pltpu.SemaphoreType.DMA((7 + copies,)),
+            pltpu.SemaphoreType.DMA((copies,)),
+        ],
         cost_estimate=pl.CostEstimate(
             flops=2 * edge_rows * width * hidden * 3, transcendentals=0, bytes_accessed=6 << 20
         ),
         name="local_ahead",
-    )(nodes, edges, w_edge, w_send, w_recv, row(edge_bias), send, recv)
+    )(nodes, w_send, w_recv, send, recv, w_edge, row(edge_bias), edges)
 
     outs = pl.pallas_call(
         lambda *refs: main_kernel(shift, steps, *refs),
-        out_shape=[
+        out_shape=[pltpu.VMEM((near_width, width), BF)] * steps
+        + [
+            pltpu.VMEM((peers * coarse_count, width), BF),
             shape((own, width), BF),
+            shape((own, width), F32),
             shape((edge_rows, width), BF),
             shape((edge_rows, hidden), BF),
-            shape((own, width), F32),
-        ]
-        + [shape((near_width, width), BF)] * steps
-        + [shape((peers * coarse_count, width), BF)],
-        in_specs=[smem()] + vmem(19 + steps),
-        out_specs=vmem(5 + steps),
+        ],
+        in_specs=[smem()] + vmem(1 + steps) + hbm(FIXED + 3),
+        out_specs=vmem(1 + steps) + hbm(4),
         scratch_shapes=[
+            pltpu.VMEM((far_width, peers), jnp.int32),
+            square(),
+            index_rows(),
+            index_rows(),
+            square(),
+            small(),
+            small(),
+            node_like(),
+            square(),
+            square(),
+            small(),
+            square(),
+            small(),
+            node_like(),
+            small(),
+            edge_like(),
+            edge_like(),
+            edge_like(),
+            node_like(),
+            pltpu.VMEM((own, width), F32),
+            edge_like(),
+            edge_like(),
             pltpu.VMEM((height, width), BF),
             pltpu.VMEM((height, hidden), BF),
             pltpu.VMEM((edge_rows, hidden), F32),
@@ -449,6 +633,8 @@
             pltpu.VMEM((own, width), F32),
             pltpu.VMEM((own_pad, width), BF),
             pltpu.VMEM((height, hidden), F32),
+            pltpu.SemaphoreType.DMA((FIXED + 3 * copies,)),
+            pltpu.SemaphoreType.DMA((2 * copies + 2,)),
         ],
         cost_estimate=pl.CostEstimate(
             flops=2 * edge_rows * width * hidden * 8, transcendentals=0, bytes_accessed=16 << 20
@@ -456,50 +642,70 @@
         name="main",
     )(
         block_count,
+        *near,
+        coarse,
+        far_lists[0].T,
+        w_send,
+        send,
+        recv,
+        w_edge_out,
+        row(edge_out_bias),
+        row(edge_gain),
+        nodes,
+        w_agg,
+        w_node,
+        row(node_bias),
+        w_node_out,
+        row(node_out_bias),
+        node_cot,
+        row(node_gain),
         pre_local,
         edges,
         edge_cot,
-        nodes,
-        node_cot,
-        send,
-        recv,
-        far_lists[0],
-        coarse,
-        *near,
-        w_send,
-        w_edge_out,
-        row(edge_out_bias),
-        row(edge_gain),
-        w_node,
-        w_agg,
-        row(node_bias),
-        w_node_out,
-        row(node_out_bias),
-        row(node_gain),
     )
-    new_nodes, new_edges, d_pre, d_node = outs[:4]
+    new_nodes, d_node, new_edges, d_pre = outs[1 + steps :]
     returned = [
-        passed_along(outs[4 + index], "patch", -offsets[index]) for index in range(steps)
+        here(passed_along(outs[index], "patch", -offsets[index])) for index in range(steps)
     ]
-    far_back = lax.all_to_all(
-        outs[4 + steps].reshape(peers, coarse_count, width),
-        "patch",
-        split_axis=0,
-        concat_axis=0,
-        tiled=True,
+    far_back = here(
+        lax.all_to_all(
+            outs[steps].reshape(peers, coarse_count, width),
+            "patch",
+            split_axis=0,
+            concat_axis=0,
+            tiled=True,
+        )
     )
 
-    edge_grad, node_sum = pl.pallas_call(
+    edge_grad, node_sum, near_hit = pl.pallas_call(
         local_back_kernel,
-        out_shape=[shape((edge_rows, width), BF), shape((own, width), F32)],
-        in_specs=vmem(8),
-        out_specs=vmem(2),
-        scratch_shapes=[pltpu.VMEM((2 * own, hidden), F32)],
+        out_shape=[
+            shape((edge_rows, width), BF),
+            pltpu.VMEM((own, width), F32),
+            pltpu.VMEM((own, steps * near_width), BF),
+        ],
+        in_specs=hbm(9),
+        out_specs=hbm(1) + vmem(2),
+        scratch_shapes=[
+            index_rows(),
+            index_rows(),
+            square(),
+            square(),
+            square(),
+            pltpu.VMEM((own, width), F32),
+            pltpu.VMEM((steps, near_width), jnp.int32),
+            edge_like(),
+            edge_like(),
+            edge_like(),
+            pltpu.VMEM((2 * own, hidden), F32),
+            pltpu.SemaphoreType.DMA((7 + 2 * copies,)),
+            pltpu.SemaphoreType.DMA((copies,)),
+        ],
         cost_estimate=pl.CostEstimate(
             flops=2 * edge_rows * width * hidden * 3, transcendentals=0, bytes_accessed=6 << 20
         ),
         name="local_back",
-    )(d_pre, edge_cot, d_node, w_edge, w_send, w_recv, send, recv)
+    )(send, recv, w_edge, w_send, w_recv, d_node, neighbour_send_lists, d_pre, edge_cot)
 
     node_grad = pl.pallas_call(
         combine_kernel,
@@ -508,7 +714,7 @@
         out_specs=vmem(1)[0],
         scratch_shapes=[pltpu.VMEM((own, width), F32)],
         name="combine",
-    )(coarse_rows, node_sum, neighbour_send_lists, far_back, *returned)
+    )(coarse_rows, node_sum, near_hit, far_back, *returned)
     return new_nodes, new_edges, node_grad, edge_grad
 
 

time: 71.8 us -> 60.6 us (0.84)
  Pallas kernels: 39.4 us -> 28.7 us
    pallas_call x1, Pallas kernels: 20.1 us -> 13.8 us  [local(): pl.pallas_call(lambda *refs: main_kernel(shift, steps, *refs), out_shape=...]
    pallas_call x1, Pallas kernels: 7.01 us -> 4.92 us  [local(): pl.pallas_call(local_back_kernel, out_shape=[shape((edge_rows, width), BF...]
    pallas_call x2, Pallas kernels: 9.74 us -> 7.88 us  [the longest x1 5.72 us: local(): pl.pallas_call(local_kernel, out_shape=shape((edge_rows, hidden), BF), in...]
    unnamed x22 -> x4, local copies, waits for them, and re-layouts: 1.36 us -> 1.51 us
  transfers between devices with their start and end apart: 10 -> 10, of which waited for: 0 -> 0; matrix products, arithmetic and copies ran while one was open for 1% -> 0% of each run, Pallas kernels for 20% -> 18%
where the time goes in v3:
time: 60.6 us; the launch traced here: 60.2 us
  Pallas kernels  28.7 us (47%)
  starting transfers between devices  28.6 us (47%)
  local copies, waits for them, and re-layouts  1.51 us (2%)
  between operations  1.38 us (2%)
    ppermute x8, starting transfers between devices, passed_along(): return lax.ppermute(value, axis, pairs)  14.4 us
    pallas_call x1, Pallas kernels, local(): pl.pallas_call(lambda *refs: main_kernel(shift, steps, *refs), out_shape=...  13.8 us
    all_to_all x1, starting transfers between devices, local(): lax.all_to_all(packed[steps], 'patch', split_axis=0, concat_axis=0, tiled...  7.34 us
    all_to_all x1, starting transfers between devices, local(): lax.all_to_all(outs[steps].reshape(peers, coarse_count, width), 'patch',...  6.83 us
    pallas_call x1, Pallas kernels, local(): pl.pallas_call(local_kernel, out_shape=shape((edge_rows, hidden), BF), in...  5.72 us
    pallas_call x1, Pallas kernels, local(): pl.pallas_call(local_back_kernel, out_shape=[shape((edge_rows, width), BF...  4.92 us
    pallas_call x1, Pallas kernels, local(): pl.pallas_call(pack_kernel, out_shape=[pltpu.VMEM((near_width, width), BF...  2.16 us
    pallas_call x1, Pallas kernels, local(): pl.pallas_call(combine_kernel, out_shape=shape((own, width), BF), in_spec...  2.14 us
  transfers between devices with their start and end apart: 10, of which 0 were waited for; matrix products, arithmetic and copies ran while one was open for 0% of the time, Pallas kernels for 18%

profile of v3, /device:TPU:1, one launch (start us, length us, event | category | flops | bytes accessed | tf_op | source)
XLA Modules:
  0.0 60.2 jit_solution(8708725860126346836)
XLA Ops:
  0.6 2.2 %pack.1 = (bf16[64,512]{1,0:T(8,128)(2,1)S(1)}, bf16[64,512]{1,0:T(8,128)(2,1)S(1)}, bf16[64,512]{1,0:T(8,128)(2,1)S(1)}, bf16[64,512]{1,0:T(8,128)(2,1)S(1)}, bf16[16,8,512]{2,1,0:T(8,128)(2,1)}) custom-call(bf16[320,512]{1,0:T(8,128)(2,1)} %refs_13_.1, s32[4,64]{1,0:T(4,128)} %refs_6_.1, s32[1,8]{1,0:T(1,128)} %bitcast.15), custom_call_target="tpu_custom_call" | custom-call | tf_op jit(solution)/shard_map/pack/pallas_call | solution.py:553
  2.8 7.3 %all-to-all-start = ((bf16[16,8,512]{2,1,0:T(8,128)(2,1)}), bf16[16,8,512]{2,1,0:T(8,128)(2,1)S(1)}, u32[]{:S(2)}, u32[]{:S(2)}) async-start(bf16[16,8,512]{2,1,0:T(8,128)(2,1)} %get-tuple-element.25), calls=%async_computation | async-start | bytes 262144 | tf_op jit(solution)/shard_map/all_to_all | solution.py:563
  10.1 1.6 %collective-permute-start = (bf16[64,512]{1,0:T(8,128)(2,1)S(1)}, bf16[64,512]{1,0:T(8,128)(2,1)S(1)}, u32[]{:S(2)}, u32[]{:S(2)}) collective-permute-start(bf16[64,512]{1,0:T(8,128)(2,1)S(1)} %get-tuple-element.21), channel_id=1, source_target_pairs={{0,1},{1,2},{2,3},{3,4},{4,5},{5,6},{6,7},{7,8},{8,9},{9,10},{10,1... | collective-permute-start | bytes 196616 | tf_op jit(solution)/shard_map/ppermute | solution.py:23
  11.8 0.0 collective-permute-start.1
  11.8 1.2 %collective-permute-start.2 = (bf16[64,512]{1,0:T(8,128)(2,1)S(1)}, bf16[64,512]{1,0:T(8,128)(2,1)S(1)}, u32[]{:S(2)}, u32[]{:S(2)}) collective-permute-start(bf16[64,512]{1,0:T(8,128)(2,1)S(1)} %get-tuple-element.23), channel_id=1, source_target_pairs={{0,2},{1,3},{2,4},{3,5},{4,6},{5,7},{6,8},{7,9},{8,10},{9,11},{10,... | collective-permute-start | bytes 196616 | tf_op jit(solution)/shard_map/ppermute | solution.py:23
  12.9 3.0 %collective-permute-start.3 = (bf16[64,512]{1,0:T(8,128)(2,1)S(1)}, bf16[64,512]{1,0:T(8,128)(2,1)S(1)}, u32[]{:S(2)}, u32[]{:S(2)}) collective-permute-start(bf16[64,512]{1,0:T(8,128)(2,1)S(1)} %get-tuple-element.24), channel_id=1, source_target_pairs={{0,14},{1,15},{2,0},{3,1},{4,2},{5,3},{6,4},{7,5},{8,6},{9,7},{10,... | collective-permute-start | bytes 196616 | tf_op jit(solution)/shard_map/ppermute | solution.py:23
  15.9 5.7 %local_ahead.1.refs_21_ = bf16[1536,512]{1,0:T(8,128)(2,1)} custom-call(bf16[320,512]{1,0:T(8,128)(2,1)} %refs_13_.1, bf16[512,512]{1,0:T(8,128)(2,1)} %refs_3_.1, bf16[512,512]{1,0:T(8,128)(2,1)} %refs_4_.1, s32[12,128]{1,0:T(8,128)} %bitcast.16, s32[12,128]{1,0:T(8,128)} %bitcast.19, bf16[512,512]{1,0:T(8,128)(2,1)} %refs_2_.3, f32[1,512]{1,0:T(1,128)} %bitcast.22, ...), custom_call_target="tpu_custom_call" | custom-call | flops 2415919104 | bytes 6291456 | tf_op jit(solution)/shard_map/local_ahead/pallas_call | solution.py:568
  22.3 0.0 collective-permute-done.refs_1_
  22.3 0.0 collective-permute-done.1.refs_2_
  22.3 0.0 collective-permute-done.2.refs_3_
  22.3 0.0 collective-permute-done.3.refs_4_
  22.3 0.0 all-to-all-done
  22.4 13.8 %main.1 = (bf16[64,512]{1,0:T(8,128)(2,1)S(1)}, bf16[64,512]{1,0:T(8,128)(2,1)S(1)}, bf16[64,512]{1,0:T(8,128)(2,1)S(1)}, bf16[64,512]{1,0:T(8,128)(2,1)S(1)}, b...) custom-call(s32[1]{0:T(128)S(6)} %copy.27.refs_0_, ...), custom_call_target="tpu_custom_call" | custom-call | flops 6442450944 | bytes 16777216 | tf_op jit(solution)/shard_map/main/pallas_call | solution.py:593
  36.1 6.8 %all-to-all-start.1 = ((bf16[16,8,512]{2,1,0:T(8,128)(2,1)}), bf16[16,8,512]{2,1,0:T(8,128)(2,1)S(1)}, u32[]{:S(2)}, u32[]{:S(2)}) async-start(bf16[16,8,512]{2,1,0:T(8,128)(2,1)} %bitcast.12), calls=%async_computation.1 | async-start | bytes 262144 | tf_op jit(solution)/shard_map/all_to_all | solution.py:671
  42.9 0.3 collective-permute-start.4
  43.2 1.5 %collective-permute-start.5 = (bf16[64,512]{1,0:T(8,128)(2,1)S(1)}, bf16[64,512]{1,0:T(8,128)(2,1)S(1)}, u32[]{:S(2)}, u32[]{:S(2)}) collective-permute-start(bf16[64,512]{1,0:T(8,128)(2,1)S(1)} %get-tuple-element.34), channel_id=1, source_target_pairs={{0,1},{1,2},{2,3},{3,4},{4,5},{5,6},{6,7},{7,8},{8,9},{9,10},{10,1... | collective-permute-start | bytes 196616 | tf_op jit(solution)/shard_map/ppermute | solution.py:23
  44.7 6.8 %collective-permute-start.6 = (bf16[64,512]{1,0:T(8,128)(2,1)S(1)}, bf16[64,512]{1,0:T(8,128)(2,1)S(1)}, u32[]{:S(2)}, u32[]{:S(2)}) collective-permute-start(bf16[64,512]{1,0:T(8,128)(2,1)S(1)} %get-tuple-element.35), channel_id=1, source_target_pairs={{0,14},{1,15},{2,0},{3,1},{4,2},{5,3},{6,4},{7,5},{8,6},{9,7},{10,... | collective-permute-start | bytes 196616 | tf_op jit(solution)/shard_map/ppermute | solution.py:23
  51.5 0.0 collective-permute-start.7
  51.5 4.9 %local_back.1 = (bf16[1536,512]{1,0:T(8,128)(2,1)}, f32[320,512]{1,0:T(8,128)S(1)}, bf16[320,256]{1,0:T(8,128)(2,1)S(1)}) custom-call(s32[12,128]{1,0:T(8,128)} %bitcast.18, s32[12,128]{1,0:T(8,128)} %bitcast.21, bf16[512,512]{1,0:T(8,128)(2,1)} %refs_2_.3, bf16[512,512]{1,0:T(8,128)(2,1)} %refs_3_.1, bf16[512,512]{1,0:T(8,128)(2,1)} %refs_4_.1, ...), custom_call_target="tpu_custom_call" | custom-call | flops 2415919104 | bytes 6291456 | tf_op jit(solution)/shard_map/local_back/pallas_call | solution.py:680
  56.5 0.0 copy-start
  56.5 0.8 %copy-done = f32[320,512]{1,0:T(8,128)} copy-done((f32[320,512]{1,0:T(8,128)}, f32[320,512]{1,0:T(8,128)S(1)}, u32[]{:S(2)}) %copy-start) | copy-done | bytes 655384
  57.3 0.0 copy-start.1
  57.3 0.7 %copy-done.1 = bf16[320,256]{1,0:T(8,128)(2,1)} copy-done((bf16[320,256]{1,0:T(8,128)(2,1)}, bf16[320,256]{1,0:T(8,128)(2,1)S(1)}, u32[]{:S(2)}) %copy-start.1) | copy-done | bytes 163864
  58.0 0.0 collective-permute-done.4.refs_0_
  58.0 0.0 collective-permute-done.5.refs_1_
  58.0 0.0 collective-permute-done.6.refs_2_
  58.0 0.0 collective-permute-done.7.refs_3_
  58.0 0.0 all-to-all-done.1.far
  58.0 2.1 %combine.1 = bf16[320,512]{1,0:T(8,128)(2,1)} custom-call(s32[8]{0:T(128)} %coarse.1, f32[320,512]{1,0:T(8,128)} %copy-done, bf16[320,256]{1,0:T(8,128)(2,1)} %copy-done.1, bf16[16,8,512]{2,1,0:T(8,128)(2,1)S(1)} %all-to-all-done.1.far, bf16[64,512]{1,0:T(8,128)(2,1)S(1)} %collective-permute-done.4.refs_0_, ...), custom_call_target="tpu_custom_call" | custom-call | tf_op jit(solution)/shard_map/combine/pallas_call | solution.py:710
Async XLA Ops:
  2.8 19.6 %all-to-all-start = ((bf16[16,8,512]{2,1,0:T(8,128)(2,1)}), bf16[16,8,512]{2,1,0:T(8,128)(2,1)S(1)}, u32[]{:S(2)}, u32[]{:S(2)}) async-start(bf16[16,8,512]{2,1,0:T(8,128)(2,1)} %get-tuple-element.25), calls=%async_computation | async-start | bytes 262144 | tf_op jit(solution)/shard_map/all_to_all | solution.py:563
  10.1 12.2 %collective-permute-start = (bf16[64,512]{1,0:T(8,128)(2,1)S(1)}, bf16[64,512]{1,0:T(8,128)(2,1)S(1)}, u32[]{:S(2)}, u32[]{:S(2)}) collective-permute-start(bf16[64,512]{1,0:T(8,128)(2,1)S(1)} %get-tuple-element.21), channel_id=1, source_target_pairs={{0,1},{1,2},{2,3},{3,4},{4,5},{5,6},{6,7},{7,8},{8,9},{9,10},{10,1... | collective-permute-start | bytes 196616 | tf_op jit(solution)/shard_map/ppermute | solution.py:23
  11.8 10.6 %collective-permute-start.1 = (bf16[64,512]{1,0:T(8,128)(2,1)S(1)}, bf16[64,512]{1,0:T(8,128)(2,1)S(1)}, u32[]{:S(2)}, u32[]{:S(2)}) collective-permute-start(bf16[64,512]{1,0:T(8,128)(2,1)S(1)} %get-tuple-element.22), channel_id=1, source_target_pairs={{0,15},{1,0},{2,1},{3,2},{4,3},{5,4},{6,5},{7,6},{8,7},{9,8},{10,9... | collective-permute-start | bytes 196616 | tf_op jit(solution)/shard_map/ppermute | solution.py:23
  11.8 10.6 %collective-permute-start.2 = (bf16[64,512]{1,0:T(8,128)(2,1)S(1)}, bf16[64,512]{1,0:T(8,128)(2,1)S(1)}, u32[]{:S(2)}, u32[]{:S(2)}) collective-permute-start(bf16[64,512]{1,0:T(8,128)(2,1)S(1)} %get-tuple-element.23), channel_id=1, source_target_pairs={{0,2},{1,3},{2,4},{3,5},{4,6},{5,7},{6,8},{7,9},{8,10},{9,11},{10,... | collective-permute-start | bytes 196616 | tf_op jit(solution)/shard_map/ppermute | solution.py:23
  12.9 9.4 %collective-permute-start.3 = (bf16[64,512]{1,0:T(8,128)(2,1)S(1)}, bf16[64,512]{1,0:T(8,128)(2,1)S(1)}, u32[]{:S(2)}, u32[]{:S(2)}) collective-permute-start(bf16[64,512]{1,0:T(8,128)(2,1)S(1)} %get-tuple-element.24), channel_id=1, source_target_pairs={{0,14},{1,15},{2,0},{3,1},{4,2},{5,3},{6,4},{7,5},{8,6},{9,7},{10,... | collective-permute-start | bytes 196616 | tf_op jit(solution)/shard_map/ppermute | solution.py:23
  36.1 21.9 %all-to-all-start.1 = ((bf16[16,8,512]{2,1,0:T(8,128)(2,1)}), bf16[16,8,512]{2,1,0:T(8,128)(2,1)S(1)}, u32[]{:S(2)}, u32[]{:S(2)}) async-start(bf16[16,8,512]{2,1,0:T(8,128)(2,1)} %bitcast.12), calls=%async_computation.1 | async-start | bytes 262144 | tf_op jit(solution)/shard_map/all_to_all | solution.py:671
  42.9 15.0 %collective-permute-start.4 = (bf16[64,512]{1,0:T(8,128)(2,1)S(1)}, bf16[64,512]{1,0:T(8,128)(2,1)S(1)}, u32[]{:S(2)}, u32[]{:S(2)}) collective-permute-start(bf16[64,512]{1,0:T(8,128)(2,1)S(1)} %get-tuple-element.33), channel_id=1, source_target_pairs={{0,15},{1,0},{2,1},{3,2},{4,3},{5,4},{6,5},{7,6},{8,7},{9,8},{10,9... | collective-permute-start | bytes 196616 | tf_op jit(solution)/shard_map/ppermute | solution.py:23
  43.2 14.8 %collective-permute-start.5 = (bf16[64,512]{1,0:T(8,128)(2,1)S(1)}, bf16[64,512]{1,0:T(8,128)(2,1)S(1)}, u32[]{:S(2)}, u32[]{:S(2)}) collective-permute-start(bf16[64,512]{1,0:T(8,128)(2,1)S(1)} %get-tuple-element.34), channel_id=1, source_target_pairs={{0,1},{1,2},{2,3},{3,4},{4,5},{5,6},{6,7},{7,8},{8,9},{9,10},{10,1... | collective-permute-start | bytes 196616 | tf_op jit(solution)/shard_map/ppermute | solution.py:23
  44.7 13.3 %collective-permute-start.6 = (bf16[64,512]{1,0:T(8,128)(2,1)S(1)}, bf16[64,512]{1,0:T(8,128)(2,1)S(1)}, u32[]{:S(2)}, u32[]{:S(2)}) collective-permute-start(bf16[64,512]{1,0:T(8,128)(2,1)S(1)} %get-tuple-element.35), channel_id=1, source_target_pairs={{0,14},{1,15},{2,0},{3,1},{4,2},{5,3},{6,4},{7,5},{8,6},{9,7},{10,... | collective-permute-start | bytes 196616 | tf_op jit(solution)/shard_map/ppermute | solution.py:23
  51.5 6.5 %collective-permute-start.7 = (bf16[64,512]{1,0:T(8,128)(2,1)S(1)}, bf16[64,512]{1,0:T(8,128)(2,1)S(1)}, u32[]{:S(2)}, u32[]{:S(2)}) collective-permute-start(bf16[64,512]{1,0:T(8,128)(2,1)S(1)} %get-tuple-element.36), channel_id=1, source_target_pairs={{0,2},{1,3},{2,4},{3,5},{4,6},{5,7},{6,8},{7,9},{8,10},{9,11},{10,... | collective-permute-start | bytes 196616 | tf_op jit(solution)/shard_map/ppermute | solution.py:23
  56.5 0.8 %copy-start = (f32[320,512]{1,0:T(8,128)}, f32[320,512]{1,0:T(8,128)S(1)}, u32[]{:S(2)}) copy-start(f32[320,512]{1,0:T(8,128)S(1)} %get-tuple-element.30.node_sum) | copy-start | bytes 1966084
  57.3 0.7 %copy-start.1 = (bf16[320,256]{1,0:T(8,128)(2,1)}, bf16[320,256]{1,0:T(8,128)(2,1)S(1)}, u32[]{:S(2)}) copy-start(bf16[320,256]{1,0:T(8,128)(2,1)S(1)} %get-tuple-element.31.hit) | copy-start | bytes 491524

commit v4 on v3

--- a/solution.py
+++ b/solution.py
@@ -17,9 +17,9 @@
 F32 = jnp.float32
 
 
-def passed_along(value, axis, steps):
+def swapped(value, axis, bit, shift):
     count = lax.axis_size(axis)
-    pairs = [(source, (source + steps) % count) for source in range(count)]
+    pairs = [(source, (((source + shift) ^ bit) - shift) % count) for source in range(count)]
     return lax.ppermute(value, axis, pairs)
 
 
@@ -126,24 +126,42 @@
     return pl.ds(pl.multiple_of(index * COPY, COPY), COPY)
 
 
-def pack_kernel(nodes, lists, coarse, *outs):
+def place():
+    index = lax.axis_index("patch")
+    return index & 1, (index >> 1) & 1
+
+
+def pack_kernel(nodes, lists, coarse, pair_out, first_out, second_out, out):
     rows = nodes[...]
     own = rows.shape[0]
-    steps, width = lists.shape
+    width = lists.shape[1]
+    _, odd = place()
     ids = lax.broadcasted_iota(jnp.int32, (own, width), 0)
-    for index in range(steps):
-        hit = ones_where(ids == lists[index : index + 1, :])
-        outs[index][...] = mm_l(hit, rows).astype(BF)
+
+    def picked(index):
+        return mm_l(ones_where(ids == lists[pl.ds(index, 1), :]), rows).astype(BF)
+
+    pair_out[:width] = picked(odd)
+    pair_out[width:] = picked(1 - odd)
+    first_out[...] = picked(2 + odd)
+    second_out[...] = picked(3 - odd)
     count = coarse.shape[1]
     hit = ones_where(lax.broadcasted_iota(jnp.int32, (own, count), 0) == coarse[...])
-    picked = mm_l(hit, rows).astype(BF)
-    out = outs[steps]
+    chosen = mm_l(hit, rows).astype(BF)
 
     def put(index, carry):
-        out[index] = picked
+        out[index] = chosen
         return carry
 
     lax.fori_loop(0, out.shape[0], put, 0)
+
+
+def join_kernel(relay, pair, first, second, first_out, second_out):
+    width = first.shape[0]
+    first_out[:width] = first[...]
+    first_out[width:] = pair[relay[0] * width : (relay[0] + 1) * width]
+    second_out[:width] = second[...]
+    second_out[width:] = pair[relay[1] * width : (relay[1] + 1) * width]
 
 
 def local_kernel(*refs):
@@ -203,24 +221,24 @@
 def main_kernel(shift, steps, *refs):
     take = iter(refs)
     count = next(take)
-    near = [next(take) for _ in range(steps)]
+    received = [next(take) for _ in range(3)]
     coarse = next(take)
     sources = [next(take) for _ in range(FIXED)]
     block_sources = [next(take) for _ in range(3)]
-    near_out = [next(take) for _ in range(steps)]
-    far_out = next(take)
+    pair_out, first_out, second_out, far_out = [next(take) for _ in range(4)]
     new_nodes_out, d_node_out, new_edges_out, d_pre_out = [next(take) for _ in range(4)]
     targets = [next(take) for _ in range(FIXED)]
     pre_in, edges, edge_cot = block_targets = [next(take) for _ in range(3)]
     new_nodes, d_node, new_edges, d_pre = [next(take) for _ in range(4)]
-    rows2, table2, slope, unit, inverse, agg, d_agg, sums2 = [next(take) for _ in range(8)]
+    stack, rows2, table2, slope, unit, inverse, agg, d_agg, sums2 = [next(take) for _ in range(9)]
     load, store = next(take), next(take)
     far_lists, w_send, send, recv, w_edge_out, edge_out_bias, edge_gain = targets[:7]
     nodes, w_agg, w_node, node_bias, w_node_out, node_out_bias, node_cot, node_gain = targets[7:]
     own = nodes.shape[0]
     width = nodes.shape[1]
     far_width, peers = far_lists.shape
-    near_width = near[0].shape[0]
+    near_width = first_out.shape[0]
+    core, odd = place()
     near_rows = steps * near_width
     height = table2.shape[0]
     coarse_rows = coarse.shape[0] // peers
@@ -269,8 +287,19 @@
         for slot in range(far_width)
     ]
     rows2[...] = jnp.zeros(rows2.shape, BF)
-    for index in range(steps):
-        rows2[index * near_width : (index + 1) * near_width] = near[index][...]
+    for index, ref in enumerate(received):
+        stack[2 * index * near_width : 2 * (index + 1) * near_width] = ref[...]
+    below = 4 - 2 * odd
+    above = 2 + 2 * odd
+    chosen = [
+        jnp.where(core == 0, below + 1, odd),
+        jnp.where(core == 0, 1 - odd, above + 1),
+        below,
+        above,
+    ]
+    for index, slot in enumerate(chosen):
+        start = pl.multiple_of(slot * near_width, near_width)
+        rows2[index * near_width : (index + 1) * near_width] = stack[pl.ds(start, near_width), :]
     for slot in range(far_width):
         start = near_rows + slot * peers
         rows2[start : start + peers] = mm_l(far_hits[slot], coarse[...]).astype(BF)
@@ -386,8 +415,16 @@
     lax.fori_loop(0, blocks, back, 0)
 
     d_rows2 = mm_t(sums2[...].astype(BF), w_send[...])
-    for index in range(steps):
-        near_out[index][...] = d_rows2[index * near_width : (index + 1) * near_width].astype(BF)
+    stack[: steps * near_width] = d_rows2[: steps * near_width].astype(BF)
+    outgoing = [
+        (pair_out, 0, 1 - core),
+        (pair_out, 1, core),
+        (first_out, 0, 3 - odd),
+        (second_out, 0, 2 + odd),
+    ]
+    for ref, index, slot in outgoing:
+        start = pl.multiple_of(slot * near_width, near_width)
+        ref[index * near_width : (index + 1) * near_width] = stack[pl.ds(start, near_width), :]
     d_coarse = None
     for slot in range(far_width):
         start = near_rows + slot * peers
@@ -461,19 +498,22 @@
     wait_all(fixed[3:])
     total = sums[...].astype(BF)
     node_sum[...] = d_node[...] + mm_t(total[:own], w_send[...]) + mm_t(total[own:], w_recv[...])
-    steps, width = lists.shape
+    width = lists.shape[1]
     ids = lax.broadcasted_iota(jnp.int32, (own, width), 0)
+    core, odd = place()
+    same = jnp.where(core == odd, 0, 2 * own)
+    other = jnp.where(core == odd, 2 * own, 0)
+    hits = [(core, 0), (2 + odd, 0), (odd, other), (3 - odd, 0), (1 - odd, same)]
     near_hit[...] = jnp.concatenate(
-        [ones_where(ids == lists[index : index + 1, :]) for index in range(steps)], axis=1
+        [ones_where(ids == lists[pl.ds(index, 1), :] + away) for index, away in hits], axis=1
     )
     for index in range(copies):
         block_out(index).wait()
 
 
-def combine_kernel(coarse, node_sum, hit, far, *refs):
-    steps = len(refs) - 2
-    near = jnp.concatenate([ref[...] for ref in refs[:steps]], axis=0)
-    out, total = refs[steps], refs[steps + 1]
+def combine_kernel(coarse, node_sum, hit, far, pair, first, second, out, total):
+    width = pair.shape[0] // 2
+    near = jnp.concatenate([pair[:width], first[...], second[...]], axis=0)
     total[...] = node_sum[...] + mm(hit[...], near)
     peers, count, _ = far.shape
     grads = far[0].astype(F32)
@@ -527,11 +567,10 @@
     edge_rows = edges.shape[0]
     peers = lax.axis_size("patch")
     steps, near_width = neighbour_send_lists.shape
-    offsets = [(index // 2 + 1) * (1 - 2 * (index % 2)) for index in range(steps)]
     coarse_count = coarse_rows.shape[0]
     far_width = far_lists.shape[2]
     shift = far_width.bit_length() - 1
-    if far_width != 1 << shift or own % 64 or edge_rows % ROWS or edge_rows % MAIN_ROWS or hidden != width:
+    if steps != 4 or peers % 4 or far_width != 1 << shift or own % 64 or edge_rows % ROWS or edge_rows % MAIN_ROWS or hidden != width:
         raise ValueError("unsupported sizes")
     slots = steps * near_width + peers * far_width
     height = -(-slots // LANES) * LANES
@@ -550,20 +589,31 @@
     node_like = lambda: pltpu.VMEM((own, width), BF)
     here = lambda value: pltpu.with_memory_space_constraint(value, pltpu.VMEM)
 
+    near_like = pltpu.VMEM((near_width, width), BF)
+    pair_like = pltpu.VMEM((2 * near_width, width), BF)
+
+    def exchanged(pair, first, second, rows, relay):
+        pair = here(swapped(pair, "patch", 1, 0))
+        rows = lax.all_to_all(rows, "patch", split_axis=0, concat_axis=0, tiled=True)
+        first, second = pl.pallas_call(
+            lambda *refs: join_kernel(relay, *refs),
+            out_shape=[pair_like] * 2,
+            in_specs=vmem(3),
+            out_specs=vmem(2),
+            name="join",
+        )(pair, here(first), here(second))
+        first = here(swapped(first, "patch", 2, 0))
+        second = here(swapped(second, "patch", 2, 2))
+        return pair, first, second, rows
+
     packed = pl.pallas_call(
         pack_kernel,
-        out_shape=[pltpu.VMEM((near_width, width), BF)] * steps
-        + [pltpu.VMEM((peers, coarse_count, width), BF)],
+        out_shape=[pair_like, near_like, near_like, pltpu.VMEM((peers, coarse_count, width), BF)],
         in_specs=vmem(3),
-        out_specs=vmem(steps + 1),
+        out_specs=vmem(4),
         name="pack",
     )(nodes, neighbour_send_lists, row(coarse_rows))
-    near = [here(passed_along(packed[index], "patch", offsets[index])) for index in range(steps)]
-    coarse = here(
-        lax.all_to_all(packed[steps], "patch", split_axis=0, concat_axis=0, tiled=True).reshape(
-            -1, width
-        )
-    )
+    *near, coarse = exchanged(*packed, (0, 1))
 
     pre_local = pl.pallas_call(
         local_kernel,
@@ -592,16 +642,18 @@
 
     outs = pl.pallas_call(
         lambda *refs: main_kernel(shift, steps, *refs),
-        out_shape=[pltpu.VMEM((near_width, width), BF)] * steps
-        + [
+        out_shape=[
+            pair_like,
+            near_like,
+            near_like,
             pltpu.VMEM((peers * coarse_count, width), BF),
             shape((own, width), BF),
             shape((own, width), F32),
             shape((edge_rows, width), BF),
             shape((edge_rows, hidden), BF),
         ],
-        in_specs=[smem()] + vmem(1 + steps) + hbm(FIXED + 3),
-        out_specs=vmem(1 + steps) + hbm(4),
+        in_specs=[smem()] + vmem(4) + hbm(FIXED + 3),
+        out_specs=vmem(4) + hbm(4),
         scratch_shapes=[
             pltpu.VMEM((far_width, peers), jnp.int32),
             square(),
@@ -625,6 +677,7 @@
             pltpu.VMEM((own, width), F32),
             edge_like(),
             edge_like(),
+            pltpu.VMEM((6 * near_width, width), BF),
             pltpu.VMEM((height, width), BF),
             pltpu.VMEM((height, hidden), BF),
             pltpu.VMEM((edge_rows, hidden), F32),
@@ -643,7 +696,7 @@
     )(
         block_count,
         *near,
-        coarse,
+        here(coarse.reshape(-1, width)),
         far_lists[0].T,
         w_send,
         send,
@@ -663,18 +716,9 @@
         edges,
         edge_cot,
     )
-    new_nodes, d_node, new_edges, d_pre = outs[1 + steps :]
-    returned = [
-        here(passed_along(outs[index], "patch", -offsets[index])) for index in range(steps)
-    ]
-    far_back = here(
-        lax.all_to_all(
-            outs[steps].reshape(peers, coarse_count, width),
-            "patch",
-            split_axis=0,
-            concat_axis=0,
-            tiled=True,
-        )
+    new_nodes, d_node, new_edges, d_pre = outs[4:]
+    *returned, far_back = exchanged(
+        *outs[:3], outs[3].reshape(peers, coarse_count, width), (1, 1)
     )
 
     edge_grad, node_sum, near_hit = pl.pallas_call(
@@ -682,7 +726,7 @@
         out_shape=[
             shape((edge_rows, width), BF),
             pltpu.VMEM((own, width), F32),
-            pltpu.VMEM((own, steps * near_width), BF),
+            pltpu.VMEM((own, 5 * near_width), BF),
         ],
         in_specs=hbm(9),
         out_specs=hbm(1) + vmem(2),
@@ -710,11 +754,11 @@
     node_grad = pl.pallas_call(
         combine_kernel,
         out_shape=shape((own, width), BF),
-        in_specs=[smem()] + vmem(3 + steps),
+        in_specs=[smem()] + vmem(6),
         out_specs=vmem(1)[0],
         scratch_shapes=[pltpu.VMEM((own, width), F32)],
         name="combine",
-    )(coarse_rows, node_sum, near_hit, far_back, *returned)
+    )(coarse_rows, here(node_sum), here(near_hit), here(far_back), *returned)
     return new_nodes, new_edges, node_grad, edge_grad
 
 

time: 60.6 us -> 52.5 us (0.87)
  the two profiles are of different devices: /device:TPU:1 before, /device:TPU:0 now
where the time goes in v4:
time: 52.5 us; the launch traced here: 52.1 us
  Pallas kernels  28.3 us (54%)
  starting transfers between devices  21.9 us (42%)
  between operations  1.4 us (3%)
    pallas_call x1, Pallas kernels, local(): pl.pallas_call(lambda *refs: main_kernel(shift, steps, *refs), out_shape=...  13.7 us
    ppermute x6, starting transfers between devices, swapped(): return lax.ppermute(value, axis, pairs)  11.1 us
    all_to_all x2, starting transfers between devices, exchanged(): lax.all_to_all(rows, 'patch', split_axis=0, concat_axis=0, tiled=True)  10.8 us
    pallas_call x1, Pallas kernels, local(): pl.pallas_call(local_kernel, out_shape=shape((edge_rows, hidden), BF), in...  5.72 us
    pallas_call x1, Pallas kernels, local(): pl.pallas_call(local_back_kernel, out_shape=[shape((edge_rows, width), BF...  4.92 us
    pallas_call x1, Pallas kernels, local(): pl.pallas_call(pack_kernel, out_shape=[pair_like, near_like, near_like, p...  2.16 us
    pallas_call x1, Pallas kernels, local(): pl.pallas_call(combine_kernel, out_shape=shape((own, width), BF), in_spec...  1.76 us
  transfers between devices with their start and end apart: 8, of which 1 were waited for; matrix products, arithmetic and copies ran while one was open for 0% of the time, Pallas kernels for 20%

profile of v4, /device:TPU:0, one launch (start us, length us, event | category | flops | bytes accessed | tf_op | source)
XLA Modules:
  0.0 52.1 jit_solution(17842745436171949501)
XLA Ops:
  0.6 2.2 %pack.1 = (bf16[128,512]{1,0:T(8,128)(2,1)S(1)}, bf16[64,512]{1,0:T(8,128)(2,1)S(1)}, bf16[64,512]{1,0:T(8,128)(2,1)S(1)}, bf16[16,8,512]{2,1,0:T(8,128)(2,1)}) custom-call(bf16[320,512]{1,0:T(8,128)(2,1)} %refs_12_.1, s32[4,64]{1,0:T(4,128)} %refs_6_.3, s32[1,8]{1,0:T(1,128)} %bitcast.15), custom_call_target="tpu_custom_call" | custom-call | tf_op jit(solution)/shard_map/pack/pallas_call | solution.py:609
  2.8 0.5 collective-permute-start
  3.3 7.0 %all-to-all-start = ((bf16[16,8,512]{2,1,0:T(8,128)(2,1)}), bf16[16,8,512]{2,1,0:T(8,128)(2,1)S(1)}, u32[]{:S(2)}, u32[]{:S(2)}) async-start(bf16[16,8,512]{2,1,0:T(8,128)(2,1)} %get-tuple-element.28), calls=%async_computation | async-start | bytes 262144 | tf_op jit(solution)/shard_map/all_to_all | solution.py:597
  11.0 0.0 collective-permute-done.refs_0_.refs_1_
  11.0 2.0 %collective-permute-start.1 = (bf16[128,512]{1,0:T(8,128)(2,1)S(1)}, bf16[128,512]{1,0:T(8,128)(2,1)S(1)}, u32[]{:S(2)}, u32[]{:S(2)}) collective-permute-start(bf16[128,512]{1,0:T(8,128)(2,1)S(1)} %get-tuple-element.26), channel_id=1, source_target_pairs={{0,2},{1,3},{2,0},{3,1},{4,6},{5,7},{6,4},{7,5},{8,10},{9,11},{10,... | collective-permute-start | bytes 393224 | tf_op jit(solution)/shard_map/ppermute | solution.py:23
  13.0 3.3 %collective-permute-start.2 = (bf16[128,512]{1,0:T(8,128)(2,1)S(1)}, bf16[128,512]{1,0:T(8,128)(2,1)S(1)}, u32[]{:S(2)}, u32[]{:S(2)}) collective-permute-start(bf16[128,512]{1,0:T(8,128)(2,1)S(1)} %get-tuple-element.27), channel_id=1, source_target_pairs={{0,14},{1,15},{2,4},{3,5},{4,2},{5,3},{6,8},{7,9},{8,6},{9,7},{10,... | collective-permute-start | bytes 393224 | tf_op jit(solution)/shard_map/ppermute | solution.py:23
  16.3 5.7 %local_ahead.1.refs_20_ = bf16[1536,512]{1,0:T(8,128)(2,1)} custom-call(bf16[320,512]{1,0:T(8,128)(2,1)} %refs_12_.1, bf16[512,512]{1,0:T(8,128)(2,1)} %refs_3_.1, bf16[512,512]{1,0:T(8,128)(2,1)} %refs_4_.1, s32[12,128]{1,0:T(8,128)} %bitcast.16, s32[12,128]{1,0:T(8,128)} %bitcast.19, bf16[512,512]{1,0:T(8,128)(2,1)} %refs_2_.3, f32[1,512]{1,0:T(1,128)} %bitcast.22, ...), custom_call_target="tpu_custom_call" | custom-call | flops 2415919104 | bytes 6291456 | tf_op jit(solution)/shard_map/local_ahead/pallas_call | solution.py:618
  22.0 0.0 all-to-all-done
  22.0 0.0 collective-permute-done.1.refs_2_
  22.0 0.0 collective-permute-done.2.refs_3_
  22.0 13.7 %main.1 = (bf16[128,512]{1,0:T(8,128)(2,1)S(1)}, bf16[64,512]{1,0:T(8,128)(2,1)S(1)}, bf16[64,512]{1,0:T(8,128)(2,1)S(1)}, bf16[128,512]{1,0:T(8,128)(2,1)}, bf1...) custom-call(s32[1]{0:T(128)S(6)} %copy.27.refs_0_, ...), custom_call_target="tpu_custom_call" | custom-call | flops 6442450944 | bytes 16777216 | tf_op jit(solution)/shard_map/main/pallas_call | solution.py:643
  35.8 0.1 collective-permute-start.3
  35.9 3.8 %all-to-all-start.1 = ((bf16[16,8,512]{2,1,0:T(8,128)(2,1)}), bf16[16,8,512]{2,1,0:T(8,128)(2,1)S(1)}, u32[]{:S(2)}, u32[]{:S(2)}) async-start(bf16[16,8,512]{2,1,0:T(8,128)(2,1)} %bitcast.12), calls=%async_computation.1 | async-start | bytes 262144 | tf_op jit(solution)/shard_map/all_to_all | solution.py:597
  39.6 0.0 collective-permute-done.3.refs_0_.pair
  39.7 2.0 %collective-permute-start.4 = (bf16[128,512]{1,0:T(8,128)(2,1)S(1)}, bf16[128,512]{1,0:T(8,128)(2,1)S(1)}, u32[]{:S(2)}, u32[]{:S(2)}) collective-permute-start(bf16[128,512]{1,0:T(8,128)(2,1)S(1)} %get-tuple-element.39), channel_id=1, source_target_pairs={{0,2},{1,3},{2,0},{3,1},{4,6},{5,7},{6,4},{7,5},{8,10},{9,11},{10,... | collective-permute-start | bytes 393224 | tf_op jit(solution)/shard_map/ppermute | solution.py:23
  41.7 3.3 %collective-permute-start.5 = (bf16[128,512]{1,0:T(8,128)(2,1)S(1)}, bf16[128,512]{1,0:T(8,128)(2,1)S(1)}, u32[]{:S(2)}, u32[]{:S(2)}) collective-permute-start(bf16[128,512]{1,0:T(8,128)(2,1)S(1)} %get-tuple-element.40), channel_id=1, source_target_pairs={{0,14},{1,15},{2,4},{3,5},{4,2},{5,3},{6,8},{7,9},{8,6},{9,7},{10,... | collective-permute-start | bytes 393224 | tf_op jit(solution)/shard_map/ppermute | solution.py:23
  44.9 4.9 %local_back.1 = (bf16[1536,512]{1,0:T(8,128)(2,1)}, f32[320,512]{1,0:T(8,128)S(1)}, bf16[320,320]{1,0:T(8,128)(2,1)S(1)}) custom-call(s32[12,128]{1,0:T(8,128)} %bitcast.18, s32[12,128]{1,0:T(8,128)} %bitcast.21, bf16[512,512]{1,0:T(8,128)(2,1)} %refs_2_.3, bf16[512,512]{1,0:T(8,128)(2,1)} %refs_3_.1, bf16[512,512]{1,0:T(8,128)(2,1)} %refs_4_.1, ...), custom_call_target="tpu_custom_call" | custom-call | flops 2415919104 | bytes 6291456 | tf_op jit(solution)/shard_map/local_back/pallas_call | solution.py:724
  49.9 0.0 all-to-all-done.1.far
  49.9 0.0 collective-permute-done.4.first
  49.9 0.5 collective-permute-done.5.second
  50.4 1.8 %combine.1 = bf16[320,512]{1,0:T(8,128)(2,1)} custom-call(s32[8]{0:T(128)} %coarse.1, f32[320,512]{1,0:T(8,128)S(1)} %get-tuple-element.33.node_sum, bf16[320,320]{1,0:T(8,128)(2,1)S(1)} %get-tuple-element.34.hit, bf16[16,8,512]{2,1,0:T(8,128)(2,1)S(1)} %all-to-all-done.1.far, bf16[128,512]{1,0:T(8,128)(2,1)S(1)} %collective-permute-done.3.refs_0_.pair, ...), custom_call_target="tpu_custom_call" | custom-call | tf_op jit(solution)/shard_map/combine/pallas_call | solution.py:754
  (2 shorter events, 0.0 us)
Async XLA Ops:
  2.8 8.2 %collective-permute-start = (bf16[128,512]{1,0:T(8,128)(2,1)S(1)}, bf16[128,512]{1,0:T(8,128)(2,1)S(1)}, u32[]{:S(2)}, u32[]{:S(2)}) collective-permute-start(bf16[128,512]{1,0:T(8,128)(2,1)S(1)} %get-tuple-element.23), channel_id=1, source_target_pairs={{0,1},{1,0},{2,3},{3,2},{4,5},{5,4},{6,7},{7,6},{8,9},{9,8},{10,11... | collective-permute-start | bytes 393224 | tf_op jit(solution)/shard_map/ppermute | solution.py:23
  3.3 18.7 %all-to-all-start = ((bf16[16,8,512]{2,1,0:T(8,128)(2,1)}), bf16[16,8,512]{2,1,0:T(8,128)(2,1)S(1)}, u32[]{:S(2)}, u32[]{:S(2)}) async-start(bf16[16,8,512]{2,1,0:T(8,128)(2,1)} %get-tuple-element.28), calls=%async_computation | async-start | bytes 262144 | tf_op jit(solution)/shard_map/all_to_all | solution.py:597
  11.0 11.0 %collective-permute-start.1 = (bf16[128,512]{1,0:T(8,128)(2,1)S(1)}, bf16[128,512]{1,0:T(8,128)(2,1)S(1)}, u32[]{:S(2)}, u32[]{:S(2)}) collective-permute-start(bf16[128,512]{1,0:T(8,128)(2,1)S(1)} %get-tuple-element.26), channel_id=1, source_target_pairs={{0,2},{1,3},{2,0},{3,1},{4,6},{5,7},{6,4},{7,5},{8,10},{9,11},{10,... | collective-permute-start | bytes 393224 | tf_op jit(solution)/shard_map/ppermute | solution.py:23
  13.0 9.0 %collective-permute-start.2 = (bf16[128,512]{1,0:T(8,128)(2,1)S(1)}, bf16[128,512]{1,0:T(8,128)(2,1)S(1)}, u32[]{:S(2)}, u32[]{:S(2)}) collective-permute-start(bf16[128,512]{1,0:T(8,128)(2,1)S(1)} %get-tuple-element.27), channel_id=1, source_target_pairs={{0,14},{1,15},{2,4},{3,5},{4,2},{5,3},{6,8},{7,9},{8,6},{9,7},{10,... | collective-permute-start | bytes 393224 | tf_op jit(solution)/shard_map/ppermute | solution.py:23
  35.8 3.9 %collective-permute-start.3 = (bf16[128,512]{1,0:T(8,128)(2,1)S(1)}, bf16[128,512]{1,0:T(8,128)(2,1)S(1)}, u32[]{:S(2)}, u32[]{:S(2)}) collective-permute-start(bf16[128,512]{1,0:T(8,128)(2,1)S(1)} %get-tuple-element.36), channel_id=1, source_target_pairs={{0,1},{1,0},{2,3},{3,2},{4,5},{5,4},{6,7},{7,6},{8,9},{9,8},{10,11... | collective-permute-start | bytes 393224 | tf_op jit(solution)/shard_map/ppermute | solution.py:23
  35.9 14.0 %all-to-all-start.1 = ((bf16[16,8,512]{2,1,0:T(8,128)(2,1)}), bf16[16,8,512]{2,1,0:T(8,128)(2,1)S(1)}, u32[]{:S(2)}, u32[]{:S(2)}) async-start(bf16[16,8,512]{2,1,0:T(8,128)(2,1)} %bitcast.12), calls=%async_computation.1 | async-start | bytes 262144 | tf_op jit(solution)/shard_map/all_to_all | solution.py:597
  39.7 10.2 %collective-permute-start.4 = (bf16[128,512]{1,0:T(8,128)(2,1)S(1)}, bf16[128,512]{1,0:T(8,128)(2,1)S(1)}, u32[]{:S(2)}, u32[]{:S(2)}) collective-permute-start(bf16[128,512]{1,0:T(8,128)(2,1)S(1)} %get-tuple-element.39), channel_id=1, source_target_pairs={{0,2},{1,3},{2,0},{3,1},{4,6},{5,7},{6,4},{7,5},{8,10},{9,11},{10,... | collective-permute-start | bytes 393224 | tf_op jit(solution)/shard_map/ppermute | solution.py:23
  41.7 8.7 %collective-permute-start.5 = (bf16[128,512]{1,0:T(8,128)(2,1)S(1)}, bf16[128,512]{1,0:T(8,128)(2,1)S(1)}, u32[]{:S(2)}, u32[]{:S(2)}) collective-permute-start(bf16[128,512]{1,0:T(8,128)(2,1)S(1)} %get-tuple-element.40), channel_id=1, source_target_pairs={{0,14},{1,15},{2,4},{3,5},{4,2},{5,3},{6,8},{7,9},{8,6},{9,7},{10,... | collective-permute-start | bytes 393224 | tf_op jit(solution)/shard_map/ppermute | solution.py:23

commit v5 on v4

--- a/solution.py
+++ b/solution.py
@@ -8,10 +8,10 @@
 BLOCK = 128
 LANES = 128
 ROWS = 512
-MAIN_ROWS = 1536
+HALVES = 2
 COPY = 256
 CHUNK = 16
-FIXED = 15
+FIXED = 16
 EPS = 1e-05
 BF = jnp.bfloat16
 F32 = jnp.float32
@@ -218,9 +218,20 @@
         block_out(index).wait()
 
 
+def pipeline(stages):
+    held = [None] * HALVES
+    for wave in range(HALVES + len(stages) - 1):
+        for index in range(HALVES):
+            if 0 <= wave - index < len(stages):
+                held[index] = stages[wave - index](index, held[index])
+    total = held[0]
+    for value in held[1:]:
+        total = total + value
+    return total
+
+
 def main_kernel(shift, steps, *refs):
     take = iter(refs)
-    count = next(take)
     received = [next(take) for _ in range(3)]
     coarse = next(take)
     sources = [next(take) for _ in range(FIXED)]
@@ -230,10 +241,10 @@
     targets = [next(take) for _ in range(FIXED)]
     pre_in, edges, edge_cot = block_targets = [next(take) for _ in range(3)]
     new_nodes, d_node, new_edges, d_pre = [next(take) for _ in range(4)]
-    stack, rows2, table2, slope, unit, inverse, agg, d_agg, sums2 = [next(take) for _ in range(9)]
+    stack, rows2, table2, slope, unit, inverse, d_agg = [next(take) for _ in range(7)]
     load, store = next(take), next(take)
-    far_lists, w_send, send, recv, w_edge_out, edge_out_bias, edge_gain = targets[:7]
-    nodes, w_agg, w_node, node_bias, w_node_out, node_out_bias, node_cot, node_gain = targets[7:]
+    far_lists, w_send, send, recv, w_edge_out, edge_out_bias, edge_gain, count = targets[:8]
+    nodes, w_agg, w_node, node_bias, w_node_out, node_out_bias, node_cot, node_gain = targets[8:]
     own = nodes.shape[0]
     width = nodes.shape[1]
     far_width, peers = far_lists.shape
@@ -242,43 +253,21 @@
     near_rows = steps * near_width
     height = table2.shape[0]
     coarse_rows = coarse.shape[0] // peers
-    parts = MAIN_ROWS // LANES
-    blocks = edges.shape[0] // MAIN_ROWS
+    half = edges.shape[0] // HALVES
+    parts = half // LANES
     copies = edges.shape[0] // COPY
-    ratio = MAIN_ROWS // COPY
-    live_count = count[0]
     fixed = copies_of(sources, targets, load)
 
-    def block_in(which, index):
-        here = rows_of(index)
-        return pltpu.make_async_copy(
-            block_sources[which].at[here, :],
-            block_targets[which].at[here, :],
-            load.at[FIXED + which * copies + index],
-        )
-
-    def block_out(which, index):
-        here = rows_of(index)
-        source, target = ((new_edges, new_edges_out), (d_pre, d_pre_out))[which]
-        return pltpu.make_async_copy(
-            source.at[here, :], target.at[here, :], store.at[which * copies + index]
-        )
-
+    whole = copies_of(block_sources, block_targets, load.at[pl.ds(FIXED, 3)])
+    edge_outs = copies_of((new_edges, d_pre), (new_edges_out, d_pre_out), store.at[pl.ds(2, 2)])
     node_outs = [
-        pltpu.make_async_copy(new_nodes, new_nodes_out, store.at[2 * copies]),
-        pltpu.make_async_copy(d_node, d_node_out, store.at[2 * copies + 1]),
+        pltpu.make_async_copy(new_nodes, new_nodes_out, store.at[0]),
+        pltpu.make_async_copy(d_node, d_node_out, store.at[1]),
     ]
     start_all(fixed[:4])
-    block_in(0, 0).start()
-    start_all(fixed[4:7])
-    block_in(1, 0).start()
-    for index in range(1, copies):
-        block_in(0, index).start()
-        block_in(1, index).start()
-    start_all(fixed[7:])
-    for index in range(copies):
-        block_in(2, index).start()
-
+    whole[0].start()
+    start_all(fixed[4:])
+    start_all(whole[1:])
     fixed[0].wait()
     far_ids = lax.broadcasted_iota(jnp.int32, (coarse.shape[0], peers), 0)
     far_base = lax.broadcasted_iota(jnp.int32, (coarse.shape[0], peers), 1) * coarse_rows
@@ -305,60 +294,62 @@
         rows2[start : start + peers] = mm_l(far_hits[slot], coarse[...]).astype(BF)
     fixed[1].wait()
     table2[...] = mm(rows2[...], w_send[...]).astype(BF)
-    wait_all(fixed[2:4])
-    agg[...] = jnp.zeros(agg.shape, F32)
-    wait_all(fixed[4:7])
-
-    def block_rows(ref, index, part):
-        return ref[pl.ds(index * parts + part, 1), :]
-
-    def ahead(index, carry):
-        start = pl.multiple_of(index * MAIN_ROWS, MAIN_ROWS)
+    wait_all(fixed[2:8])
+
+    def live_gain(block):
+        return edge_gain[...] * jnp.where(count[...] > block, 1.0, 0.0)
+
+    def picked(ref, index, part):
+        here = index * parts + part
+        return ref[here : here + 1, :]
+
+    def remote_row(index, part):
+        return remote_index(picked(send, index, part), own, near_rows, peers, shift)
+
+    def pick_remote(index, _):
         hit = jnp.concatenate(
-            [
-                pick(remote_index(block_rows(send, index, part), own, near_rows, peers, shift), height)
-                for part in range(parts)
-            ],
-            axis=0,
+            [pick(remote_row(index, part), height) for part in range(parts)], axis=0
         )
-        remote = mm(hit, table2[...])
+        return mm(hit, table2[...])
+
+    def activate(index, remote):
+        if index == 0:
+            whole[0].wait()
         hidden = []
-        for low in range(0, MAIN_ROWS, CHUNK):
-            if low % COPY == 0:
-                block_in(0, index * ratio + low // COPY).wait()
-            here = pl.ds(start + low, CHUNK)
+        for low in range(0, half, CHUNK):
+            here = slice(index * half + low, index * half + low + CHUNK)
             value = pre_in[here, :].astype(F32) + remote[low : low + CHUNK]
             part_hidden, part_slope = silu_parts(value)
             slope[here, :] = part_slope
             hidden.append(part_hidden.astype(BF))
-        out = mm(jnp.concatenate(hidden, axis=0), w_edge_out[...])
+        return jnp.concatenate(hidden, axis=0)
+
+    def project(index, hidden):
+        return mm(hidden, w_edge_out[...])
+
+    def message_of(index, out):
         sent = []
-        for low in range(0, MAIN_ROWS, CHUNK):
-            if low % COPY == 0:
-                block_in(1, index * ratio + low // COPY).wait()
-            here = pl.ds(start + low, CHUNK)
+        for low in range(0, half, CHUNK):
+            here = slice(index * half + low, index * half + low + CHUNK)
             if low % BLOCK == 0:
-                live = jnp.where(index * parts + low // BLOCK < live_count, 1.0, 0.0)
-                live_gain = edge_gain[...] * live.astype(F32)
+                gain = live_gain((index * half + low) // BLOCK)
             part_unit, part_inverse = norm_parts(out[low : low + CHUNK] + edge_out_bias[...])
             unit[here, :] = part_unit
             inverse[here, :] = part_inverse
-            message = part_unit * live_gain
-            new_edges[here, :] = (edges[here, :].astype(F32) + message).astype(BF)
-            sent.append(message.astype(BF))
-            if (low + CHUNK) % COPY == 0:
-                block_out(0, index * ratio + low // COPY).start()
-        hit_t = jnp.concatenate(
-            [pick_t(block_rows(recv, index, part), own) for part in range(parts)], axis=1
+            sent.append((part_unit * gain).astype(BF))
+        return jnp.concatenate(sent, axis=0)
+
+    def gather_up(index, sent):
+        hit = jnp.concatenate(
+            [pick_t(picked(recv, index, part), own) for part in range(parts)], axis=1
         )
-        agg[...] += mm(hit_t, jnp.concatenate(sent, axis=0))
-        return carry
-
-    lax.fori_loop(0, blocks, ahead, 0)
-
-    wait_all(fixed[7:])
+        return mm(hit, sent)
+
+    total = pipeline([pick_remote, activate, project, message_of, gather_up])
+    wait_all(fixed[8:])
+    wait_all(whole[1:])
     rows = nodes[...]
-    pre_node = mm(rows, w_node[...]) + mm(agg[...].astype(BF), w_agg[...]) + node_bias[...]
+    pre_node = mm(rows, w_node[...]) + mm(total.astype(BF), w_agg[...]) + node_bias[...]
     node_hidden, node_slope = silu_parts(pre_node)
     node_out = mm(node_hidden.astype(BF), w_node_out[...]) + node_out_bias[...]
     node_unit, node_inverse = norm_parts(node_out)
@@ -370,51 +361,52 @@
     d_agg[...] = jnp.zeros(d_agg.shape, BF)
     d_agg[:own] = mm_t(d_pre_node, w_agg[...]).astype(BF)
     d_node[...] = cot + mm_t(d_pre_node, w_node[...])
-    sums2[...] = jnp.zeros(sums2.shape, F32)
+    for low in range(0, edges.shape[0], CHUNK):
+        here = slice(low, low + CHUNK)
+        if low % BLOCK == 0:
+            gain = live_gain(low // BLOCK)
+        new_edges[here, :] = (edges[here, :].astype(F32) + unit[here, :] * gain).astype(BF)
     start_all(node_outs)
-
-    def back(index, carry):
-        start = pl.multiple_of(index * MAIN_ROWS, MAIN_ROWS)
+    edge_outs[0].start()
+
+    def pick_back(index, _):
         hit = jnp.concatenate(
-            [pick(block_rows(recv, index, part), d_agg.shape[0]) for part in range(parts)], axis=0
+            [pick(picked(recv, index, part), d_agg.shape[0]) for part in range(parts)], axis=0
         )
-        d_sent = mm(hit, d_agg[...])
+        return mm(hit, d_agg[...])
+
+    def norm_grad(index, d_sent):
         outs = []
-        for low in range(0, MAIN_ROWS, CHUNK):
-            if low % COPY == 0:
-                block_in(2, index * ratio + low // COPY).wait()
-            here = pl.ds(start + low, CHUNK)
+        for low in range(0, half, CHUNK):
+            here = slice(index * half + low, index * half + low + CHUNK)
             if low % BLOCK == 0:
-                live = jnp.where(index * parts + low // BLOCK < live_count, 1.0, 0.0)
-                live_gain = edge_gain[...] * live.astype(F32)
+                gain = live_gain((index * half + low) // BLOCK)
             d_message = edge_cot[here, :].astype(F32) + d_sent[low : low + CHUNK]
-            d_unit = d_message * live_gain
-            outs.append(norm_back(d_unit, unit[here, :], inverse[here, :]).astype(BF))
-        d_hid = mm_t(jnp.concatenate(outs, axis=0), w_edge_out[...])
-        pres = []
-        for low in range(0, MAIN_ROWS, CHUNK):
-            here = pl.ds(start + low, CHUNK)
+            outs.append(norm_back(d_message * gain, unit[here, :], inverse[here, :]).astype(BF))
+        return jnp.concatenate(outs, axis=0)
+
+    def project_back(index, d_out):
+        return mm_t(d_out, w_edge_out[...])
+
+    def activate_back(index, d_hid):
+        grads = []
+        for low in range(0, half, CHUNK):
+            here = slice(index * half + low, index * half + low + CHUNK)
             part = (d_hid[low : low + CHUNK] * slope[here, :]).astype(BF)
             d_pre[here, :] = part
-            pres.append(part)
-            if (low + CHUNK) % COPY == 0:
-                block_out(1, index * ratio + low // COPY).start()
-        hit_t = jnp.concatenate(
-            [
-                pick_t(
-                    remote_index(block_rows(send, index, part), own, near_rows, peers, shift),
-                    height,
-                )
-                for part in range(parts)
-            ],
-            axis=1,
+            grads.append(part)
+        return jnp.concatenate(grads, axis=0)
+
+    def gather_back(index, grads):
+        hit = jnp.concatenate(
+            [pick_t(remote_row(index, part), height) for part in range(parts)], axis=1
         )
-        sums2[...] += mm(hit_t, jnp.concatenate(pres, axis=0))
-        return carry
-
-    lax.fori_loop(0, blocks, back, 0)
-
-    d_rows2 = mm_t(sums2[...].astype(BF), w_send[...])
+        return mm(hit, grads)
+
+    sums2 = pipeline([pick_back, norm_grad, project_back, activate_back, gather_back])
+    edge_outs[1].start()
+
+    d_rows2 = mm_t(sums2.astype(BF), w_send[...])
     stack[: steps * near_width] = d_rows2[: steps * near_width].astype(BF)
     outgoing = [
         (pair_out, 0, 1 - core),
@@ -431,18 +423,16 @@
         term = mm(far_hits[slot], d_rows2[start : start + peers].astype(BF))
         d_coarse = term if d_coarse is None else d_coarse + term
     far_out[...] = d_coarse.astype(BF)
-    for index in range(copies):
-        block_out(0, index).wait()
-        block_out(1, index).wait()
+    wait_all(edge_outs)
     wait_all(node_outs)
 
 
 def local_back_kernel(*refs):
-    sources, block_sources = refs[:7], refs[7:9]
-    edge_grad_out, node_sum, near_hit = refs[9:12]
-    targets, block_targets = refs[12:19], refs[19:21]
-    edge_grad, sums, load, store = refs[21:]
-    send, recv, w_edge, w_send, w_recv, d_node, lists = targets
+    sources, block_sources = refs[:8], refs[8:10]
+    edge_grad_out, node_sum, near_hit = refs[10:13]
+    targets, block_targets = refs[13:21], refs[21:23]
+    edge_grad, sums, load, store = refs[23:]
+    send, recv, w_edge, w_send, w_recv, d_node, lists, coarse = targets
     d_pre, cot = block_targets
     own = d_node.shape[0]
     parts = ROWS // LANES
@@ -455,7 +445,7 @@
         return pltpu.make_async_copy(
             block_sources[which].at[here, :],
             block_targets[which].at[here, :],
-            load.at[7 + which * copies + index],
+            load.at[8 + which * copies + index],
         )
 
     def block_out(index):
@@ -504,25 +494,25 @@
     same = jnp.where(core == odd, 0, 2 * own)
     other = jnp.where(core == odd, 2 * own, 0)
     hits = [(core, 0), (2 + odd, 0), (odd, other), (3 - odd, 0), (1 - odd, same)]
-    near_hit[...] = jnp.concatenate(
+    count = coarse.shape[1]
+    far_slots = near_hit.shape[1] - 5 * width
+    spread = ones_where(
+        (lax.broadcasted_iota(jnp.int32, (count, far_slots), 1) & (count - 1))
+        == lax.broadcasted_iota(jnp.int32, (count, far_slots), 0)
+    )
+    coarse_hit = ones_where(lax.broadcasted_iota(jnp.int32, (own, count), 0) == coarse[...])
+    near_hit[:, : 5 * width] = jnp.concatenate(
         [ones_where(ids == lists[pl.ds(index, 1), :] + away) for index, away in hits], axis=1
     )
+    near_hit[:, 5 * width :] = mm(coarse_hit, spread).astype(BF)
     for index in range(copies):
         block_out(index).wait()
 
 
-def combine_kernel(coarse, node_sum, hit, far, pair, first, second, out, total):
+def combine_kernel(node_sum, hit, far, pair, first, second, out):
     width = pair.shape[0] // 2
-    near = jnp.concatenate([pair[:width], first[...], second[...]], axis=0)
-    total[...] = node_sum[...] + mm(hit[...], near)
-    peers, count, _ = far.shape
-    grads = far[0].astype(F32)
-    for index in range(1, peers):
-        grads = grads + far[index].astype(F32)
-    for index in range(count):
-        here = pl.ds(coarse[index], 1)
-        total[here, :] = total[here, :] + grads[index : index + 1]
-    out[...] = total[...].astype(BF)
+    rows = jnp.concatenate([pair[:width], first[...], second[...], far[...]], axis=0)
+    out[...] = (node_sum[...] + mm(hit[...], rows)).astype(BF)
 
 
 def vmem(count):
@@ -531,10 +521,6 @@
 
 def hbm(count):
     return [pl.BlockSpec(memory_space=pltpu.HBM) for _ in range(count)]
-
-
-def smem():
-    return pl.BlockSpec(memory_space=pltpu.SMEM)
 
 
 def local(
@@ -570,7 +556,7 @@
     coarse_count = coarse_rows.shape[0]
     far_width = far_lists.shape[2]
     shift = far_width.bit_length() - 1
-    if steps != 4 or peers % 4 or far_width != 1 << shift or own % 64 or edge_rows % ROWS or edge_rows % MAIN_ROWS or hidden != width:
+    if steps != 4 or coarse_count & (coarse_count - 1) or (5 * near_width) % 64 or peers % 4 or far_width != 1 << shift or own % 64 or edge_rows % ROWS or edge_rows % (HALVES * BLOCK) or hidden != width:
         raise ValueError("unsupported sizes")
     slots = steps * near_width + peers * far_width
     height = -(-slots // LANES) * LANES
@@ -608,7 +594,7 @@
 
     packed = pl.pallas_call(
         pack_kernel,
-        out_shape=[pair_like, near_like, near_like, pltpu.VMEM((peers, coarse_count, width), BF)],
+        out_shape=[pair_like, near_like, near_like, shape((peers, coarse_count, width), BF)],
         in_specs=vmem(3),
         out_specs=vmem(4),
         name="pack",
@@ -646,13 +632,13 @@
             pair_like,
             near_like,
             near_like,
-            pltpu.VMEM((peers * coarse_count, width), BF),
+            shape((peers * coarse_count, width), BF),
             shape((own, width), BF),
             shape((own, width), F32),
             shape((edge_rows, width), BF),
             shape((edge_rows, hidden), BF),
         ],
-        in_specs=[smem()] + vmem(4) + hbm(FIXED + 3),
+        in_specs=vmem(4) + hbm(FIXED + 3),
         out_specs=vmem(4) + hbm(4),
         scratch_shapes=[
             pltpu.VMEM((far_width, peers), jnp.int32),
@@ -662,6 +648,7 @@
             square(),
             small(),
             small(),
+            pltpu.VMEM((1, 1), jnp.int32),
             node_like(),
             square(),
             square(),
@@ -683,18 +670,15 @@
             pltpu.VMEM((edge_rows, hidden), F32),
             pltpu.VMEM((edge_rows, width), F32),
             pltpu.VMEM((edge_rows, 1), F32),
-            pltpu.VMEM((own, width), F32),
             pltpu.VMEM((own_pad, width), BF),
-            pltpu.VMEM((height, hidden), F32),
-            pltpu.SemaphoreType.DMA((FIXED + 3 * copies,)),
-            pltpu.SemaphoreType.DMA((2 * copies + 2,)),
+            pltpu.SemaphoreType.DMA((FIXED + 3,)),
+            pltpu.SemaphoreType.DMA((4,)),
         ],
         cost_estimate=pl.CostEstimate(
             flops=2 * edge_rows * width * hidden * 8, transcendentals=0, bytes_accessed=16 << 20
         ),
         name="main",
     )(
-        block_count,
         *near,
         here(coarse.reshape(-1, width)),
         far_lists[0].T,
@@ -704,6 +688,7 @@
         w_edge_out,
         row(edge_out_bias),
         row(edge_gain),
+        block_count.reshape(1, 1),
         nodes,
         w_agg,
         w_node,
@@ -726,9 +711,9 @@
         out_shape=[
             shape((edge_rows, width), BF),
             pltpu.VMEM((own, width), F32),
-            pltpu.VMEM((own, 5 * near_width), BF),
+            pltpu.VMEM((own, 5 * near_width + peers * coarse_count), BF),
         ],
-        in_specs=hbm(9),
+        in_specs=hbm(10),
         out_specs=hbm(1) + vmem(2),
         scratch_shapes=[
             index_rows(),
@@ -738,27 +723,38 @@
             square(),
             pltpu.VMEM((own, width), F32),
             pltpu.VMEM((steps, near_width), jnp.int32),
+            pltpu.VMEM((1, coarse_count), jnp.int32),
             edge_like(),
             edge_like(),
             edge_like(),
             pltpu.VMEM((2 * own, hidden), F32),
-            pltpu.SemaphoreType.DMA((7 + 2 * copies,)),
+            pltpu.SemaphoreType.DMA((8 + 2 * copies,)),
             pltpu.SemaphoreType.DMA((copies,)),
         ],
         cost_estimate=pl.CostEstimate(
             flops=2 * edge_rows * width * hidden * 3, transcendentals=0, bytes_accessed=6 << 20
         ),
         name="local_back",
-    )(send, recv, w_edge, w_send, w_recv, d_node, neighbour_send_lists, d_pre, edge_cot)
+    )(
+        send,
+        recv,
+        w_edge,
+        w_send,
+        w_recv,
+        d_node,
+        neighbour_send_lists,
+        row(coarse_rows),
+        d_pre,
+        edge_cot,
+    )
 
     node_grad = pl.pallas_call(
         combine_kernel,
         out_shape=shape((own, width), BF),
-        in_specs=[smem()] + vmem(6),
+        in_specs=vmem(6),
         out_specs=vmem(1)[0],
-        scratch_shapes=[pltpu.VMEM((own, width), F32)],
         name="combine",
-    )(coarse_rows, here(node_sum), here(near_hit), here(far_back), *returned)
+    )(here(node_sum), here(near_hit), here(far_back.reshape(-1, width)), *returned)
     return new_nodes, new_edges, node_grad, edge_grad
 
 

time: 52.5 us -> 50.5 us (0.962)
  Pallas kernels: 28.3 us -> 26.5 us
    pallas_call x1, Pallas kernels: 13.7 us -> 12.4 us  [local(): pl.pallas_call(lambda *refs: main_kernel(shift, steps, *refs), out_shape=...]
    pallas_call x1, Pallas kernels: 1.76 us -> 1.06 us  [local(): pl.pallas_call(combine_kernel, out_shape=shape((own, width), BF), in_spec...]
  transfers between devices with their start and end apart: 8 -> 8, of which waited for: 1 -> 1; matrix products, arithmetic and copies ran while one was open for 0% -> 0% of each run, Pallas kernels for 20% -> 22%
where the time goes in v5:
time: 50.5 us; the launch traced here: 50.1 us
  Pallas kernels  26.5 us (52%)
  starting transfers between devices  21.9 us (43%)
  between operations  1.4 us (3%)
    pallas_call x1, Pallas kernels, local(): pl.pallas_call(lambda *refs: main_kernel(shift, steps, *refs), out_shape=...  12.4 us
    ppermute x6, starting transfers between devices, swapped(): return lax.ppermute(value, axis, pairs)  11.1 us
    all_to_all x2, starting transfers between devices, exchanged(): lax.all_to_all(rows, 'patch', split_axis=0, concat_axis=0, tiled=True)  10.8 us
    pallas_call x1, Pallas kernels, local(): pl.pallas_call(local_kernel, out_shape=shape((edge_rows, hidden), BF), in...  5.72 us
    pallas_call x1, Pallas kernels, local(): pl.pallas_call(local_back_kernel, out_shape=[shape((edge_rows, width), BF...  5.05 us
    pallas_call x1, Pallas kernels, local(): pl.pallas_call(pack_kernel, out_shape=[pair_like, near_like, near_like, s...  2.16 us
    pallas_call x1, Pallas kernels, local(): pl.pallas_call(combine_kernel, out_shape=shape((own, width), BF), in_spec...  1.06 us
  transfers between devices with their start and end apart: 8, of which 1 were waited for; matrix products, arithmetic and copies ran while one was open for 0% of the time, Pallas kernels for 22%

profile of v5, /device:TPU:0, one launch (start us, length us, event | category | flops | bytes accessed | tf_op | source)
XLA Modules:
  0.0 50.1 jit_solution(13241125610262351560)
XLA Ops:
  0.6 2.2 %pack.1 = (bf16[128,512]{1,0:T(8,128)(2,1)S(1)}, bf16[64,512]{1,0:T(8,128)(2,1)S(1)}, bf16[64,512]{1,0:T(8,128)(2,1)S(1)}, bf16[16,8,512]{2,1,0:T(8,128)(2,1)}) custom-call(bf16[320,512]{1,0:T(8,128)(2,1)} %refs_12_.1, s32[4,64]{1,0:T(4,128)} %refs_6_.1, s32[1,8]{1,0:T(1,128)} %bitcast.20), custom_call_target="tpu_custom_call" | custom-call | tf_op jit(solution)/shard_map/pack/pallas_call | solution.py:595
  2.8 0.5 collective-permute-start
  3.3 7.0 %all-to-all-start = ((bf16[16,8,512]{2,1,0:T(8,128)(2,1)}), bf16[16,8,512]{2,1,0:T(8,128)(2,1)S(1)}, u32[]{:S(2)}, u32[]{:S(2)}) async-start(bf16[16,8,512]{2,1,0:T(8,128)(2,1)} %get-tuple-element.28), calls=%async_computation | async-start | bytes 262144 | tf_op jit(solution)/shard_map/all_to_all | solution.py:583
  11.0 0.0 collective-permute-done.refs_0_
  11.0 2.0 %collective-permute-start.1 = (bf16[128,512]{1,0:T(8,128)(2,1)S(1)}, bf16[128,512]{1,0:T(8,128)(2,1)S(1)}, u32[]{:S(2)}, u32[]{:S(2)}) collective-permute-start(bf16[128,512]{1,0:T(8,128)(2,1)S(1)} %get-tuple-element.26), channel_id=1, source_target_pairs={{0,2},{1,3},{2,0},{3,1},{4,6},{5,7},{6,4},{7,5},{8,10},{9,11},{10,... | collective-permute-start | bytes 393224 | tf_op jit(solution)/shard_map/ppermute | solution.py:23
  13.0 3.3 %collective-permute-start.2 = (bf16[128,512]{1,0:T(8,128)(2,1)S(1)}, bf16[128,512]{1,0:T(8,128)(2,1)S(1)}, u32[]{:S(2)}, u32[]{:S(2)}) collective-permute-start(bf16[128,512]{1,0:T(8,128)(2,1)S(1)} %get-tuple-element.27), channel_id=1, source_target_pairs={{0,14},{1,15},{2,4},{3,5},{4,2},{5,3},{6,8},{7,9},{8,6},{9,7},{10,... | collective-permute-start | bytes 393224 | tf_op jit(solution)/shard_map/ppermute | solution.py:23
  16.3 5.7 %local_ahead.1.refs_20_ = bf16[1536,512]{1,0:T(8,128)(2,1)} custom-call(bf16[320,512]{1,0:T(8,128)(2,1)} %refs_12_.1, bf16[512,512]{1,0:T(8,128)(2,1)} %refs_3_.1, bf16[512,512]{1,0:T(8,128)(2,1)} %refs_4_.1, s32[12,128]{1,0:T(8,128)} %bitcast.22, s32[12,128]{1,0:T(8,128)} %bitcast.25, bf16[512,512]{1,0:T(8,128)(2,1)} %refs_2_.3, f32[1,512]{1,0:T(1,128)} %bitcast.28, ...), custom_call_target="tpu_custom_call" | custom-call | flops 2415919104 | bytes 6291456 | tf_op jit(solution)/shard_map/local_ahead/pallas_call | solution.py:604
  22.0 0.0 all-to-all-done
  22.0 0.0 collective-permute-done.1.refs_1_
  22.0 0.0 collective-permute-done.2.refs_2_
  22.0 12.4 %main.1 = (bf16[128,512]{1,0:T(8,128)(2,1)S(1)}, bf16[64,512]{1,0:T(8,128)(2,1)S(1)}, bf16[64,512]{1,0:T(8,128)(2,1)S(1)}, bf16[128,512]{1,0:T(8,128)(2,1)}, bf1...) custom-call(bf16[128,512]{1,0:T(8,128)(2,1)S(1)} %collective-permute-done.ref, ...), custom_call_target="tpu_custom_call" | custom-call | flops 6442450944 | bytes 16777216 | tf_op jit(solution)/shard_map/main/pallas_call | solution.py:629
  34.5 0.1 collective-permute-start.3
  34.5 3.8 %all-to-all-start.1 = ((bf16[16,8,512]{2,1,0:T(8,128)(2,1)}), bf16[16,8,512]{2,1,0:T(8,128)(2,1)S(1)}, u32[]{:S(2)}, u32[]{:S(2)}) async-start(bf16[16,8,512]{2,1,0:T(8,128)(2,1)} %bitcast.19), calls=%async_computation.1 | async-start | bytes 262144 | tf_op jit(solution)/shard_map/all_to_all | solution.py:583
  38.3 0.0 collective-permute-done.3.refs_0_.pair
  38.3 2.0 %collective-permute-start.4 = (bf16[128,512]{1,0:T(8,128)(2,1)S(1)}, bf16[128,512]{1,0:T(8,128)(2,1)S(1)}, u32[]{:S(2)}, u32[]{:S(2)}) collective-permute-start(bf16[128,512]{1,0:T(8,128)(2,1)S(1)} %get-tuple-element.39), channel_id=1, source_target_pairs={{0,2},{1,3},{2,0},{3,1},{4,6},{5,7},{6,4},{7,5},{8,10},{9,11},{10,... | collective-permute-start | bytes 393224 | tf_op jit(solution)/shard_map/ppermute | solution.py:23
  40.3 3.3 %collective-permute-start.5 = (bf16[128,512]{1,0:T(8,128)(2,1)S(1)}, bf16[128,512]{1,0:T(8,128)(2,1)S(1)}, u32[]{:S(2)}, u32[]{:S(2)}) collective-permute-start(bf16[128,512]{1,0:T(8,128)(2,1)S(1)} %get-tuple-element.40), channel_id=1, source_target_pairs={{0,14},{1,15},{2,4},{3,5},{4,2},{5,3},{6,8},{7,9},{8,6},{9,7},{10,... | collective-permute-start | bytes 393224 | tf_op jit(solution)/shard_map/ppermute | solution.py:23
  43.6 5.0 %local_back.1 = (bf16[1536,512]{1,0:T(8,128)(2,1)}, f32[320,512]{1,0:T(8,128)S(1)}, bf16[320,448]{1,0:T(8,128)(2,1)S(1)}) custom-call(s32[12,128]{1,0:T(8,128)} %bitcast.24, s32[12,128]{1,0:T(8,128)} %bitcast.27, bf16[512,512]{1,0:T(8,128)(2,1)} %refs_2_.3, bf16[512,512]{1,0:T(8,128)(2,1)} %refs_3_.1, bf16[512,512]{1,0:T(8,128)(2,1)} %refs_4_.1, ...), custom_call_target="tpu_custom_call" | custom-call | flops 2415919104 | bytes 6291456 | tf_op jit(solution)/shard_map/local_back/pallas_call | solution.py:709
  48.7 0.0 all-to-all-done.1
  48.7 0.0 collective-permute-done.4.first
  48.7 0.3 collective-permute-done.5.second
  49.0 1.1 %combine.1 = bf16[320,512]{1,0:T(8,128)(2,1)} custom-call(f32[320,512]{1,0:T(8,128)S(1)} %get-tuple-element.33.node_sum, bf16[320,448]{1,0:T(8,128)(2,1)S(1)} %get-tuple-element.34.hit, bf16[128,512]{1,0:T(8,128)(2,1)S(1)} %bitcast.17, bf16[128,512]{1,0:T(8,128)(2,1)S(1)} %collective-permute-done.3.refs_0_.pair, ...), custom_call_target="tpu_custom_call" | custom-call | tf_op jit(solution)/shard_map/combine/pallas_call | solution.py:751
  (2 shorter events, 0.0 us)
Async XLA Ops:
  2.8 8.2 %collective-permute-start = (bf16[128,512]{1,0:T(8,128)(2,1)S(1)}, bf16[128,512]{1,0:T(8,128)(2,1)S(1)}, u32[]{:S(2)}, u32[]{:S(2)}) collective-permute-start(bf16[128,512]{1,0:T(8,128)(2,1)S(1)} %get-tuple-element.23), channel_id=1, source_target_pairs={{0,1},{1,0},{2,3},{3,2},{4,5},{5,4},{6,7},{7,6},{8,9},{9,8},{10,11... | collective-permute-start | bytes 393224 | tf_op jit(solution)/shard_map/ppermute | solution.py:23
  3.3 18.7 %all-to-all-start = ((bf16[16,8,512]{2,1,0:T(8,128)(2,1)}), bf16[16,8,512]{2,1,0:T(8,128)(2,1)S(1)}, u32[]{:S(2)}, u32[]{:S(2)}) async-start(bf16[16,8,512]{2,1,0:T(8,128)(2,1)} %get-tuple-element.28), calls=%async_computation | async-start | bytes 262144 | tf_op jit(solution)/shard_map/all_to_all | solution.py:583
  11.0 11.0 %collective-permute-start.1 = (bf16[128,512]{1,0:T(8,128)(2,1)S(1)}, bf16[128,512]{1,0:T(8,128)(2,1)S(1)}, u32[]{:S(2)}, u32[]{:S(2)}) collective-permute-start(bf16[128,512]{1,0:T(8,128)(2,1)S(1)} %get-tuple-element.26), channel_id=1, source_target_pairs={{0,2},{1,3},{2,0},{3,1},{4,6},{5,7},{6,4},{7,5},{8,10},{9,11},{10,... | collective-permute-start | bytes 393224 | tf_op jit(solution)/shard_map/ppermute | solution.py:23
  13.0 9.0 %collective-permute-start.2 = (bf16[128,512]{1,0:T(8,128)(2,1)S(1)}, bf16[128,512]{1,0:T(8,128)(2,1)S(1)}, u32[]{:S(2)}, u32[]{:S(2)}) collective-permute-start(bf16[128,512]{1,0:T(8,128)(2,1)S(1)} %get-tuple-element.27), channel_id=1, source_target_pairs={{0,14},{1,15},{2,4},{3,5},{4,2},{5,3},{6,8},{7,9},{8,6},{9,7},{10,... | collective-permute-start | bytes 393224 | tf_op jit(solution)/shard_map/ppermute | solution.py:23
  34.5 3.8 %collective-permute-start.3 = (bf16[128,512]{1,0:T(8,128)(2,1)S(1)}, bf16[128,512]{1,0:T(8,128)(2,1)S(1)}, u32[]{:S(2)}, u32[]{:S(2)}) collective-permute-start(bf16[128,512]{1,0:T(8,128)(2,1)S(1)} %get-tuple-element.36), channel_id=1, source_target_pairs={{0,1},{1,0},{2,3},{3,2},{4,5},{5,4},{6,7},{7,6},{8,9},{9,8},{10,11... | collective-permute-start | bytes 393224 | tf_op jit(solution)/shard_map/ppermute | solution.py:23
  34.5 14.1 %all-to-all-start.1 = ((bf16[16,8,512]{2,1,0:T(8,128)(2,1)}), bf16[16,8,512]{2,1,0:T(8,128)(2,1)S(1)}, u32[]{:S(2)}, u32[]{:S(2)}) async-start(bf16[16,8,512]{2,1,0:T(8,128)(2,1)} %bitcast.19), calls=%async_computation.1 | async-start | bytes 262144 | tf_op jit(solution)/shard_map/all_to_all | solution.py:583
  38.3 10.3 %collective-permute-start.4 = (bf16[128,512]{1,0:T(8,128)(2,1)S(1)}, bf16[128,512]{1,0:T(8,128)(2,1)S(1)}, u32[]{:S(2)}, u32[]{:S(2)}) collective-permute-start(bf16[128,512]{1,0:T(8,128)(2,1)S(1)} %get-tuple-element.39), channel_id=1, source_target_pairs={{0,2},{1,3},{2,0},{3,1},{4,6},{5,7},{6,4},{7,5},{8,10},{9,11},{10,... | collective-permute-start | bytes 393224 | tf_op jit(solution)/shard_map/ppermute | solution.py:23
  40.3 8.7 %collective-permute-start.5 = (bf16[128,512]{1,0:T(8,128)(2,1)S(1)}, bf16[128,512]{1,0:T(8,128)(2,1)S(1)}, u32[]{:S(2)}, u32[]{:S(2)}) collective-permute-start(bf16[128,512]{1,0:T(8,128)(2,1)S(1)} %get-tuple-element.40), channel_id=1, source_target_pairs={{0,14},{1,15},{2,4},{3,5},{4,2},{5,3},{6,8},{7,9},{8,6},{9,7},{10,... | collective-permute-start | bytes 393224 | tf_op jit(solution)/shard_map/ppermute | solution.py:23

commit v6 on v5

--- a/solution.py
+++ b/solution.py
@@ -11,7 +11,7 @@
 HALVES = 2
 COPY = 256
 CHUNK = 16
-FIXED = 16
+FIXED = 13
 EPS = 1e-05
 BF = jnp.bfloat16
 F32 = jnp.float32
@@ -131,7 +131,7 @@
     return index & 1, (index >> 1) & 1
 
 
-def pack_kernel(nodes, lists, coarse, pair_out, first_out, second_out, out):
+def pack_kernel(nodes, lists, coarse, pair_out, first_out, second_out, out, chosen, sems):
     rows = nodes[...]
     own = rows.shape[0]
     width = lists.shape[1]
@@ -141,19 +141,27 @@
     def picked(index):
         return mm_l(ones_where(ids == lists[pl.ds(index, 1), :]), rows).astype(BF)
 
+    count = coarse.shape[1]
+    hit = ones_where(lax.broadcasted_iota(jnp.int32, (own, count), 0) == coarse[...])
+    chosen[...] = mm_l(hit, rows).astype(BF)
+
+    def copy_to(index):
+        return pltpu.make_async_copy(chosen, out.at[index], sems.at[index])
+
+    def put(index, carry):
+        copy_to(index).start()
+        return carry
+
+    def done(index, carry):
+        copy_to(index).wait()
+        return carry
+
+    lax.fori_loop(0, out.shape[0], put, 0)
     pair_out[:width] = picked(odd)
     pair_out[width:] = picked(1 - odd)
     first_out[...] = picked(2 + odd)
     second_out[...] = picked(3 - odd)
-    count = coarse.shape[1]
-    hit = ones_where(lax.broadcasted_iota(jnp.int32, (own, count), 0) == coarse[...])
-    chosen = mm_l(hit, rows).astype(BF)
-
-    def put(index, carry):
-        out[index] = chosen
-        return carry
-
-    lax.fori_loop(0, out.shape[0], put, 0)
+    lax.fori_loop(0, out.shape[0], done, 0)
 
 
 def join_kernel(relay, pair, first, second, first_out, second_out):
@@ -166,8 +174,8 @@
 
 def local_kernel(*refs):
     sources, edges_in, out = refs[:7], refs[7], refs[8]
-    targets, edges, table, value, load, store = refs[9:16], *refs[16:]
-    nodes, w_send, w_recv, send, recv, w_edge, bias = targets
+    w_send, send, recv, nodes, w_recv, w_edge, bias, edges, table, value, load, store = refs[9:]
+    targets = (nodes, w_send, w_recv, send, recv, w_edge, bias)
     own = nodes.shape[0]
     parts = ROWS // LANES
     copies = edges.shape[0] // COPY
@@ -233,7 +241,7 @@
 def main_kernel(shift, steps, *refs):
     take = iter(refs)
     received = [next(take) for _ in range(3)]
-    coarse = next(take)
+    coarse, w_send, send, recv = [next(take) for _ in range(4)]
     sources = [next(take) for _ in range(FIXED)]
     block_sources = [next(take) for _ in range(3)]
     pair_out, first_out, second_out, far_out = [next(take) for _ in range(4)]
@@ -241,10 +249,10 @@
     targets = [next(take) for _ in range(FIXED)]
     pre_in, edges, edge_cot = block_targets = [next(take) for _ in range(3)]
     new_nodes, d_node, new_edges, d_pre = [next(take) for _ in range(4)]
-    stack, rows2, table2, slope, unit, inverse, d_agg = [next(take) for _ in range(7)]
+    stack, rows2, table2, slope, unit, inverse, d_agg, far_rows = [next(take) for _ in range(8)]
     load, store = next(take), next(take)
-    far_lists, w_send, send, recv, w_edge_out, edge_out_bias, edge_gain, count = targets[:8]
-    nodes, w_agg, w_node, node_bias, w_node_out, node_out_bias, node_cot, node_gain = targets[8:]
+    far_lists, w_edge_out, edge_out_bias, edge_gain, count = targets[:5]
+    nodes, w_agg, w_node, node_bias, w_node_out, node_out_bias, node_cot, node_gain = targets[5:]
     own = nodes.shape[0]
     width = nodes.shape[1]
     far_width, peers = far_lists.shape
@@ -264,9 +272,9 @@
         pltpu.make_async_copy(new_nodes, new_nodes_out, store.at[0]),
         pltpu.make_async_copy(d_node, d_node_out, store.at[1]),
     ]
-    start_all(fixed[:4])
+    fixed[0].start()
     whole[0].start()
-    start_all(fixed[4:])
+    start_all(fixed[1:])
     start_all(whole[1:])
     fixed[0].wait()
     far_ids = lax.broadcasted_iota(jnp.int32, (coarse.shape[0], peers), 0)
@@ -292,10 +300,7 @@
     for slot in range(far_width):
         start = near_rows + slot * peers
         rows2[start : start + peers] = mm_l(far_hits[slot], coarse[...]).astype(BF)
-    fixed[1].wait()
     table2[...] = mm(rows2[...], w_send[...]).astype(BF)
-    wait_all(fixed[2:8])
-
     def live_gain(block):
         return edge_gain[...] * jnp.where(count[...] > block, 1.0, 0.0)
 
@@ -315,6 +320,7 @@
     def activate(index, remote):
         if index == 0:
             whole[0].wait()
+            wait_all(fixed[1:5])
         hidden = []
         for low in range(0, half, CHUNK):
             here = slice(index * half + low, index * half + low + CHUNK)
@@ -346,7 +352,7 @@
         return mm(hit, sent)
 
     total = pipeline([pick_remote, activate, project, message_of, gather_up])
-    wait_all(fixed[8:])
+    wait_all(fixed[5:])
     wait_all(whole[1:])
     rows = nodes[...]
     pre_node = mm(rows, w_node[...]) + mm(total.astype(BF), w_agg[...]) + node_bias[...]
@@ -406,8 +412,16 @@
     sums2 = pipeline([pick_back, norm_grad, project_back, activate_back, gather_back])
     edge_outs[1].start()
 
-    d_rows2 = mm_t(sums2.astype(BF), w_send[...])
-    stack[: steps * near_width] = d_rows2[: steps * near_width].astype(BF)
+    sums2 = sums2.astype(BF)
+    d_far = mm_t(sums2[near_rows:], w_send[...])
+    d_coarse = None
+    for slot in range(far_width):
+        term = mm(far_hits[slot], d_far[slot * peers : (slot + 1) * peers].astype(BF))
+        d_coarse = term if d_coarse is None else d_coarse + term
+    far_rows[...] = d_coarse.astype(BF)
+    far_copy = pltpu.make_async_copy(far_rows, far_out, store.at[4])
+    far_copy.start()
+    stack[: steps * near_width] = mm_t(sums2[:near_rows], w_send[...]).astype(BF)
     outgoing = [
         (pair_out, 0, 1 - core),
         (pair_out, 1, core),
@@ -417,12 +431,7 @@
     for ref, index, slot in outgoing:
         start = pl.multiple_of(slot * near_width, near_width)
         ref[index * near_width : (index + 1) * near_width] = stack[pl.ds(start, near_width), :]
-    d_coarse = None
-    for slot in range(far_width):
-        start = near_rows + slot * peers
-        term = mm(far_hits[slot], d_rows2[start : start + peers].astype(BF))
-        d_coarse = term if d_coarse is None else d_coarse + term
-    far_out[...] = d_coarse.astype(BF)
+    far_copy.wait()
     wait_all(edge_outs)
     wait_all(node_outs)
 
@@ -596,22 +605,23 @@
         pack_kernel,
         out_shape=[pair_like, near_like, near_like, shape((peers, coarse_count, width), BF)],
         in_specs=vmem(3),
-        out_specs=vmem(4),
+        out_specs=vmem(3) + hbm(1),
+        scratch_shapes=[
+            pltpu.VMEM((coarse_count, width), BF),
+            pltpu.SemaphoreType.DMA((peers,)),
+        ],
         name="pack",
     )(nodes, neighbour_send_lists, row(coarse_rows))
     *near, coarse = exchanged(*packed, (0, 1))
 
-    pre_local = pl.pallas_call(
+    pre_local, *kept = pl.pallas_call(
         local_kernel,
-        out_shape=shape((edge_rows, hidden), BF),
+        out_shape=[shape((edge_rows, hidden), BF), square(), index_rows(), index_rows()],
         in_specs=hbm(8),
-        out_specs=hbm(1)[0],
+        out_specs=hbm(1) + vmem(3),
         scratch_shapes=[
             node_like(),
             square(),
-            square(),
-            index_rows(),
-            index_rows(),
             square(),
             small(),
             edge_like(),
@@ -638,13 +648,10 @@
             shape((edge_rows, width), BF),
             shape((edge_rows, hidden), BF),
         ],
-        in_specs=vmem(4) + hbm(FIXED + 3),
-        out_specs=vmem(4) + hbm(4),
+        in_specs=vmem(7) + hbm(FIXED + 3),
+        out_specs=vmem(3) + hbm(5),
         scratch_shapes=[
             pltpu.VMEM((far_width, peers), jnp.int32),
-            square(),
-            index_rows(),
-            index_rows(),
             square(),
             small(),
             small(),
@@ -671,8 +678,9 @@
             pltpu.VMEM((edge_rows, width), F32),
             pltpu.VMEM((edge_rows, 1), F32),
             pltpu.VMEM((own_pad, width), BF),
+            pltpu.VMEM((peers * coarse_count, width), BF),
             pltpu.SemaphoreType.DMA((FIXED + 3,)),
-            pltpu.SemaphoreType.DMA((4,)),
+            pltpu.SemaphoreType.DMA((5,)),
         ],
         cost_estimate=pl.CostEstimate(
             flops=2 * edge_rows * width * hidden * 8, transcendentals=0, bytes_accessed=16 << 20
@@ -681,10 +689,8 @@
     )(
         *near,
         here(coarse.reshape(-1, width)),
+        *[here(value) for value in kept],
         far_lists[0].T,
-        w_send,
-        send,
-        recv,
         w_edge_out,
         row(edge_out_bias),
         row(edge_gain),

time: 50.5 us -> 49.3 us (0.976)
  Pallas kernels: 26.5 us -> 25.2 us
    pallas_call x1, Pallas kernels: 12.4 us -> 11.4 us  [local(): pl.pallas_call(lambda *refs: main_kernel(shift, steps, *refs), out_shape=...]
where the time goes in v6:
time: 49.3 us; the launch traced here: 48.9 us
  Pallas kernels  25.2 us (51%)
  starting transfers between devices  21.9 us (44%)
  between operations  1.41 us (3%)
    pallas_call x1, Pallas kernels, local(): pl.pallas_call(lambda *refs: main_kernel(shift, steps, *refs), out_shape=...  11.4 us
    ppermute x6, starting transfers between devices, swapped(): return lax.ppermute(value, axis, pairs)  11.1 us
    all_to_all x2, starting transfers between devices, exchanged(): lax.all_to_all(rows, 'patch', split_axis=0, concat_axis=0, tiled=True)  10.8 us
    pallas_call x1, Pallas kernels, local(): pl.pallas_call(local_kernel, out_shape=[shape((edge_rows, hidden), BF), s...  5.71 us
    pallas_call x1, Pallas kernels, local(): pl.pallas_call(local_back_kernel, out_shape=[shape((edge_rows, width), BF...  5.05 us
    pallas_call x1, Pallas kernels, local(): pl.pallas_call(pack_kernel, out_shape=[pair_like, near_like, near_like, s...  1.98 us
    pallas_call x1, Pallas kernels, local(): pl.pallas_call(combine_kernel, out_shape=shape((own, width), BF), in_spec...  1.06 us
  transfers between devices with their start and end apart: 8, of which 1 were waited for; matrix products, arithmetic and copies ran while one was open for 0% of the time, Pallas kernels for 22%

profile of v6, /device:TPU:0, one launch (start us, length us, event | category | flops | bytes accessed | tf_op | source)
XLA Modules:
  0.0 48.9 jit_solution(16425654092856824475)
XLA Ops:
  0.6 2.0 %pack.1 = (bf16[128,512]{1,0:T(8,128)(2,1)S(1)}, bf16[64,512]{1,0:T(8,128)(2,1)S(1)}, bf16[64,512]{1,0:T(8,128)(2,1)S(1)}, bf16[16,8,512]{2,1,0:T(8,128)(2,1)}) custom-call(bf16[320,512]{1,0:T(8,128)(2,1)} %refs_12_.1, s32[4,64]{1,0:T(4,128)} %refs_6_.1, s32[1,8]{1,0:T(1,128)} %bitcast.20), custom_call_target="tpu_custom_call" | custom-call | tf_op jit(solution)/shard_map/pack/pallas_call | solution.py:604
  2.6 0.6 %collective-permute-start = (bf16[128,512]{1,0:T(8,128)(2,1)S(1)}, bf16[128,512]{1,0:T(8,128)(2,1)S(1)}, u32[]{:S(2)}, u32[]{:S(2)}) collective-permute-start(bf16[128,512]{1,0:T(8,128)(2,1)S(1)} %get-tuple-element.27), channel_id=1, source_target_pairs={{0,1},{1,0},{2,3},{3,2},{4,5},{5,4},{6,7},{7,6},{8,9},{9,8},{10,11... | collective-permute-start | bytes 393224 | tf_op jit(solution)/shard_map/ppermute | solution.py:23
  3.2 7.0 %all-to-all-start = ((bf16[16,8,512]{2,1,0:T(8,128)(2,1)}), bf16[16,8,512]{2,1,0:T(8,128)(2,1)S(1)}, u32[]{:S(2)}, u32[]{:S(2)}) async-start(bf16[16,8,512]{2,1,0:T(8,128)(2,1)} %get-tuple-element.32), calls=%async_computation | async-start | bytes 262144 | tf_op jit(solution)/shard_map/all_to_all | solution.py:592
  10.9 0.0 collective-permute-done.refs_0_
  10.9 2.0 %collective-permute-start.1 = (bf16[128,512]{1,0:T(8,128)(2,1)S(1)}, bf16[128,512]{1,0:T(8,128)(2,1)S(1)}, u32[]{:S(2)}, u32[]{:S(2)}) collective-permute-start(bf16[128,512]{1,0:T(8,128)(2,1)S(1)} %get-tuple-element.30), channel_id=1, source_target_pairs={{0,2},{1,3},{2,0},{3,1},{4,6},{5,7},{6,4},{7,5},{8,10},{9,11},{10,... | collective-permute-start | bytes 393224 | tf_op jit(solution)/shard_map/ppermute | solution.py:23
  12.9 3.3 %collective-permute-start.2 = (bf16[128,512]{1,0:T(8,128)(2,1)S(1)}, bf16[128,512]{1,0:T(8,128)(2,1)S(1)}, u32[]{:S(2)}, u32[]{:S(2)}) collective-permute-start(bf16[128,512]{1,0:T(8,128)(2,1)S(1)} %get-tuple-element.31), channel_id=1, source_target_pairs={{0,14},{1,15},{2,4},{3,5},{4,2},{5,3},{6,8},{7,9},{8,6},{9,7},{10,... | collective-permute-start | bytes 393224 | tf_op jit(solution)/shard_map/ppermute | solution.py:23
  16.2 5.7 %local_ahead.1 = (bf16[1536,512]{1,0:T(8,128)(2,1)}, bf16[512,512]{1,0:T(8,128)(2,1)S(1)}, s32[12,128]{1,0:T(8,128)S(1)}, s32[12,128]{1,0:T(8,128)S(1)}) custom-call(bf16[320,512]{1,0:T(8,128)(2,1)} %refs_12_.1, bf16[512,512]{1,0:T(8,128)(2,1)} %refs_3_.1, bf16[512,512]{1,0:T(8,128)(2,1)} %refs_4_.1, s32[12,128]{1,0:T(8,128)} %bitcast.22, ...), custom_call_target="tpu_custom_call" | custom-call | flops 2415919104 | bytes 6291456 | tf_op jit(solution)/shard_map/local_ahead/pallas_call | solution.py:617
  21.9 0.0 all-to-all-done
  21.9 0.0 collective-permute-done.1.refs_1_
  21.9 0.0 collective-permute-done.2.refs_2_
  21.9 11.4 %main.1 = (bf16[128,512]{1,0:T(8,128)(2,1)S(1)}, bf16[64,512]{1,0:T(8,128)(2,1)S(1)}, bf16[64,512]{1,0:T(8,128)(2,1)S(1)}, bf16[128,512]{1,0:T(8,128)(2,1)}, bf1...) custom-call(bf16[128,512]{1,0:T(8,128)(2,1)S(1)} %collective-permute-done.ref, ...), custom_call_target="tpu_custom_call" | custom-call | flops 6442450944 | bytes 16777216 | tf_op jit(solution)/shard_map/main/pallas_call | solution.py:639
  33.3 0.1 collective-permute-start.3
  33.4 3.8 %all-to-all-start.1 = ((bf16[16,8,512]{2,1,0:T(8,128)(2,1)}), bf16[16,8,512]{2,1,0:T(8,128)(2,1)S(1)}, u32[]{:S(2)}, u32[]{:S(2)}) async-start(bf16[16,8,512]{2,1,0:T(8,128)(2,1)} %bitcast.19), calls=%async_computation.1 | async-start | bytes 262144 | tf_op jit(solution)/shard_map/all_to_all | solution.py:592
  37.2 0.0 collective-permute-done.3.refs_0_.pair
  37.2 2.0 %collective-permute-start.4 = (bf16[128,512]{1,0:T(8,128)(2,1)S(1)}, bf16[128,512]{1,0:T(8,128)(2,1)S(1)}, u32[]{:S(2)}, u32[]{:S(2)}) collective-permute-start(bf16[128,512]{1,0:T(8,128)(2,1)S(1)} %get-tuple-element.47), channel_id=1, source_target_pairs={{0,2},{1,3},{2,0},{3,1},{4,6},{5,7},{6,4},{7,5},{8,10},{9,11},{10,... | collective-permute-start | bytes 393224 | tf_op jit(solution)/shard_map/ppermute | solution.py:23
  39.2 3.3 %collective-permute-start.5 = (bf16[128,512]{1,0:T(8,128)(2,1)S(1)}, bf16[128,512]{1,0:T(8,128)(2,1)S(1)}, u32[]{:S(2)}, u32[]{:S(2)}) collective-permute-start(bf16[128,512]{1,0:T(8,128)(2,1)S(1)} %get-tuple-element.48), channel_id=1, source_target_pairs={{0,14},{1,15},{2,4},{3,5},{4,2},{5,3},{6,8},{7,9},{8,6},{9,7},{10,... | collective-permute-start | bytes 393224 | tf_op jit(solution)/shard_map/ppermute | solution.py:23
  42.4 5.0 %local_back.1 = (bf16[1536,512]{1,0:T(8,128)(2,1)}, f32[320,512]{1,0:T(8,128)S(1)}, bf16[320,448]{1,0:T(8,128)(2,1)S(1)}) custom-call(s32[12,128]{1,0:T(8,128)} %bitcast.23, s32[12,128]{1,0:T(8,128)} %bitcast.25, bf16[512,512]{1,0:T(8,128)(2,1)} %refs_2_.3, bf16[512,512]{1,0:T(8,128)(2,1)} %refs_3_.1, bf16[512,512]{1,0:T(8,128)(2,1)} %refs_4_.1, ...), custom_call_target="tpu_custom_call" | custom-call | flops 2415919104 | bytes 6291456 | tf_op jit(solution)/shard_map/local_back/pallas_call | solution.py:715
  47.5 0.0 all-to-all-done.1
  47.5 0.0 collective-permute-done.4.first
  47.5 0.3 collective-permute-done.5.second
  47.9 1.1 %combine.1 = bf16[320,512]{1,0:T(8,128)(2,1)} custom-call(f32[320,512]{1,0:T(8,128)S(1)} %get-tuple-element.41.node_sum, bf16[320,448]{1,0:T(8,128)(2,1)S(1)} %get-tuple-element.42.hit, bf16[128,512]{1,0:T(8,128)(2,1)S(1)} %bitcast.17, bf16[128,512]{1,0:T(8,128)(2,1)S(1)} %collective-permute-done.3.refs_0_.pair, ...), custom_call_target="tpu_custom_call" | custom-call | tf_op jit(solution)/shard_map/combine/pallas_call | solution.py:757
  (2 shorter events, 0.0 us)
Async XLA Ops:
  2.6 8.3 %collective-permute-start = (bf16[128,512]{1,0:T(8,128)(2,1)S(1)}, bf16[128,512]{1,0:T(8,128)(2,1)S(1)}, u32[]{:S(2)}, u32[]{:S(2)}) collective-permute-start(bf16[128,512]{1,0:T(8,128)(2,1)S(1)} %get-tuple-element.27), channel_id=1, source_target_pairs={{0,1},{1,0},{2,3},{3,2},{4,5},{5,4},{6,7},{7,6},{8,9},{9,8},{10,11... | collective-permute-start | bytes 393224 | tf_op jit(solution)/shard_map/ppermute | solution.py:23
  3.2 18.7 %all-to-all-start = ((bf16[16,8,512]{2,1,0:T(8,128)(2,1)}), bf16[16,8,512]{2,1,0:T(8,128)(2,1)S(1)}, u32[]{:S(2)}, u32[]{:S(2)}) async-start(bf16[16,8,512]{2,1,0:T(8,128)(2,1)} %get-tuple-element.32), calls=%async_computation | async-start | bytes 262144 | tf_op jit(solution)/shard_map/all_to_all | solution.py:592
  10.9 11.0 %collective-permute-start.1 = (bf16[128,512]{1,0:T(8,128)(2,1)S(1)}, bf16[128,512]{1,0:T(8,128)(2,1)S(1)}, u32[]{:S(2)}, u32[]{:S(2)}) collective-permute-start(bf16[128,512]{1,0:T(8,128)(2,1)S(1)} %get-tuple-element.30), channel_id=1, source_target_pairs={{0,2},{1,3},{2,0},{3,1},{4,6},{5,7},{6,4},{7,5},{8,10},{9,11},{10,... | collective-permute-start | bytes 393224 | tf_op jit(solution)/shard_map/ppermute | solution.py:23
  12.9 9.0 %collective-permute-start.2 = (bf16[128,512]{1,0:T(8,128)(2,1)S(1)}, bf16[128,512]{1,0:T(8,128)(2,1)S(1)}, u32[]{:S(2)}, u32[]{:S(2)}) collective-permute-start(bf16[128,512]{1,0:T(8,128)(2,1)S(1)} %get-tuple-element.31), channel_id=1, source_target_pairs={{0,14},{1,15},{2,4},{3,5},{4,2},{5,3},{6,8},{7,9},{8,6},{9,7},{10,... | collective-permute-start | bytes 393224 | tf_op jit(solution)/shard_map/ppermute | solution.py:23
  33.3 3.8 %collective-permute-start.3 = (bf16[128,512]{1,0:T(8,128)(2,1)S(1)}, bf16[128,512]{1,0:T(8,128)(2,1)S(1)}, u32[]{:S(2)}, u32[]{:S(2)}) collective-permute-start(bf16[128,512]{1,0:T(8,128)(2,1)S(1)} %get-tuple-element.44), channel_id=1, source_target_pairs={{0,1},{1,0},{2,3},{3,2},{4,5},{5,4},{6,7},{7,6},{8,9},{9,8},{10,11... | collective-permute-start | bytes 393224 | tf_op jit(solution)/shard_map/ppermute | solution.py:23
  33.4 14.1 %all-to-all-start.1 = ((bf16[16,8,512]{2,1,0:T(8,128)(2,1)}), bf16[16,8,512]{2,1,0:T(8,128)(2,1)S(1)}, u32[]{:S(2)}, u32[]{:S(2)}) async-start(bf16[16,8,512]{2,1,0:T(8,128)(2,1)} %bitcast.19), calls=%async_computation.1 | async-start | bytes 262144 | tf_op jit(solution)/shard_map/all_to_all | solution.py:592
  37.2 10.3 %collective-permute-start.4 = (bf16[128,512]{1,0:T(8,128)(2,1)S(1)}, bf16[128,512]{1,0:T(8,128)(2,1)S(1)}, u32[]{:S(2)}, u32[]{:S(2)}) collective-permute-start(bf16[128,512]{1,0:T(8,128)(2,1)S(1)} %get-tuple-element.47), channel_id=1, source_target_pairs={{0,2},{1,3},{2,0},{3,1},{4,6},{5,7},{6,4},{7,5},{8,10},{9,11},{10,... | collective-permute-start | bytes 393224 | tf_op jit(solution)/shard_map/ppermute | solution.py:23
  39.2 8.7 %collective-permute-start.5 = (bf16[128,512]{1,0:T(8,128)(2,1)S(1)}, bf16[128,512]{1,0:T(8,128)(2,1)S(1)}, u32[]{:S(2)}, u32[]{:S(2)}) collective-permute-start(bf16[128,512]{1,0:T(8,128)(2,1)S(1)} %get-tuple-element.48), channel_id=1, source_target_pairs={{0,14},{1,15},{2,4},{3,5},{4,2},{5,3},{6,8},{7,9},{8,6},{9,7},{10,... | collective-permute-start | bytes 393224 | tf_op jit(solution)/shard_map/ppermute | solution.py:23
